TPU v7x, 32 devices: a whole 2x2x4 slice. The times are simulated.
32 devices in a mesh: ctx: 32 (over z, y, x, core).
Axes of the slice: x: 2, y: 2, z: 4, core: 2. Of those that a mesh axis runs over, the one named last changes fastest.
Arguments:
- queries: bfloat16 [16384, 4096], P('ctx'), may hold values from -140 to 140
- keys: bfloat16 [16384, 1024], P('ctx'), may hold values from -6 to 6
- values: bfloat16 [16384, 1024], P('ctx'), may hold values from -6 to 6
- proj_weight: bfloat16 [8, 128, 256], replicated, may hold values from -10 to 10
Outputs:
- attended: bfloat16 [16384, 4096], P('ctx')
All inputs are finite; a program needn't handle non-finite values.
Results may differ from a plain program's by a relative error of at most 0.0055.
The roundings to bfloat16 on the way count: a program that leaves them out, or rounds other values in their place, can miss the bound.
Values may be sent and summed in bfloat16 or wider, within the bound.
No kernel may reach another device: no remote copies, remote signals or barrier semaphores. Data moves between devices by JAX's collectives and lax.ppermute only.
A program may use at most 192 MiB of HBM per device.

v0:
```python
import functools
import math

import jax
import jax.numpy as jnp
from jax import lax
from jax.experimental import pallas as pl
from jax.experimental.pallas import tpu as pltpu
from jax.sharding import PartitionSpec as P

H = 32
KV = 8
HD = 128
GROUP = H // KV
R = 256
HALF = 256
AUX = 8
ROWS = 2 * HD + AUX
T_ROW = 2 * HD
M_ROW = 2 * HD + 1
EXP2_SCALE = math.log2(math.e) / math.sqrt(HD)
FAR_AWAY = 1e30

HEAD_BITS = (8, 4, 1)
HALF_BIT = 16


def normalize(x):
    centered = x - jnp.mean(x, axis=-1, keepdims=True)
    spread = jnp.mean(centered * centered, axis=-1, keepdims=True)
    return centered * lax.rsqrt(spread + 1e-05)


def project_kernel(own, k_ref, v_ref, w0_ref, w1_ref, top_ref, bot_ref, part_ref):
    keys = k_ref[...]
    values = v_ref[...]
    near_k = normalize(keys.astype(jnp.float32)).astype(jnp.bfloat16)
    near_v = normalize(values.astype(jnp.float32)).astype(jnp.bfloat16)
    top_ref[:, :HD] = near_k[:HALF]
    top_ref[:, HD:] = near_v[:HALF]
    bot_ref[:, :HD] = near_k[HALF:]
    bot_ref[:, HD:] = near_v[HALF:]
    weight = jnp.concatenate([w0_ref[0], w1_ref[0]], axis=1)
    logits = jnp.dot(near_k, weight, preferred_element_type=jnp.float32)
    top = jnp.max(logits, axis=0, keepdims=True)
    expo = jnp.exp(logits - top)
    total = jnp.sum(expo, axis=0, keepdims=True)
    upper = expo.astype(jnp.bfloat16)
    lower = (expo - upper.astype(jnp.float32)).astype(jnp.bfloat16)
    pair = jnp.concatenate([keys, values], axis=1)
    dims = (((0,), (0,)), ((), ()))
    both = lax.dot_general(pair, upper, dims, preferred_element_type=jnp.float32)
    both = both + lax.dot_general(pair, lower, dims, preferred_element_type=jnp.float32)
    part_ref[0, : 2 * HD] = both
    row = lax.broadcasted_iota(jnp.int32, (AUX, R), 0)
    part_ref[0, 2 * HD :] = jnp.where(row == 0, total, jnp.where(row == 1, top, 0.0))


def project(own, keys, values, proj_weight):
    tok = keys.shape[0]
    head = lambda p, own: p ^ own[0]
    return pl.pallas_call(
        project_kernel,
        out_shape=(
            jax.ShapeDtypeStruct((HALF, KV * 2 * HD), jnp.bfloat16),
            jax.ShapeDtypeStruct((HALF, KV * 2 * HD), jnp.bfloat16),
            jax.ShapeDtypeStruct((KV, ROWS, R), jnp.float32),
        ),
        grid_spec=pltpu.PrefetchScalarGridSpec(
            num_scalar_prefetch=1,
            grid=(KV,),
            in_specs=[
                pl.BlockSpec((tok, HD), lambda p, own: (0, head(p, own))),
                pl.BlockSpec((tok, HD), lambda p, own: (0, head(p, own))),
                pl.BlockSpec((1, HD, R // 2), lambda p, own: (head(p, own), 0, own[1])),
                pl.BlockSpec((1, HD, R // 2), lambda p, own: (head(p, own), 0, 1 - own[1])),
            ],
            out_specs=[
                pl.BlockSpec((HALF, 2 * HD), lambda p, own: (0, head(p, own))),
                pl.BlockSpec((HALF, 2 * HD), lambda p, own: (0, head(p, own))),
                pl.BlockSpec((1, ROWS, R), lambda p, own: (p, 0, 0)),
            ],
        ),
        compiler_params=pltpu.CompilerParams(vmem_limit_bytes=32 << 20),
        cost_estimate=pl.CostEstimate(
            flops=KV * tok * R * HD * 10, bytes_accessed=8 << 20, transcendentals=KV * tok * R
        ),
        name="project",
    )(own, keys, values, proj_weight, proj_weight)


def merge(parts):
    tops = [x[:, M_ROW : M_ROW + 1] for x in parts]
    top = functools.reduce(jnp.maximum, tops)
    row = lax.broadcasted_iota(jnp.int32, parts[0].shape, 1)
    added = sum(x * jnp.exp(t - top) for x, t in zip(parts, tops))
    return jnp.where(row == M_ROW, top, added)


def swap(x, bits):
    peers = lax.axis_size("ctx")
    return lax.ppermute(x, "ctx", [(i, i ^ bits) for i in range(peers)])


def attend_kernel(own, q_ref, b_ref, top_ref, bot_ref, a_ref, g_ref, o_ref):
    nears = (b_ref, top_ref, bot_ref, a_ref)
    hide = (
        jnp.where(own[2] > 0, 0.0, FAR_AWAY),
        0.0,
        0.0,
        jnp.where(own[3] > 0, 0.0, FAR_AWAY),
    )
    far_k = jnp.concatenate([g_ref[0, 0, :HD], g_ref[0, 1, :HD]], axis=1)
    far_v = jnp.concatenate([g_ref[0, 0, HD:], g_ref[0, 1, HD:]], axis=1)
    flip = (((1,), (1,)), ((), ()))
    rows = 256
    for start in range(0, q_ref.shape[0], rows):
        for g in range(GROUP):
            q = q_ref[start : start + rows, g * HD : (g + 1) * HD]
            scores = [
                lax.dot_general(q, x[:, :HD], flip, preferred_element_type=jnp.float32)
                for x in nears
            ]
            far = jnp.dot(q, far_k, preferred_element_type=jnp.float32)
            tops = [jnp.max(s, axis=1, keepdims=True) - w for s, w in zip(scores, hide)]
            top = functools.reduce(jnp.maximum, tops)
            top = jnp.maximum(top, jnp.max(far, axis=1, keepdims=True))
            expo = [jnp.exp2((s - (top + w)) * EXP2_SCALE) for s, w in zip(scores, hide)]
            expo.append(jnp.exp2((far - top) * EXP2_SCALE))
            total = sum(jnp.sum(e, axis=1, keepdims=True) for e in expo)
            inverse = 1.0 / total
            probs = [(e * inverse).astype(jnp.bfloat16) for e in expo]
            mixed = lax.dot_general(probs[4], far_v, flip, preferred_element_type=jnp.float32)
            for p, x in zip(probs, nears):
                mixed = mixed + jnp.dot(p, x[:, HD:], preferred_element_type=jnp.float32)
            o_ref[start : start + rows, g * HD : (g + 1) * HD] = mixed.astype(jnp.bfloat16)


def attend(own, queries, before, top, bot, after, far):
    tok = queries.shape[0]
    head = lambda p, own: p ^ own[0]
    near = pl.BlockSpec((HALF, 2 * HD), lambda p, own: (0, head(p, own)))
    return pl.pallas_call(
        attend_kernel,
        out_shape=jax.ShapeDtypeStruct(queries.shape, jnp.bfloat16),
        grid_spec=pltpu.PrefetchScalarGridSpec(
            num_scalar_prefetch=1,
            grid=(KV,),
            in_specs=[
                pl.BlockSpec((tok, GROUP * HD), lambda p, own: (0, head(p, own))),
                near,
                near,
                near,
                near,
                pl.BlockSpec((1, 2, 2 * HD, R // 2), lambda p, own: (p, 0, 0, 0)),
            ],
            out_specs=pl.BlockSpec((tok, GROUP * HD), lambda p, own: (0, head(p, own))),
        ),
        compiler_params=pltpu.CompilerParams(vmem_limit_bytes=48 << 20),
        cost_estimate=pl.CostEstimate(
            flops=4 * H * tok * 1280 * HD, bytes_accessed=16 << 20, transcendentals=H * tok * 1280
        ),
        name="attend",
    )(own, queries, before, top, bot, after, far)


def on_device(queries, keys, values, proj_weight):
    peers = lax.axis_size("ctx")
    me = lax.axis_index("ctx")
    bit = lambda b: (me & b) // b
    own_head = sum(bit(b) << s for s, b in enumerate(HEAD_BITS))
    own = jnp.stack(
        [own_head, bit(HALF_BIT), (me > 0).astype(jnp.int32), (me < peers - 1).astype(jnp.int32)]
    ).astype(jnp.int32)
    near_top, near_bot, part = project(own, keys, values, proj_weight)
    b0, b1, b2 = HEAD_BITS
    part = merge([part[:4], swap(part[4:], b2)])
    arrived = [swap(part[1:2], b0), swap(part[2:3], b1), swap(part[3:4], b0 ^ b1)]
    up = [(i, i + 1) for i in range(peers - 1)]
    down = [(i + 1, i) for i in range(peers - 1)]
    before = lax.ppermute(near_bot, "ctx", up)
    after = lax.ppermute(near_top, "ctx", down)
    part = merge([part[:1]] + arrived)
    part = merge([part[:, :, : R // 2], swap(part[:, :, R // 2 :], HALF_BIT)])
    rest = 1
    while rest < peers:
        if rest not in HEAD_BITS + (HALF_BIT,):
            part = merge([part, swap(part, rest)])
        rest *= 2
    far = (part[:, : 2 * HD] / part[:, T_ROW : T_ROW + 1]).astype(jnp.bfloat16)[:, None]
    far = jnp.concatenate([far, swap(far, HALF_BIT)], axis=1)
    for b in HEAD_BITS:
        far = jnp.concatenate([far, swap(far, b)], axis=0)
    return attend(own, queries, before, near_top, near_bot, after, far)


def solution(mesh):
    in_specs = (P("ctx", None), P("ctx", None), P("ctx", None), P())
    out_specs = P("ctx", None)
    return jax.shard_map(
        on_device, mesh=mesh, in_specs=in_specs, out_specs=out_specs, check_vma=False
    )
```

profile of v0, /device:TPU:1, one launch (start us, length us, event | category | flops | bytes accessed | tf_op | source)
XLA Modules:
  0.0 138.0 jit_solution(5467609863760063907)
XLA Ops:
  0.0 0.1 pad_add_fusion.own
  0.1 0.0 copy-start
  0.1 1.2 copy-done
  1.3 0.0 copy-start.1
  1.3 1.2 copy-done.1
  2.5 0.0 copy-start.2
  2.5 1.0 copy-done.2
  3.6 9.8 %project.1 = (bf16[256,2048]{1,0:T(8,128)(2,1)S(1)}, bf16[256,2048]{1,0:T(8,128)(2,1)S(1)}, f32[8,264,256]{2,1,0:T(8,128)S(1)}) custom-call(s32[4]{0:T(128)S(1)} %pad_add_fusion.own, bf16[512,1024]{1,0:T(8,128)(2,1)S(1)} %copy-done, bf16[512,1024]{1,0:T(8,128)(2,1)S(1)} %copy-done.1, bf16[8,128,256]{2,1,0:T(8,128)(2,1)S(1)} %copy-done.2, ...), custom_call_target="tpu_custom_call" | custom-call | flops 1342177280 | bytes 8388608 | tf_op jit(solution)/shard_map/project/pallas_call | solution.py:62
  13.4 0.1 slice.64
  13.5 0.1 collective-permute-start.2
  13.6 2.7 %collective-permute-done.2 = f32[4,264,256]{2,1,0:T(8,128)S(1)} collective-permute-done((f32[4,264,256]{2,1,0:T(8,128)S(1)}, f32[4,264,256]{2,1,0:T(8,128)S(1)}, u32[]{:S(2)}, u32[]{:S(2)}) %collective-permute-start.2) | collective-permute-done | bytes 1081376 | tf_op jit(solution)/shard_map/ppermute | solution.py:102
  16.3 0.2 add_select_fusion
  16.5 0.1 fusion.10
  16.6 2.5 %collective-permute-start.3 = (f32[1,264,256]{2,1,0:T(8,128)S(1)}, f32[1,264,256]{2,1,0:T(8,128)S(1)}, u32[]{:S(2)}, u32[]{:S(2)}) collective-permute-start(f32[1,264,256]{2,1,0:T(8,128)S(1)} %get-tuple-element.15), channel_id=1, source_target_pairs={{0,8},{1,9},{2,10},{3,11},{4,12},{5,13},{6,14},{7,15},{8,0},{9,1},... | collective-permute-start | bytes 811016 | tf_op jit(solution)/shard_map/ppermute | solution.py:102
  19.1 1.1 collective-permute-start.5
  20.2 0.1 collective-permute-start.4
  20.4 5.3 %collective-permute-done.3 = f32[1,264,256]{2,1,0:T(8,128)S(1)} collective-permute-done((f32[1,264,256]{2,1,0:T(8,128)S(1)}, f32[1,264,256]{2,1,0:T(8,128)S(1)}, u32[]{:S(2)}, u32[]{:S(2)}) %collective-permute-start.3) | collective-permute-done | bytes 270368 | tf_op jit(solution)/shard_map/ppermute | solution.py:102
  25.6 6.6 %collective-permute-done.5 = f32[1,264,256]{2,1,0:T(8,128)S(1)} collective-permute-done((f32[1,264,256]{2,1,0:T(8,128)S(1)}, f32[1,264,256]{2,1,0:T(8,128)S(1)}, u32[]{:S(2)}, u32[]{:S(2)}) %collective-permute-start.5) | collective-permute-done | bytes 270368 | tf_op jit(solution)/shard_map/ppermute | solution.py:102
  32.3 0.0 collective-permute-done.4
  32.3 0.1 fusion.3
  32.5 2.4 %collective-permute-start.6 = (f32[1,264,128]{2,1,0:T(8,128)S(1)}, f32[1,264,128]{2,1,0:T(8,128)S(1)}, u32[]{:S(2)}, u32[]{:S(2)}) collective-permute-start(f32[1,264,128]{2,1,0:T(8,128)S(1)} %slice.93), channel_id=1, source_target_pairs={{0,16},{1,17},{2,18},{3,19},{4,20},{5,21},{6,22},{7,23},{8,24},{9,... | collective-permute-start | bytes 405512 | tf_op jit(solution)/shard_map/ppermute | solution.py:102
  34.8 3.9 %collective-permute-done.6 = f32[1,264,128]{2,1,0:T(8,128)S(1)} collective-permute-done((f32[1,264,128]{2,1,0:T(8,128)S(1)}, f32[1,264,128]{2,1,0:T(8,128)S(1)}, u32[]{:S(2)}, u32[]{:S(2)}) %collective-permute-start.6) | collective-permute-done | bytes 135200 | tf_op jit(solution)/shard_map/ppermute | solution.py:102
  38.7 0.1 fusion.5
  38.9 1.3 collective-permute-start.7
  40.1 2.6 %collective-permute-done.7 = f32[1,264,128]{2,1,0:T(8,128)S(1)} collective-permute-done((f32[1,264,128]{2,1,0:T(8,128)S(1)}, f32[1,264,128]{2,1,0:T(8,128)S(1)}, u32[]{:S(2)}, u32[]{:S(2)}) %collective-permute-start.7) | collective-permute-done | bytes 135200 | tf_op jit(solution)/shard_map/ppermute | solution.py:102
  42.8 0.1 add_select_fusion.1
  43.0 1.0 collective-permute-start.8
  44.0 3.0 %collective-permute-done.8 = bf16[1,1,256,128]{3,2,1,0:T(8,128)(2,1)S(1)} collective-permute-done((bf16[1,1,256,128]{3,2,1,0:T(8,128)(2,1)S(1)}, bf16[1,1,256,128]{3,2,1,0:T(8,128)(2,1)S(1)}, u32[]{:S(2)}, u32[]{:S(2)}) %collective-permute-start.8) | collective-permute-done | bytes 65568 | tf_op jit(solution)/shard_map/ppermute | solution.py:102
  47.1 1.2 collective-permute-start.9
  48.3 2.7 %collective-permute-done.9 = bf16[1,2,256,128]{3,2,1,0:T(8,128)(2,1)S(1)} collective-permute-done((bf16[1,2,256,128]{3,2,1,0:T(8,128)(2,1)S(1)}, bf16[1,2,256,128]{3,2,1,0:T(8,128)(2,1)S(1)}, u32[]{:S(2)}, u32[]{:S(2)}) %collective-permute-start.9) | collective-permute-done | bytes 131104 | tf_op jit(solution)/shard_map/ppermute | solution.py:102
  51.0 4.4 %collective-permute-start.10 = (bf16[2,2,256,128]{3,2,1,0:T(8,128)(2,1)S(1)}, bf16[2,2,256,128]{3,2,1,0:T(8,128)(2,1)S(1)}, u32[]{:S(2)}, u32[]{:S(2)}) collective-permute-start(bf16[2,2,256,128]{3,2,1,0:T(8,128)(2,1)S(1)} %pad_maximum_fusion.2), channel_id=1, source_target_pairs={{0,4},{1,5},{2,6},{3,7},{4,0},{5,1},{6,2},{7,3},{8,12},{9,13},{10,... | collective-permute-start | bytes 786440 | tf_op jit(solution)/shard_map/ppermute | solution.py:102
  55.4 6.5 %collective-permute-start = (bf16[256,2048]{1,0:T(8,128)(2,1)S(1)}, bf16[256,2048]{1,0:T(8,128)(2,1)S(1)}, u32[]{:S(2)}, u32[]{:S(2)}) collective-permute-start(bf16[256,2048]{1,0:T(8,128)(2,1)S(1)} %get-tuple-element.8.bot_ref), channel_id=1, source_target_pairs={{0,1},{1,2},{2,3},{3,4},{4,5},{5,6},{6,7},{7,8},{8,9},{9,10},{10,1... | collective-permute-start | bytes 3145736 | tf_op jit(solution)/shard_map/ppermute | solution.py:181
  61.9 1.9 %collective-permute-start.1 = (bf16[256,2048]{1,0:T(8,128)(2,1)S(1)}, bf16[256,2048]{1,0:T(8,128)(2,1)S(1)}, u32[]{:S(2)}, u32[]{:S(2)}) collective-permute-start(bf16[256,2048]{1,0:T(8,128)(2,1)S(1)} %get-tuple-element.9.top_ref), channel_id=1, source_target_pairs={{1,0},{2,1},{3,2},{4,3},{5,4},{6,5},{7,6},{8,7},{9,8},{10,9},{11,1... | collective-permute-start | bytes 3145736 | tf_op jit(solution)/shard_map/ppermute | solution.py:182
  63.9 0.0 collective-permute-done.10
  63.9 0.1 pad_maximum_fusion.1
  63.9 3.2 %collective-permute-start.11 = (bf16[4,2,256,128]{3,2,1,0:T(8,128)(2,1)S(1)}, bf16[4,2,256,128]{3,2,1,0:T(8,128)(2,1)S(1)}, u32[]{:S(2)}, u32[]{:S(2)}) collective-permute-start(bf16[4,2,256,128]{3,2,1,0:T(8,128)(2,1)S(1)} %pad_maximum_fusion.1), channel_id=1, source_target_pairs={{0,1},{1,0},{2,3},{3,2},{4,5},{5,4},{6,7},{7,6},{8,9},{9,8},{10,11... | collective-permute-start | bytes 1572872 | tf_op jit(solution)/shard_map/ppermute | solution.py:102
  67.2 1.5 %collective-permute-done.11 = bf16[4,2,256,128]{3,2,1,0:T(8,128)(2,1)S(1)} collective-permute-done((bf16[4,2,256,128]{3,2,1,0:T(8,128)(2,1)S(1)}, bf16[4,2,256,128]{3,2,1,0:T(8,128)(2,1)S(1)}, u32[]{:S(2)}, u32[]{:S(2)}) %collective-permute-start.11) | collective-permute-done | bytes 524320 | tf_op jit(solution)/shard_map/ppermute | solution.py:102
  68.7 0.1 pad_maximum_fusion.g_ref
  68.8 16.1 %collective-permute-done.b_ref = bf16[256,2048]{1,0:T(8,128)(2,1)S(1)} collective-permute-done((bf16[256,2048]{1,0:T(8,128)(2,1)S(1)}, bf16[256,2048]{1,0:T(8,128)(2,1)S(1)}, u32[]{:S(2)}, u32[]{:S(2)}) %collective-permute-start) | collective-permute-done | bytes 1048608 | tf_op jit(solution)/shard_map/ppermute | solution.py:181
  84.9 1.6 %collective-permute-done.1.a_ref = bf16[256,2048]{1,0:T(8,128)(2,1)S(1)} collective-permute-done((bf16[256,2048]{1,0:T(8,128)(2,1)S(1)}, bf16[256,2048]{1,0:T(8,128)(2,1)S(1)}, u32[]{:S(2)}, u32[]{:S(2)}) %collective-permute-start.1) | collective-permute-done | bytes 1048608 | tf_op jit(solution)/shard_map/ppermute | solution.py:182
  86.5 51.5 %attend.1 = bf16[512,4096]{1,0:T(8,128)(2,1)} custom-call(s32[4]{0:T(128)S(1)} %pad_add_fusion.own, bf16[512,4096]{1,0:T(8,128)(2,1)} %q_ref.1, bf16[256,2048]{1,0:T(8,128)(2,1)S(1)} %collective-permute-done.b_ref, bf16[256,2048]{1,0:T(8,128)(2,1)S(1)} %get-tuple-element.9.top_ref, bf16[256,2048]{1,0:T(8,128)(2,1)S(1)} %get-tuple-element.8.bot_ref, ...), custom_call_target="tpu_custom_call" | custom-call | flops 10737418240 | bytes 16777216 | tf_op jit(solution)/shard_map/attend/pallas_call | solution.py:143
  (14 shorter events, 0.2 us)
Async XLA Ops:
  0.1 1.2 copy-start
  1.3 1.2 copy-start.1
  2.5 1.0 copy-start.2
  13.5 2.8 %collective-permute-start.2 = (f32[4,264,256]{2,1,0:T(8,128)S(1)}, f32[4,264,256]{2,1,0:T(8,128)S(1)}, u32[]{:S(2)}, u32[]{:S(2)}) collective-permute-start(f32[4,264,256]{2,1,0:T(8,128)S(1)} %slice.64), channel_id=1, source_target_pairs={{0,1},{1,0},{2,3},{3,2},{4,5},{5,4},{6,7},{7,6},{8,9},{9,8},{10,11... | collective-permute-start | bytes 3244040 | tf_op jit(solution)/shard_map/ppermute | solution.py:102
  16.6 9.0 %collective-permute-start.3 = (f32[1,264,256]{2,1,0:T(8,128)S(1)}, f32[1,264,256]{2,1,0:T(8,128)S(1)}, u32[]{:S(2)}, u32[]{:S(2)}) collective-permute-start(f32[1,264,256]{2,1,0:T(8,128)S(1)} %get-tuple-element.15), channel_id=1, source_target_pairs={{0,8},{1,9},{2,10},{3,11},{4,12},{5,13},{6,14},{7,15},{8,0},{9,1},... | collective-permute-start | bytes 811016 | tf_op jit(solution)/shard_map/ppermute | solution.py:102
  19.1 13.2 %collective-permute-start.5 = (f32[1,264,256]{2,1,0:T(8,128)S(1)}, f32[1,264,256]{2,1,0:T(8,128)S(1)}, u32[]{:S(2)}, u32[]{:S(2)}) collective-permute-start(f32[1,264,256]{2,1,0:T(8,128)S(1)} %get-tuple-element.16), channel_id=1, source_target_pairs={{0,12},{1,13},{2,14},{3,15},{4,8},{5,9},{6,10},{7,11},{8,4},{9,5},... | collective-permute-start | bytes 811016 | tf_op jit(solution)/shard_map/ppermute | solution.py:102
  20.2 12.1 %collective-permute-start.4 = (f32[1,264,256]{2,1,0:T(8,128)S(1)}, f32[1,264,256]{2,1,0:T(8,128)S(1)}, u32[]{:S(2)}, u32[]{:S(2)}) collective-permute-start(f32[1,264,256]{2,1,0:T(8,128)S(1)} %get-tuple-element.17), channel_id=1, source_target_pairs={{0,4},{1,5},{2,6},{3,7},{4,0},{5,1},{6,2},{7,3},{8,12},{9,13},{10,... | collective-permute-start | bytes 811016 | tf_op jit(solution)/shard_map/ppermute | solution.py:102
  32.5 6.3 %collective-permute-start.6 = (f32[1,264,128]{2,1,0:T(8,128)S(1)}, f32[1,264,128]{2,1,0:T(8,128)S(1)}, u32[]{:S(2)}, u32[]{:S(2)}) collective-permute-start(f32[1,264,128]{2,1,0:T(8,128)S(1)} %slice.93), channel_id=1, source_target_pairs={{0,16},{1,17},{2,18},{3,19},{4,20},{5,21},{6,22},{7,23},{8,24},{9,... | collective-permute-start | bytes 405512 | tf_op jit(solution)/shard_map/ppermute | solution.py:102
  38.9 3.9 %collective-permute-start.7 = (f32[1,264,128]{2,1,0:T(8,128)S(1)}, f32[1,264,128]{2,1,0:T(8,128)S(1)}, u32[]{:S(2)}, u32[]{:S(2)}) collective-permute-start(f32[1,264,128]{2,1,0:T(8,128)S(1)} %fusion.5), channel_id=1, source_target_pairs={{0,2},{1,3},{2,0},{3,1},{4,6},{5,7},{6,4},{7,5},{8,10},{9,11},{10,... | collective-permute-start | bytes 405512 | tf_op jit(solution)/shard_map/ppermute | solution.py:102
  43.0 4.1 %collective-permute-start.8 = (bf16[1,1,256,128]{3,2,1,0:T(8,128)(2,1)S(1)}, bf16[1,1,256,128]{3,2,1,0:T(8,128)(2,1)S(1)}, u32[]{:S(2)}, u32[]{:S(2)}) collective-permute-start(bf16[1,1,256,128]{3,2,1,0:T(8,128)(2,1)S(1)} %fusion.7), channel_id=1, source_target_pairs={{0,16},{1,17},{2,18},{3,19},{4,20},{5,21},{6,22},{7,23},{8,24},{9,... | collective-permute-start | bytes 196616 | tf_op jit(solution)/shard_map/ppermute | solution.py:102
  47.1 3.9 %collective-permute-start.9 = (bf16[1,2,256,128]{3,2,1,0:T(8,128)(2,1)S(1)}, bf16[1,2,256,128]{3,2,1,0:T(8,128)(2,1)S(1)}, u32[]{:S(2)}, u32[]{:S(2)}) collective-permute-start(bf16[1,2,256,128]{3,2,1,0:T(8,128)(2,1)S(1)} %pad_maximum_fusion.3), channel_id=1, source_target_pairs={{0,8},{1,9},{2,10},{3,11},{4,12},{5,13},{6,14},{7,15},{8,0},{9,1},... | collective-permute-start | bytes 393224 | tf_op jit(solution)/shard_map/ppermute | solution.py:102
  51.0 12.9 %collective-permute-start.10 = (bf16[2,2,256,128]{3,2,1,0:T(8,128)(2,1)S(1)}, bf16[2,2,256,128]{3,2,1,0:T(8,128)(2,1)S(1)}, u32[]{:S(2)}, u32[]{:S(2)}) collective-permute-start(bf16[2,2,256,128]{3,2,1,0:T(8,128)(2,1)S(1)} %pad_maximum_fusion.2), channel_id=1, source_target_pairs={{0,4},{1,5},{2,6},{3,7},{4,0},{5,1},{6,2},{7,3},{8,12},{9,13},{10,... | collective-permute-start | bytes 786440 | tf_op jit(solution)/shard_map/ppermute | solution.py:102
  55.4 29.5 %collective-permute-start = (bf16[256,2048]{1,0:T(8,128)(2,1)S(1)}, bf16[256,2048]{1,0:T(8,128)(2,1)S(1)}, u32[]{:S(2)}, u32[]{:S(2)}) collective-permute-start(bf16[256,2048]{1,0:T(8,128)(2,1)S(1)} %get-tuple-element.8.bot_ref), channel_id=1, source_target_pairs={{0,1},{1,2},{2,3},{3,4},{4,5},{5,6},{6,7},{7,8},{8,9},{9,10},{10,1... | collective-permute-start | bytes 3145736 | tf_op jit(solution)/shard_map/ppermute | solution.py:181
  61.9 24.6 %collective-permute-start.1 = (bf16[256,2048]{1,0:T(8,128)(2,1)S(1)}, bf16[256,2048]{1,0:T(8,128)(2,1)S(1)}, u32[]{:S(2)}, u32[]{:S(2)}) collective-permute-start(bf16[256,2048]{1,0:T(8,128)(2,1)S(1)} %get-tuple-element.9.top_ref), channel_id=1, source_target_pairs={{1,0},{2,1},{3,2},{4,3},{5,4},{6,5},{7,6},{8,7},{9,8},{10,9},{11,1... | collective-permute-start | bytes 3145736 | tf_op jit(solution)/shard_map/ppermute | solution.py:182
  63.9 4.8 %collective-permute-start.11 = (bf16[4,2,256,128]{3,2,1,0:T(8,128)(2,1)S(1)}, bf16[4,2,256,128]{3,2,1,0:T(8,128)(2,1)S(1)}, u32[]{:S(2)}, u32[]{:S(2)}) collective-permute-start(bf16[4,2,256,128]{3,2,1,0:T(8,128)(2,1)S(1)} %pad_maximum_fusion.1), channel_id=1, source_target_pairs={{0,1},{1,0},{2,3},{3,2},{4,5},{5,4},{6,7},{7,6},{8,9},{9,8},{10,11... | collective-permute-start | bytes 1572872 | tf_op jit(solution)/shard_map/ppermute | solution.py:102
where the time goes:
time: 138 us
  Pallas kernels  61.3 us (44%)
  waiting for transfers between devices  46.1 us (33%)
  starting transfers between devices  25.9 us (19%)
  local copies, waits for them, and re-layouts  3.65 us (3%)
    pallas_call x1, Pallas kernels, attend(): pl.pallas_call(attend_kernel, out_shape=jax.ShapeDtypeStruct(queries.shap...  51.5 us
    ppermute x10, waiting for transfers between devices, swap(): return lax.ppermute(x, 'ctx', [(i, i ^ bits) for i in range(peers)])  28.4 us
    ppermute x10, starting transfers between devices, swap(): return lax.ppermute(x, 'ctx', [(i, i ^ bits) for i in range(peers)])  17.4 us
    ppermute x1, waiting for transfers between devices, on_device(): before = lax.ppermute(near_bot, 'ctx', up)  16.1 us
    pallas_call x1, Pallas kernels, project(): pl.pallas_call(project_kernel, out_shape=(jax.ShapeDtypeStruct((HALF, KV...  9.82 us
    ppermute x1, starting transfers between devices, on_device(): before = lax.ppermute(near_bot, 'ctx', up)  6.53 us
    unnamed x8, local copies, waits for them, and re-layouts  3.5 us
  transfers between devices with their start and end apart: 12, of which 10 were waited for; matrix products, arithmetic and copies ran while one was open for 0% of the time, Pallas kernels for 0%

commit v1 on v0

v1 whole, which is shorter than its diff:
```python
import functools
import math

import jax
import jax.numpy as jnp
from jax import lax
from jax.experimental import pallas as pl
from jax.experimental.pallas import tpu as pltpu
from jax.sharding import PartitionSpec as P

H = 32
KV = 8
HD = 128
GROUP = H // KV
R = 256
HALF = 256
AUX = 8
ROWS = 2 * HD + AUX
T_ROW = 2 * HD
M_ROW = 2 * HD + 1
EXP2_SCALE = math.log2(math.e) / math.sqrt(HD)
FAR_AWAY = 1e30
BLOCKS = 5
PROJECT_VMEM = 60 << 20
ATTEND_VMEM = 48 << 20

HEAD_BITS = (8, 4, 1)
HALF_BIT = 2


def normalize(x):
    centered = x - jnp.mean(x, axis=-1, keepdims=True)
    spread = jnp.mean(centered * centered, axis=-1, keepdims=True)
    return centered * lax.rsqrt(spread + 1e-05)


def project_kernel(own, k_ref, v_ref, w0_ref, w1_ref, top_ref, bot_ref, part_ref):
    for i in range(2):
        side = (i ^ own[0]) & 1
        lane = pl.multiple_of(side * HD, HD)
        keys = k_ref[:, pl.ds(lane, HD)]
        values = v_ref[:, pl.ds(lane, HD)]
        near_k = normalize(keys.astype(jnp.float32)).astype(jnp.bfloat16)
        near_v = normalize(values.astype(jnp.float32)).astype(jnp.bfloat16)
        near = jnp.concatenate([near_k, near_v], axis=1)
        wide = pl.multiple_of(side * 2 * HD, 2 * HD)
        top_ref[:, pl.ds(wide, 2 * HD)] = near[:HALF]
        bot_ref[:, pl.ds(wide, 2 * HD)] = near[HALF:]
        weight = jnp.concatenate([w0_ref[side], w1_ref[side]], axis=1)
        logits = jnp.dot(near_k, weight, preferred_element_type=jnp.float32)
        top = jnp.max(logits, axis=0, keepdims=True)
        expo = jnp.exp(logits - top)
        total = jnp.sum(expo, axis=0, keepdims=True)
        upper = expo.astype(jnp.bfloat16)
        lower = (expo - upper.astype(jnp.float32)).astype(jnp.bfloat16)
        pair = jnp.concatenate([keys, values], axis=1)
        dims = (((0,), (0,)), ((), ()))
        both = lax.dot_general(pair, upper, dims, preferred_element_type=jnp.float32)
        both = both + lax.dot_general(pair, lower, dims, preferred_element_type=jnp.float32)
        part_ref[i, : 2 * HD] = both
        row = lax.broadcasted_iota(jnp.int32, (AUX, R), 0)
        part_ref[i, 2 * HD :] = jnp.where(row == 0, total, jnp.where(row == 1, top, 0.0))


def project(base, own, keys, values, proj_weight):
    tok = keys.shape[0]
    two = lambda i, own: (base + 2 * i ^ own[0]) // 2
    count = KV // 2
    wide = pl.BlockSpec((HALF, 4 * HD), lambda i, own: (0, two(i, own) % (count // 2)))
    return pl.pallas_call(
        project_kernel,
        out_shape=(
            jax.ShapeDtypeStruct((HALF, count * 2 * HD), jnp.bfloat16),
            jax.ShapeDtypeStruct((HALF, count * 2 * HD), jnp.bfloat16),
            jax.ShapeDtypeStruct((count, ROWS, R), jnp.float32),
        ),
        grid_spec=pltpu.PrefetchScalarGridSpec(
            num_scalar_prefetch=1,
            grid=(count // 2,),
            in_specs=[
                pl.BlockSpec((tok, 2 * HD), lambda i, own: (0, two(i, own))),
                pl.BlockSpec((tok, 2 * HD), lambda i, own: (0, two(i, own))),
                pl.BlockSpec((2, HD, R // 2), lambda i, own: (two(i, own), 0, own[1])),
                pl.BlockSpec((2, HD, R // 2), lambda i, own: (two(i, own), 0, 1 - own[1])),
            ],
            out_specs=[wide, wide, pl.BlockSpec((2, ROWS, R), lambda i, own: (i, 0, 0))],
        ),
        compiler_params=pltpu.CompilerParams(vmem_limit_bytes=PROJECT_VMEM),
        cost_estimate=pl.CostEstimate(
            flops=count * tok * R * HD * 10, bytes_accessed=4 << 20, transcendentals=count * tok * R
        ),
        name="project",
    )(own, keys, values, proj_weight, proj_weight)


def merge(parts):
    tops = [x[:, M_ROW : M_ROW + 1] for x in parts]
    top = functools.reduce(jnp.maximum, tops)
    row = lax.broadcasted_iota(jnp.int32, parts[0].shape, 1)
    added = sum(x * jnp.exp(t - top) for x, t in zip(parts, tops))
    return jnp.where(row == M_ROW, top, added)


def swap(x, bits):
    peers = lax.axis_size("ctx")
    return lax.ppermute(x, "ctx", [(i, i ^ bits) for i in range(peers)])


def attend_kernel(own, q_ref, b_ref, top_ref, bot_ref, a_ref, g_ref, *refs):
    o_ref, k_ref, v_ref = refs[-3:]
    hide = (
        jnp.where(own[2] > 0, 0.0, FAR_AWAY),
        0.0,
        0.0,
        jnp.where(own[3] > 0, 0.0, FAR_AWAY),
        0.0,
    )
    for i, x in enumerate((b_ref, top_ref, bot_ref, a_ref)):
        k_ref[i * HALF : (i + 1) * HALF] = x[:, :HD]
        v_ref[:, i * HALF : (i + 1) * HALF] = x[:, HD:].T
    for i in range(2):
        at = 4 * HALF + i * HD
        k_ref[at : at + HD] = g_ref[0, i, :HD].T
        v_ref[:, at : at + HD] = g_ref[0, i, HD:]
    flip = (((1,), (1,)), ((), ()))

    def score(g, i):
        return lax.dot_general(
            k_ref[i * HALF : (i + 1) * HALF],
            q_ref[:, g * HD : (g + 1) * HD],
            flip,
            preferred_element_type=jnp.float32,
        )

    scores = [score(0, i) for i in range(BLOCKS)]
    for g in range(GROUP):
        tops = [jnp.max(s, axis=0, keepdims=True) - w for s, w in zip(scores, hide)]
        top = functools.reduce(jnp.maximum, tops)
        ahead, expo, total = [], [], 0.0
        for i in range(BLOCKS):
            if g + 1 < GROUP:
                ahead.append(score(g + 1, i))
            e = jnp.exp2((scores[i] - (top + hide[i])) * EXP2_SCALE)
            total = total + jnp.sum(e, axis=0, keepdims=True)
            expo.append(e)
        inverse = 1.0 / total
        probs = jnp.concatenate([(e * inverse).astype(jnp.bfloat16) for e in expo], axis=0)
        mixed = jnp.dot(v_ref[...], probs, preferred_element_type=jnp.float32)
        o_ref[:, g * HD : (g + 1) * HD] = mixed.T.astype(jnp.bfloat16)
        scores = ahead


def attend(base, own, queries, before, top, bot, after, far, out=None):
    tok = queries.shape[0]
    count = far.shape[0]
    head = lambda i, own: base + i ^ own[0]
    near = pl.BlockSpec((HALF, 2 * HD), lambda i, own: (0, head(i, own) % (KV // 2)))
    extra = [] if out is None else [out]
    return pl.pallas_call(
        attend_kernel,
        out_shape=jax.ShapeDtypeStruct(queries.shape, jnp.bfloat16),
        grid_spec=pltpu.PrefetchScalarGridSpec(
            num_scalar_prefetch=1,
            grid=(count,),
            in_specs=[
                pl.BlockSpec((tok, GROUP * HD), lambda i, own: (0, head(i, own))),
                near,
                near,
                near,
                near,
                pl.BlockSpec((1, 2, 2 * HD, R // 2), lambda i, own: (i, 0, 0, 0)),
            ]
            + [pl.BlockSpec(memory_space=pl.ANY)] * len(extra),
            out_specs=pl.BlockSpec((tok, GROUP * HD), lambda i, own: (0, head(i, own))),
            scratch_shapes=[
                pltpu.VMEM((BLOCKS * HALF, HD), jnp.bfloat16),
                pltpu.VMEM((HD, BLOCKS * HALF), jnp.bfloat16),
            ],
        ),
        input_output_aliases={7: 0} if extra else {},
        compiler_params=pltpu.CompilerParams(vmem_limit_bytes=ATTEND_VMEM),
        cost_estimate=pl.CostEstimate(
            flops=4 * count * GROUP * tok * 1280 * HD,
            bytes_accessed=2 * count << 20,
            transcendentals=count * GROUP * tok * 1280,
        ),
        name="attend",
    )(own, queries, before, top, bot, after, far, *extra)


def on_device(queries, keys, values, proj_weight):
    peers = lax.axis_size("ctx")
    me = lax.axis_index("ctx")
    bit = lambda b: (me & b) // b
    own_head = sum(bit(b) << s for s, b in enumerate(HEAD_BITS))
    own = jnp.stack(
        [own_head, bit(HALF_BIT), (me > 0).astype(jnp.int32), (me < peers - 1).astype(jnp.int32)]
    ).astype(jnp.int32)
    b0, b1, b2 = HEAD_BITS
    up = [(i, i + 1) for i in range(peers - 1)]
    down = [(i + 1, i) for i in range(peers - 1)]
    top1, bot1, sent = project(KV // 2, own, keys, values, proj_weight)
    top0, bot0, kept = project(0, own, keys, values, proj_weight)
    before0 = lax.ppermute(bot1, "ctx", up)
    after0 = lax.ppermute(top1, "ctx", down)
    before1 = lax.ppermute(bot0, "ctx", up)
    after1 = lax.ppermute(top0, "ctx", down)
    part = merge([kept, swap(sent, b2)])
    part, before0, after0 = lax.optimization_barrier((part, before0, after0))
    pieces = []
    for place in range(KV // 2):
        for half in range(2):
            piece = part[place : place + 1, :, half * HD : (half + 1) * HD]
            bits = b0 * (place & 1) ^ b1 * (place >> 1) ^ HALF_BIT * half
            pieces.append(swap(piece, bits) if bits else piece)
    part = merge(pieces)
    rest = 1
    while rest < peers:
        if rest not in HEAD_BITS + (HALF_BIT,):
            part = merge([part, swap(part, rest)])
        rest *= 2
    far = (part[:, : 2 * HD] / part[:, T_ROW : T_ROW + 1]).astype(jnp.bfloat16)[:, None]
    at0 = jnp.concatenate([far, swap(far, HALF_BIT)], axis=1)
    near0 = (before0, top0, bot0, after0)
    at1 = swap(at0, b0)
    out = attend(0, own, queries, *near0, at0)
    at1, out, before1, after1 = lax.optimization_barrier((at1, out, before1, after1))
    near1 = (before1, top1, bot1, after1)
    out = attend(1, own, queries, *near0, at1, out)
    at01 = jnp.concatenate([at0, at1], axis=0)
    at23 = swap(at01, b1)
    at45 = swap(at01, b2)
    out = attend(4, own, queries, *near1, at45, out)
    at23, out = lax.optimization_barrier((at23, out))
    at67 = swap(at23, b2)
    out = attend(2, own, queries, *near0, at23, out)
    return attend(6, own, queries, *near1, at67, out)


def solution(mesh):
    in_specs = (P("ctx", None), P("ctx", None), P("ctx", None), P())
    out_specs = P("ctx", None)
    return jax.shard_map(
        on_device, mesh=mesh, in_specs=in_specs, out_specs=out_specs, check_vma=False
    )
```

time: 138 us -> 107 us (0.78)
  waiting for transfers between devices: 46.1 us -> 24.1 us
  Pallas kernels: 61.3 us -> 52.2 us
  local copies, waits for them, and re-layouts: 3.65 us -> 0.09 us
  other arithmetic: 0.93 us -> 3.25 us
    ppermute x2 -> x4, waiting for transfers between devices: 17.7 us -> 4.18 us  [the longest x1 4.17 us: on_device(): after0 = lax.ppermute(top1, 'ctx', down)]
    pallas_call x1 -> x5, Pallas kernels: 51.5 us -> 41.8 us  [attend(): pl.pallas_call(attend_kernel, out_shape=jax.ShapeDtypeStruct(queries.shap...]
    ppermute x10 -> x14, waiting for transfers between devices: 28.4 us -> 19.9 us  [swap(): return lax.ppermute(x, 'ctx', [(i, i ^ bits) for i in range(peers)])]
    ppermute x2 -> x4, starting transfers between devices: 8.45 us -> 12.1 us  [the longest x1 4.45 us: on_device(): before0 = lax.ppermute(bot1, 'ctx', up)]
    unnamed x8 -> x12, local copies, waits for them, and re-layouts: 3.5 us -> 0.03 us
    ppermute x10 -> x14, starting transfers between devices: 17.4 us -> 14.3 us  [swap(): return lax.ppermute(x, 'ctx', [(i, i ^ bits) for i in range(peers)])]
    pallas_call x1 -> x2, Pallas kernels: 9.82 us -> 10.4 us  [project(): pl.pallas_call(project_kernel, out_shape=(jax.ShapeDtypeStruct((HALF, cou...]
  transfers between devices with their start and end apart: 12 -> 18, of which waited for: 10 -> 8; matrix products, arithmetic and copies ran while one was open for 0% -> 2% of each run, Pallas kernels for 0% -> 35%
where the time goes in v1:
time: 107 us; the launch traced here: 106 us
  Pallas kernels  52.2 us (49%)
  starting transfers between devices  26.5 us (25%)
  waiting for transfers between devices  24.1 us (23%)
  other arithmetic  3.25 us (3%)
    pallas_call x5, Pallas kernels, attend(): pl.pallas_call(attend_kernel, out_shape=jax.ShapeDtypeStruct(queries.shap...  41.8 us
    ppermute x14, waiting for transfers between devices, swap(): return lax.ppermute(x, 'ctx', [(i, i ^ bits) for i in range(peers)])  19.9 us
    ppermute x14, starting transfers between devices, swap(): return lax.ppermute(x, 'ctx', [(i, i ^ bits) for i in range(peers)])  14.3 us
    pallas_call x2, Pallas kernels, project(): pl.pallas_call(project_kernel, out_shape=(jax.ShapeDtypeStruct((HALF, cou...  10.4 us
    ppermute x1, starting transfers between devices, on_device(): before0 = lax.ppermute(bot1, 'ctx', up)  4.45 us
    ppermute x1, waiting for transfers between devices, on_device(): after0 = lax.ppermute(top1, 'ctx', down)  4.17 us
    ppermute x1, starting transfers between devices, on_device(): before1 = lax.ppermute(bot0, 'ctx', up)  3.21 us
    ppermute x1, starting transfers between devices, on_device(): after1 = lax.ppermute(top0, 'ctx', down)  2.53 us
  transfers between devices with their start and end apart: 18, of which 8 were waited for; matrix products, arithmetic and copies ran while one was open for 2% of the time, Pallas kernels for 35%

profile of v1, /device:TPU:1, one launch (start us, length us, event | category | flops | bytes accessed | tf_op | source)
XLA Modules:
  0.0 106.3 jit_solution(355462279453063823)
XLA Ops:
  0.0 0.7 pad_add_fusion.own
  0.7 5.2 %project.3 = (bf16[256,1024]{1,0:T(8,128)(2,1)}, bf16[256,1024]{1,0:T(8,128)(2,1)}, f32[4,264,256]{2,1,0:T(8,128)}) custom-call(s32[4]{0:T(128)} %pad_add_fusion.own, bf16[512,1024]{1,0:T(8,128)(2,1)} %k_ref.3, bf16[512,1024]{1,0:T(8,128)(2,1)} %v_ref.3, bf16[8,128,256]{2,1,0:T(8,128)(2,1)} %w1_ref.3, bf16[8,128,256]{2,1,0:T(8,128)(2,1)} %w1_ref.3), custom_call_target="tpu_custom_call" | custom-call | flops 671088640 | bytes 4194304 | tf_op jit(solution)/shard_map/project/pallas_call | solution.py:70
  5.9 0.1 collective-permute-start
  6.0 4.5 %collective-permute-start.1 = (bf16[256,1024]{1,0:T(8,128)(2,1)}, bf16[256,1024]{1,0:T(8,128)(2,1)S(1)}, u32[]{:S(2)}, u32[]{:S(2)}) collective-permute-start(bf16[256,1024]{1,0:T(8,128)(2,1)} %get-tuple-element.22.bot_ref), channel_id=1, source_target_pairs={{0,1},{1,2},{2,3},{3,4},{4,5},{5,6},{6,7},{7,8},{8,9},{9,10},{10,1... | collective-permute-start | bytes 1572872 | tf_op jit(solution)/shard_map/ppermute | solution.py:204
  10.4 1.9 %collective-permute-start.2 = (bf16[256,1024]{1,0:T(8,128)(2,1)}, bf16[256,1024]{1,0:T(8,128)(2,1)S(1)}, u32[]{:S(2)}, u32[]{:S(2)}) collective-permute-start(bf16[256,1024]{1,0:T(8,128)(2,1)} %get-tuple-element.23.top_ref), channel_id=1, source_target_pairs={{1,0},{2,1},{3,2},{4,3},{5,4},{6,5},{7,6},{8,7},{9,8},{10,9},{11,1... | collective-permute-start | bytes 1572872 | tf_op jit(solution)/shard_map/ppermute | solution.py:205
  12.4 5.2 %project.2 = (bf16[256,1024]{1,0:T(8,128)(2,1)}, bf16[256,1024]{1,0:T(8,128)(2,1)}, f32[4,264,256]{2,1,0:T(8,128)}) custom-call(s32[4]{0:T(128)} %pad_add_fusion.own, bf16[512,1024]{1,0:T(8,128)(2,1)} %k_ref.3, bf16[512,1024]{1,0:T(8,128)(2,1)} %v_ref.3, bf16[8,128,256]{2,1,0:T(8,128)(2,1)} %w1_ref.3, bf16[8,128,256]{2,1,0:T(8,128)(2,1)} %w1_ref.3), custom_call_target="tpu_custom_call" | custom-call | flops 671088640 | bytes 4194304 | tf_op jit(solution)/shard_map/project/pallas_call | solution.py:70
  17.5 0.0 collective-permute-done
  17.5 0.8 subtract_exponential_fusion.1
  18.4 1.4 %add_select_fusion = f32[4,264,256]{2,1,0:T(8,128)S(1)} fusion(f32[4,264,256]{2,1,0:T(8,128)S(1)} %collective-permute-done, f32[4,264,256]{2,1,0:T(8,128)} %get-tuple-element.20, f32[4,256]{1,0:T(4,128)S(1)} %bitcast.38, f32[4,256]{1,0:T(4,128)S(1)} %get-tuple-element.56, f32[4,256]{1,0:T(4,128)S(1)} %get-tuple-element.57, pred[264]{0:T(512)(128)(4,1)S(1)} %iota_compare_fusion), kind=kLoop, calls=%fused_computation | loop fusion | flops 1081344 | bytes 3256584 | tf_op jit(solution)/shard_map/jit(_where)/select_n | solution.py:101
  19.8 0.0 collective-permute-done.1.b_ref
  19.8 4.2 %collective-permute-done.2.a_ref = bf16[256,1024]{1,0:T(8,128)(2,1)S(1)} collective-permute-done((bf16[256,1024]{1,0:T(8,128)(2,1)}, bf16[256,1024]{1,0:T(8,128)(2,1)S(1)}, u32[]{:S(2)}, u32[]{:S(2)}) %collective-permute-start.2) | collective-permute-done | bytes 524320 | tf_op jit(solution)/shard_map/ppermute | solution.py:205
  24.0 0.1 fusion.3
  24.0 0.0 copy-start
  24.0 0.0 copy-start.1
  24.1 0.0 copy-start.4
  24.1 1.3 %collective-permute-start.3 = (f32[1,264,128]{2,1,0:T(8,128)S(1)}, f32[1,264,128]{2,1,0:T(8,128)S(1)}, u32[]{:S(2)}, u32[]{:S(2)}) collective-permute-start(f32[1,264,128]{2,1,0:T(8,128)S(1)} %get-tuple-element.39), channel_id=1, source_target_pairs={{0,2},{1,3},{2,0},{3,1},{4,6},{5,7},{6,4},{7,5},{8,10},{9,11},{10,... | collective-permute-start | bytes 405512 | tf_op jit(solution)/shard_map/ppermute | solution.py:106
  25.3 2.1 %collective-permute-start.9 = (f32[1,264,128]{2,1,0:T(8,128)S(1)}, f32[1,264,128]{2,1,0:T(8,128)S(1)}, u32[]{:S(2)}, u32[]{:S(2)}) collective-permute-start(f32[1,264,128]{2,1,0:T(8,128)S(1)} %get-tuple-element.40), channel_id=1, source_target_pairs={{0,14},{1,15},{2,12},{3,13},{4,10},{5,11},{6,8},{7,9},{8,6},{9,7},... | collective-permute-start | bytes 405512 | tf_op jit(solution)/shard_map/ppermute | solution.py:106
  27.5 0.2 collective-permute-start.8
  27.7 1.2 %collective-permute-start.7 = (f32[1,264,128]{2,1,0:T(8,128)S(1)}, f32[1,264,128]{2,1,0:T(8,128)S(1)}, u32[]{:S(2)}, u32[]{:S(2)}) collective-permute-start(f32[1,264,128]{2,1,0:T(8,128)S(1)} %get-tuple-element.42), channel_id=1, source_target_pairs={{0,6},{1,7},{2,4},{3,5},{4,2},{5,3},{6,0},{7,1},{8,14},{9,15},{10,... | collective-permute-start | bytes 405512 | tf_op jit(solution)/shard_map/ppermute | solution.py:106
  28.9 1.2 %collective-permute-start.6 = (f32[1,264,128]{2,1,0:T(8,128)S(1)}, f32[1,264,128]{2,1,0:T(8,128)S(1)}, u32[]{:S(2)}, u32[]{:S(2)}) collective-permute-start(f32[1,264,128]{2,1,0:T(8,128)S(1)} %get-tuple-element.43), channel_id=1, source_target_pairs={{0,4},{1,5},{2,6},{3,7},{4,0},{5,1},{6,2},{7,3},{8,12},{9,13},{10,... | collective-permute-start | bytes 405512 | tf_op jit(solution)/shard_map/ppermute | solution.py:106
  30.1 1.5 %collective-permute-done.3 = f32[1,264,128]{2,1,0:T(8,128)S(1)} collective-permute-done((f32[1,264,128]{2,1,0:T(8,128)S(1)}, f32[1,264,128]{2,1,0:T(8,128)S(1)}, u32[]{:S(2)}, u32[]{:S(2)}) %collective-permute-start.3) | collective-permute-done | bytes 135200 | tf_op jit(solution)/shard_map/ppermute | solution.py:106
  31.6 2.8 %collective-permute-start.5 = (f32[1,264,128]{2,1,0:T(8,128)S(1)}, f32[1,264,128]{2,1,0:T(8,128)S(1)}, u32[]{:S(2)}, u32[]{:S(2)}) collective-permute-start(f32[1,264,128]{2,1,0:T(8,128)S(1)} %get-tuple-element.44), channel_id=1, source_target_pairs={{0,10},{1,11},{2,8},{3,9},{4,14},{5,15},{6,12},{7,13},{8,2},{9,3},... | collective-permute-start | bytes 405512 | tf_op jit(solution)/shard_map/ppermute | solution.py:106
  34.4 0.0 collective-permute-done.9
  34.4 0.7 collective-permute-start.4
  35.1 1.6 %collective-permute-done.8 = f32[1,264,128]{2,1,0:T(8,128)S(1)} collective-permute-done((f32[1,264,128]{2,1,0:T(8,128)S(1)}, f32[1,264,128]{2,1,0:T(8,128)S(1)}, u32[]{:S(2)}, u32[]{:S(2)}) %collective-permute-start.8) | collective-permute-done | bytes 135200 | tf_op jit(solution)/shard_map/ppermute | solution.py:106
  36.7 3.9 %collective-permute-done.7 = f32[1,264,128]{2,1,0:T(8,128)S(1)} collective-permute-done((f32[1,264,128]{2,1,0:T(8,128)S(1)}, f32[1,264,128]{2,1,0:T(8,128)S(1)}, u32[]{:S(2)}, u32[]{:S(2)}) %collective-permute-start.7) | collective-permute-done | bytes 135200 | tf_op jit(solution)/shard_map/ppermute | solution.py:106
  40.6 0.4 collective-permute-done.6
  41.1 0.0 collective-permute-done.5
  41.1 0.2 collective-permute-done.4
  41.3 0.1 add_select_fusion.2
  41.4 2.7 %collective-permute-start.10 = (f32[1,264,128]{2,1,0:T(8,128)S(1)}, f32[1,264,128]{2,1,0:T(8,128)S(1)}, u32[]{:S(2)}, u32[]{:S(2)}) collective-permute-start(f32[1,264,128]{2,1,0:T(8,128)S(1)} %add_select_fusion.2), channel_id=1, source_target_pairs={{0,16},{1,17},{2,18},{3,19},{4,20},{5,21},{6,22},{7,23},{8,24},{9,... | collective-permute-start | bytes 405512 | tf_op jit(solution)/shard_map/ppermute | solution.py:106
  44.1 0.0 copy-done
  44.1 2.5 %collective-permute-start.14 = (bf16[256,1024]{1,0:T(8,128)(2,1)S(1)}, bf16[256,1024]{1,0:T(8,128)(2,1)S(1)}, u32[]{:S(2)}, u32[]{:S(2)}) collective-permute-start(bf16[256,1024]{1,0:T(8,128)(2,1)S(1)} %copy-done), channel_id=1, source_target_pairs={{1,0},{2,1},{3,2},{4,3},{5,4},{6,5},{7,6},{8,7},{9,8},{10,9},{11,1... | collective-permute-start | bytes 1572872 | tf_op jit(solution)/shard_map/ppermute | solution.py:207
  46.6 0.0 copy-done.1
  46.7 3.2 %collective-permute-start.13 = (bf16[256,1024]{1,0:T(8,128)(2,1)S(1)}, bf16[256,1024]{1,0:T(8,128)(2,1)S(1)}, u32[]{:S(2)}, u32[]{:S(2)}) collective-permute-start(bf16[256,1024]{1,0:T(8,128)(2,1)S(1)} %copy-done.1), channel_id=1, source_target_pairs={{0,1},{1,2},{2,3},{3,4},{4,5},{5,6},{6,7},{7,8},{8,9},{9,10},{10,1... | collective-permute-start | bytes 1572872 | tf_op jit(solution)/shard_map/ppermute | solution.py:206
  49.9 0.8 collective-permute-done.10
  50.7 0.1 add_select_fusion.1
  50.9 0.4 collective-permute-start.11
  51.3 11.4 %collective-permute-done.11 = bf16[1,1,256,128]{3,2,1,0:T(8,128)(2,1)S(1)} collective-permute-done((bf16[1,1,256,128]{3,2,1,0:T(8,128)(2,1)S(1)}, bf16[1,1,256,128]{3,2,1,0:T(8,128)(2,1)S(1)}, u32[]{:S(2)}, u32[]{:S(2)}) %collective-permute-start.11) | collective-permute-done | bytes 65568 | tf_op jit(solution)/shard_map/ppermute | solution.py:106
  62.7 0.4 collective-permute-start.12
  63.1 0.0 copy-done.4
  63.1 6.1 %attend.5.refs_0_ = bf16[512,4096]{1,0:T(8,128)(2,1)} custom-call(s32[4]{0:T(128)S(1)} %copy-done.4, bf16[512,4096]{1,0:T(8,128)(2,1)} %q_ref.9, bf16[256,1024]{1,0:T(8,128)(2,1)S(1)} %collective-permute-done.1.b_ref, bf16[256,1024]{1,0:T(8,128)(2,1)S(1)} %copy-done, bf16[256,1024]{1,0:T(8,128)(2,1)S(1)} %copy-done.1, ...), custom_call_target="tpu_custom_call" | custom-call | flops 1342177280 | bytes 2097152 | tf_op jit(solution)/shard_map/attend/pallas_call | solution.py:159
  69.2 0.0 collective-permute-done.14.a_ref
  69.2 0.0 collective-permute-done.13.b_ref
  69.2 0.0 collective-permute-done.12.g_ref
  69.3 0.0 copy-start.2
  69.3 0.0 copy-start.3
  69.3 0.1 collective-permute-start.16
  69.4 0.9 collective-permute-start.15
  70.2 6.1 %attend.6.refs_0_ = bf16[512,4096]{1,0:T(8,128)(2,1)} custom-call(s32[4]{0:T(128)S(1)} %copy-done.4, bf16[512,4096]{1,0:T(8,128)(2,1)} %q_ref.9, bf16[256,1024]{1,0:T(8,128)(2,1)S(1)} %collective-permute-done.1.b_ref, bf16[256,1024]{1,0:T(8,128)(2,1)S(1)} %copy-done, bf16[256,1024]{1,0:T(8,128)(2,1)S(1)} %copy-done.1, ...), custom_call_target="tpu_custom_call", output_to_operand_aliasing={{}: (7, {})} | custom-call | flops 1342177280 | bytes 2097152 | tf_op jit(solution)/shard_map/attend/pallas_call | solution.py:159
  76.3 0.0 collective-permute-done.16.g_ref
  76.3 0.0 copy-done.2
  76.3 0.0 copy-done.3
  76.3 10.0 %attend.7.refs_0_ = bf16[512,4096]{1,0:T(8,128)(2,1)} custom-call(s32[4]{0:T(128)S(1)} %copy-done.4, bf16[512,4096]{1,0:T(8,128)(2,1)} %q_ref.9, bf16[256,1024]{1,0:T(8,128)(2,1)S(1)} %collective-permute-done.13.b_ref, bf16[256,1024]{1,0:T(8,128)(2,1)S(1)} %copy-done.2, bf16[256,1024]{1,0:T(8,128)(2,1)S(1)} %copy-done.3, ...), custom_call_target="tpu_custom_call", output_to_operand_aliasing={{}: (7, {})} | custom-call | flops 2684354560 | bytes 4194304 | tf_op jit(solution)/shard_map/attend/pallas_call | solution.py:159
  86.3 0.0 collective-permute-done.15.g_ref
  86.3 0.3 collective-permute-start.17
  86.7 9.8 %attend.8.refs_0_ = bf16[512,4096]{1,0:T(8,128)(2,1)} custom-call(s32[4]{0:T(128)S(1)} %copy-done.4, bf16[512,4096]{1,0:T(8,128)(2,1)} %q_ref.9, bf16[256,1024]{1,0:T(8,128)(2,1)S(1)} %collective-permute-done.1.b_ref, bf16[256,1024]{1,0:T(8,128)(2,1)S(1)} %copy-done, bf16[256,1024]{1,0:T(8,128)(2,1)S(1)} %copy-done.1, ...), custom_call_target="tpu_custom_call", output_to_operand_aliasing={{}: (7, {})} | custom-call | flops 2684354560 | bytes 4194304 | tf_op jit(solution)/shard_map/attend/pallas_call | solution.py:159
  96.5 0.0 collective-permute-done.17.g_ref
  96.5 9.8 %attend.9 = bf16[512,4096]{1,0:T(8,128)(2,1)} custom-call(s32[4]{0:T(128)S(1)} %copy-done.4, bf16[512,4096]{1,0:T(8,128)(2,1)} %q_ref.9, bf16[256,1024]{1,0:T(8,128)(2,1)S(1)} %collective-permute-done.13.b_ref, bf16[256,1024]{1,0:T(8,128)(2,1)S(1)} %copy-done.2, bf16[256,1024]{1,0:T(8,128)(2,1)S(1)} %copy-done.3, ...), custom_call_target="tpu_custom_call", output_to_operand_aliasing={{}: (7, {})} | custom-call | flops 2684354560 | bytes 4194304 | tf_op jit(solution)/shard_map/attend/pallas_call | solution.py:159
  (11 shorter events, 0.1 us)
Async XLA Ops:
  5.9 11.6 %collective-permute-start = (f32[4,264,256]{2,1,0:T(8,128)}, f32[4,264,256]{2,1,0:T(8,128)S(1)}, u32[]{:S(2)}, u32[]{:S(2)}) collective-permute-start(f32[4,264,256]{2,1,0:T(8,128)} %get-tuple-element.21), channel_id=1, source_target_pairs={{0,1},{1,0},{2,3},{3,2},{4,5},{5,4},{6,7},{7,6},{8,9},{9,8},{10,11... | collective-permute-start | bytes 3244040 | tf_op jit(solution)/shard_map/ppermute | solution.py:106
  6.0 13.8 %collective-permute-start.1 = (bf16[256,1024]{1,0:T(8,128)(2,1)}, bf16[256,1024]{1,0:T(8,128)(2,1)S(1)}, u32[]{:S(2)}, u32[]{:S(2)}) collective-permute-start(bf16[256,1024]{1,0:T(8,128)(2,1)} %get-tuple-element.22.bot_ref), channel_id=1, source_target_pairs={{0,1},{1,2},{2,3},{3,4},{4,5},{5,6},{6,7},{7,8},{8,9},{9,10},{10,1... | collective-permute-start | bytes 1572872 | tf_op jit(solution)/shard_map/ppermute | solution.py:204
  10.4 13.5 %collective-permute-start.2 = (bf16[256,1024]{1,0:T(8,128)(2,1)}, bf16[256,1024]{1,0:T(8,128)(2,1)S(1)}, u32[]{:S(2)}, u32[]{:S(2)}) collective-permute-start(bf16[256,1024]{1,0:T(8,128)(2,1)} %get-tuple-element.23.top_ref), channel_id=1, source_target_pairs={{1,0},{2,1},{3,2},{4,3},{5,4},{6,5},{7,6},{8,7},{9,8},{10,9},{11,1... | collective-permute-start | bytes 1572872 | tf_op jit(solution)/shard_map/ppermute | solution.py:205
  24.0 20.1 %copy-start = (bf16[256,1024]{1,0:T(8,128)(2,1)S(1)}, bf16[256,1024]{1,0:T(8,128)(2,1)}, u32[]{:S(2)}) copy-start(bf16[256,1024]{1,0:T(8,128)(2,1)} %get-tuple-element.26.top_ref) | copy-start | bytes 1572868
  24.0 22.6 %copy-start.1 = (bf16[256,1024]{1,0:T(8,128)(2,1)S(1)}, bf16[256,1024]{1,0:T(8,128)(2,1)}, u32[]{:S(2)}) copy-start(bf16[256,1024]{1,0:T(8,128)(2,1)} %get-tuple-element.27.bot_ref) | copy-start | bytes 1572868
  24.1 39.1 %copy-start.4 = (s32[4]{0:T(128)S(1)}, s32[4]{0:T(128)}, u32[]{:S(2)}) copy-start(s32[4]{0:T(128)} %pad_add_fusion.own) | copy-start | bytes 52
  24.1 7.5 %collective-permute-start.3 = (f32[1,264,128]{2,1,0:T(8,128)S(1)}, f32[1,264,128]{2,1,0:T(8,128)S(1)}, u32[]{:S(2)}, u32[]{:S(2)}) collective-permute-start(f32[1,264,128]{2,1,0:T(8,128)S(1)} %get-tuple-element.39), channel_id=1, source_target_pairs={{0,2},{1,3},{2,0},{3,1},{4,6},{5,7},{6,4},{7,5},{8,10},{9,11},{10,... | collective-permute-start | bytes 405512 | tf_op jit(solution)/shard_map/ppermute | solution.py:106
  25.3 9.1 %collective-permute-start.9 = (f32[1,264,128]{2,1,0:T(8,128)S(1)}, f32[1,264,128]{2,1,0:T(8,128)S(1)}, u32[]{:S(2)}, u32[]{:S(2)}) collective-permute-start(f32[1,264,128]{2,1,0:T(8,128)S(1)} %get-tuple-element.40), channel_id=1, source_target_pairs={{0,14},{1,15},{2,12},{3,13},{4,10},{5,11},{6,8},{7,9},{8,6},{9,7},... | collective-permute-start | bytes 405512 | tf_op jit(solution)/shard_map/ppermute | solution.py:106
  27.5 9.2 %collective-permute-start.8 = (f32[1,264,128]{2,1,0:T(8,128)S(1)}, f32[1,264,128]{2,1,0:T(8,128)S(1)}, u32[]{:S(2)}, u32[]{:S(2)}) collective-permute-start(f32[1,264,128]{2,1,0:T(8,128)S(1)} %get-tuple-element.41), channel_id=1, source_target_pairs={{0,12},{1,13},{2,14},{3,15},{4,8},{5,9},{6,10},{7,11},{8,4},{9,5},... | collective-permute-start | bytes 405512 | tf_op jit(solution)/shard_map/ppermute | solution.py:106
  27.7 13.0 %collective-permute-start.7 = (f32[1,264,128]{2,1,0:T(8,128)S(1)}, f32[1,264,128]{2,1,0:T(8,128)S(1)}, u32[]{:S(2)}, u32[]{:S(2)}) collective-permute-start(f32[1,264,128]{2,1,0:T(8,128)S(1)} %get-tuple-element.42), channel_id=1, source_target_pairs={{0,6},{1,7},{2,4},{3,5},{4,2},{5,3},{6,0},{7,1},{8,14},{9,15},{10,... | collective-permute-start | bytes 405512 | tf_op jit(solution)/shard_map/ppermute | solution.py:106
  28.9 12.2 %collective-permute-start.6 = (f32[1,264,128]{2,1,0:T(8,128)S(1)}, f32[1,264,128]{2,1,0:T(8,128)S(1)}, u32[]{:S(2)}, u32[]{:S(2)}) collective-permute-start(f32[1,264,128]{2,1,0:T(8,128)S(1)} %get-tuple-element.43), channel_id=1, source_target_pairs={{0,4},{1,5},{2,6},{3,7},{4,0},{5,1},{6,2},{7,3},{8,12},{9,13},{10,... | collective-permute-start | bytes 405512 | tf_op jit(solution)/shard_map/ppermute | solution.py:106
  31.6 9.5 %collective-permute-start.5 = (f32[1,264,128]{2,1,0:T(8,128)S(1)}, f32[1,264,128]{2,1,0:T(8,128)S(1)}, u32[]{:S(2)}, u32[]{:S(2)}) collective-permute-start(f32[1,264,128]{2,1,0:T(8,128)S(1)} %get-tuple-element.44), channel_id=1, source_target_pairs={{0,10},{1,11},{2,8},{3,9},{4,14},{5,15},{6,12},{7,13},{8,2},{9,3},... | collective-permute-start | bytes 405512 | tf_op jit(solution)/shard_map/ppermute | solution.py:106
  34.4 6.8 %collective-permute-start.4 = (f32[1,264,128]{2,1,0:T(8,128)S(1)}, f32[1,264,128]{2,1,0:T(8,128)S(1)}, u32[]{:S(2)}, u32[]{:S(2)}) collective-permute-start(f32[1,264,128]{2,1,0:T(8,128)S(1)} %get-tuple-element.45), channel_id=1, source_target_pairs={{0,8},{1,9},{2,10},{3,11},{4,12},{5,13},{6,14},{7,15},{8,0},{9,1},... | collective-permute-start | bytes 405512 | tf_op jit(solution)/shard_map/ppermute | solution.py:106
  41.4 9.2 %collective-permute-start.10 = (f32[1,264,128]{2,1,0:T(8,128)S(1)}, f32[1,264,128]{2,1,0:T(8,128)S(1)}, u32[]{:S(2)}, u32[]{:S(2)}) collective-permute-start(f32[1,264,128]{2,1,0:T(8,128)S(1)} %add_select_fusion.2), channel_id=1, source_target_pairs={{0,16},{1,17},{2,18},{3,19},{4,20},{5,21},{6,22},{7,23},{8,24},{9,... | collective-permute-start | bytes 405512 | tf_op jit(solution)/shard_map/ppermute | solution.py:106
  44.1 25.1 %collective-permute-start.14 = (bf16[256,1024]{1,0:T(8,128)(2,1)S(1)}, bf16[256,1024]{1,0:T(8,128)(2,1)S(1)}, u32[]{:S(2)}, u32[]{:S(2)}) collective-permute-start(bf16[256,1024]{1,0:T(8,128)(2,1)S(1)} %copy-done), channel_id=1, source_target_pairs={{1,0},{2,1},{3,2},{4,3},{5,4},{6,5},{7,6},{8,7},{9,8},{10,9},{11,1... | collective-permute-start | bytes 1572872 | tf_op jit(solution)/shard_map/ppermute | solution.py:207
  46.7 22.6 %collective-permute-start.13 = (bf16[256,1024]{1,0:T(8,128)(2,1)S(1)}, bf16[256,1024]{1,0:T(8,128)(2,1)S(1)}, u32[]{:S(2)}, u32[]{:S(2)}) collective-permute-start(bf16[256,1024]{1,0:T(8,128)(2,1)S(1)} %copy-done.1), channel_id=1, source_target_pairs={{0,1},{1,2},{2,3},{3,4},{4,5},{5,6},{6,7},{7,8},{8,9},{9,10},{10,1... | collective-permute-start | bytes 1572872 | tf_op jit(solution)/shard_map/ppermute | solution.py:206
  50.9 11.9 %collective-permute-start.11 = (bf16[1,1,256,128]{3,2,1,0:T(8,128)(2,1)S(1)}, bf16[1,1,256,128]{3,2,1,0:T(8,128)(2,1)S(1)}, u32[]{:S(2)}, u32[]{:S(2)}) collective-permute-start(bf16[1,1,256,128]{3,2,1,0:T(8,128)(2,1)S(1)} %fusion.1), channel_id=1, source_target_pairs={{0,2},{1,3},{2,0},{3,1},{4,6},{5,7},{6,4},{7,5},{8,10},{9,11},{10,... | collective-permute-start | bytes 196616 | tf_op jit(solution)/shard_map/ppermute | solution.py:106
  62.7 6.5 %collective-permute-start.12 = (bf16[1,2,256,128]{3,2,1,0:T(8,128)(2,1)S(1)}, bf16[1,2,256,128]{3,2,1,0:T(8,128)(2,1)S(1)}, u32[]{:S(2)}, u32[]{:S(2)}) collective-permute-start(bf16[1,2,256,128]{3,2,1,0:T(8,128)(2,1)S(1)} %pad_maximum_fusion.1.g_ref), channel_id=1, source_target_pairs={{0,8},{1,9},{2,10},{3,11},{4,12},{5,13},{6,14},{7,15},{8,0},{9,1},... | collective-permute-start | bytes 393224 | tf_op jit(solution)/shard_map/ppermute | solution.py:106
  69.3 7.0 %copy-start.2 = (bf16[256,1024]{1,0:T(8,128)(2,1)S(1)}, bf16[256,1024]{1,0:T(8,128)(2,1)}, u32[]{:S(2)}) copy-start(bf16[256,1024]{1,0:T(8,128)(2,1)} %get-tuple-element.23.top_ref) | copy-start | bytes 1572868
  69.3 7.0 %copy-start.3 = (bf16[256,1024]{1,0:T(8,128)(2,1)S(1)}, bf16[256,1024]{1,0:T(8,128)(2,1)}, u32[]{:S(2)}) copy-start(bf16[256,1024]{1,0:T(8,128)(2,1)} %get-tuple-element.22.bot_ref) | copy-start | bytes 1572868
  69.3 7.0 %collective-permute-start.16 = (bf16[2,2,256,128]{3,2,1,0:T(8,128)(2,1)S(1)}, bf16[2,2,256,128]{3,2,1,0:T(8,128)(2,1)S(1)}, u32[]{:S(2)}, u32[]{:S(2)}) collective-permute-start(bf16[2,2,256,128]{3,2,1,0:T(8,128)(2,1)S(1)} %pad_maximum_fusion), channel_id=1, source_target_pairs={{0,1},{1,0},{2,3},{3,2},{4,5},{5,4},{6,7},{7,6},{8,9},{9,8},{10,11... | collective-permute-start | bytes 786440 | tf_op jit(solution)/shard_map/ppermute | solution.py:106
  69.4 17.0 %collective-permute-start.15 = (bf16[2,2,256,128]{3,2,1,0:T(8,128)(2,1)S(1)}, bf16[2,2,256,128]{3,2,1,0:T(8,128)(2,1)S(1)}, u32[]{:S(2)}, u32[]{:S(2)}) collective-permute-start(bf16[2,2,256,128]{3,2,1,0:T(8,128)(2,1)S(1)} %pad_maximum_fusion), channel_id=1, source_target_pairs={{0,4},{1,5},{2,6},{3,7},{4,0},{5,1},{6,2},{7,3},{8,12},{9,13},{10,... | collective-permute-start | bytes 786440 | tf_op jit(solution)/shard_map/ppermute | solution.py:106
  86.3 10.2 %collective-permute-start.17 = (bf16[2,2,256,128]{3,2,1,0:T(8,128)(2,1)S(1)}, bf16[2,2,256,128]{3,2,1,0:T(8,128)(2,1)S(1)}, u32[]{:S(2)}, u32[]{:S(2)}) collective-permute-start(bf16[2,2,256,128]{3,2,1,0:T(8,128)(2,1)S(1)} %collective-permute-done.15.g_ref), channel_id=1, source_target_pairs={{0,1},{1,0},{2,3},{3,2},{4,5},{5,4},{6,7},{7,6},{8,9},{9,8},{10,11... | collective-permute-start | bytes 786440 | tf_op jit(solution)/shard_map/ppermute | solution.py:106

commit v2 on v1

--- a/solution.py
+++ b/solution.py
@@ -203,17 +203,18 @@
     top0, bot0, kept = project(0, own, keys, values, proj_weight)
     before0 = lax.ppermute(bot1, "ctx", up)
     after0 = lax.ppermute(top1, "ctx", down)
-    before1 = lax.ppermute(bot0, "ctx", up)
-    after1 = lax.ppermute(top0, "ctx", down)
     part = merge([kept, swap(sent, b2)])
-    part, before0, after0 = lax.optimization_barrier((part, before0, after0))
-    pieces = []
-    for place in range(KV // 2):
-        for half in range(2):
-            piece = part[place : place + 1, :, half * HD : (half + 1) * HD]
-            bits = b0 * (place & 1) ^ b1 * (place >> 1) ^ HALF_BIT * half
-            pieces.append(swap(piece, bits) if bits else piece)
-    part = merge(pieces)
+    blocks = [(place, half) for place in range(KV // 2) for half in range(2)]
+    cut = lambda place, half: part[place : place + 1, :, half * HD : (half + 1) * HD]
+    pieces = {block: cut(*block) for block in blocks}
+    late = [block for block in blocks if block[1]]
+    target = lambda place, half: b0 * (place & 1) ^ b1 * (place >> 1) ^ HALF_BIT * half
+    first = [swap(pieces[block], target(*block)) for block in blocks[2::2]]
+    held = lax.optimization_barrier(([pieces[x] for x in late], first[0], before0, after0))
+    _, first[0], before0, after0 = held
+    second = [swap(x, target(*block)) for x, block in zip(held[0], late)]
+    arrived = [pieces[0, 0]] + first + second
+    part = merge(arrived)
     rest = 1
     while rest < peers:
         if rest not in HEAD_BITS + (HALF_BIT,):
@@ -222,19 +223,20 @@
     far = (part[:, : 2 * HD] / part[:, T_ROW : T_ROW + 1]).astype(jnp.bfloat16)[:, None]
     at0 = jnp.concatenate([far, swap(far, HALF_BIT)], axis=1)
     near0 = (before0, top0, bot0, after0)
+    at0, bot_sent, top_sent = lax.optimization_barrier((at0, bot0, top0))
     at1 = swap(at0, b0)
+    before1 = lax.ppermute(bot_sent, "ctx", up)
+    after1 = lax.ppermute(top_sent, "ctx", down)
     out = attend(0, own, queries, *near0, at0)
-    at1, out, before1, after1 = lax.optimization_barrier((at1, out, before1, after1))
-    near1 = (before1, top1, bot1, after1)
-    out = attend(1, own, queries, *near0, at1, out)
+    at1, out = lax.optimization_barrier((at1, out))
     at01 = jnp.concatenate([at0, at1], axis=0)
     at23 = swap(at01, b1)
-    at45 = swap(at01, b2)
-    out = attend(4, own, queries, *near1, at45, out)
-    at23, out = lax.optimization_barrier((at23, out))
-    at67 = swap(at23, b2)
+    out = attend(1, own, queries, *near0, at1, out)
+    at23, out, before1, after1 = lax.optimization_barrier((at23, out, before1, after1))
+    near1 = (before1, top1, bot1, after1)
+    at4567 = swap(jnp.concatenate([at01, at23], axis=0), b2)
     out = attend(2, own, queries, *near0, at23, out)
-    return attend(6, own, queries, *near1, at67, out)
+    return attend(4, own, queries, *near1, at4567, out)
 
 
 def solution(mesh):

time: 107 us -> 104 us (0.972)
  waiting for transfers between devices: 24.1 us -> 12.6 us
  starting transfers between devices: 26.5 us -> 37.7 us
  Pallas kernels: 52.2 us -> 50 us
    ppermute x14 -> x13, starting transfers between devices: 14.3 us -> 23.5 us  [swap(): return lax.ppermute(x, 'ctx', [(i, i ^ bits) for i in range(peers)])]
    ppermute x14 -> x13, waiting for transfers between devices: 19.9 us -> 11.2 us  [swap(): return lax.ppermute(x, 'ctx', [(i, i ^ bits) for i in range(peers)])]
    ppermute x1, waiting for transfers between devices: 4.17 us -> 1.37 us  [on_device(): after0 = lax.ppermute(top1, 'ctx', down)]
    pallas_call x5 -> x4, Pallas kernels: 41.8 us -> 39.6 us  [attend(): pl.pallas_call(attend_kernel, out_shape=jax.ShapeDtypeStruct(queries.shap...]
    ppermute x2, starting transfers between devices: 5.73 us -> 7.81 us  [the longest x1 5.71 us: on_device(): before1 = lax.ppermute(bot_sent, 'ctx', up)]
  transfers between devices with their start and end apart: 18 -> 17, of which waited for: 8 -> 5; matrix products, arithmetic and copies ran while one was open for 2% -> 2% of each run, Pallas kernels for 35% -> 26%
where the time goes in v2:
time: 104 us
  Pallas kernels  50 us (48%)
  starting transfers between devices  37.7 us (36%)
  waiting for transfers between devices  12.6 us (12%)
  other arithmetic  3.22 us (3%)
    pallas_call x4, Pallas kernels, attend(): pl.pallas_call(attend_kernel, out_shape=jax.ShapeDtypeStruct(queries.shap...  39.6 us
    ppermute x13, starting transfers between devices, swap(): return lax.ppermute(x, 'ctx', [(i, i ^ bits) for i in range(peers)])  23.5 us
    ppermute x13, waiting for transfers between devices, swap(): return lax.ppermute(x, 'ctx', [(i, i ^ bits) for i in range(peers)])  11.2 us
    pallas_call x2, Pallas kernels, project(): pl.pallas_call(project_kernel, out_shape=(jax.ShapeDtypeStruct((HALF, cou...  10.4 us
    ppermute x1, starting transfers between devices, on_device(): before1 = lax.ppermute(bot_sent, 'ctx', up)  5.71 us
    ppermute x1, starting transfers between devices, on_device(): before0 = lax.ppermute(bot1, 'ctx', up)  4.45 us
    ppermute x1, starting transfers between devices, on_device(): after1 = lax.ppermute(top_sent, 'ctx', down)  2.1 us
  transfers between devices with their start and end apart: 17, of which 5 were waited for; matrix products, arithmetic and copies ran while one was open for 2% of the time, Pallas kernels for 26%

profile of v2, /device:TPU:1, one launch (start us, length us, event | category | flops | bytes accessed | tf_op | source)
XLA Modules:
  0.0 103.8 jit_solution(14864862873675874142)
XLA Ops:
  0.0 0.6 pad_add_fusion.own
  0.6 5.2 %project.3 = (bf16[256,1024]{1,0:T(8,128)(2,1)}, bf16[256,1024]{1,0:T(8,128)(2,1)}, f32[4,264,256]{2,1,0:T(8,128)}) custom-call(s32[4]{0:T(128)} %pad_add_fusion.own, bf16[512,1024]{1,0:T(8,128)(2,1)} %k_ref.3, bf16[512,1024]{1,0:T(8,128)(2,1)} %v_ref.3, bf16[8,128,256]{2,1,0:T(8,128)(2,1)} %w1_ref.3, bf16[8,128,256]{2,1,0:T(8,128)(2,1)} %w1_ref.3), custom_call_target="tpu_custom_call" | custom-call | flops 671088640 | bytes 4194304 | tf_op jit(solution)/shard_map/project/pallas_call | solution.py:70
  5.8 0.1 collective-permute-start
  5.9 4.4 %collective-permute-start.2 = (bf16[256,1024]{1,0:T(8,128)(2,1)}, bf16[256,1024]{1,0:T(8,128)(2,1)S(1)}, u32[]{:S(2)}, u32[]{:S(2)}) collective-permute-start(bf16[256,1024]{1,0:T(8,128)(2,1)} %get-tuple-element.29.bot_ref), channel_id=1, source_target_pairs={{0,1},{1,2},{2,3},{3,4},{4,5},{5,6},{6,7},{7,8},{8,9},{9,10},{10,1... | collective-permute-start | bytes 1572872 | tf_op jit(solution)/shard_map/ppermute | solution.py:204
  10.3 1.9 %collective-permute-start.3 = (bf16[256,1024]{1,0:T(8,128)(2,1)}, bf16[256,1024]{1,0:T(8,128)(2,1)S(1)}, u32[]{:S(2)}, u32[]{:S(2)}) collective-permute-start(bf16[256,1024]{1,0:T(8,128)(2,1)} %get-tuple-element.30.top_ref), channel_id=1, source_target_pairs={{1,0},{2,1},{3,2},{4,3},{5,4},{6,5},{7,6},{8,7},{9,8},{10,9},{11,1... | collective-permute-start | bytes 1572872 | tf_op jit(solution)/shard_map/ppermute | solution.py:205
  12.3 5.2 %project.2 = (bf16[256,1024]{1,0:T(8,128)(2,1)}, bf16[256,1024]{1,0:T(8,128)(2,1)}, f32[4,264,256]{2,1,0:T(8,128)}) custom-call(s32[4]{0:T(128)} %pad_add_fusion.own, bf16[512,1024]{1,0:T(8,128)(2,1)} %k_ref.3, bf16[512,1024]{1,0:T(8,128)(2,1)} %v_ref.3, bf16[8,128,256]{2,1,0:T(8,128)(2,1)} %w1_ref.3, bf16[8,128,256]{2,1,0:T(8,128)(2,1)} %w1_ref.3), custom_call_target="tpu_custom_call" | custom-call | flops 671088640 | bytes 4194304 | tf_op jit(solution)/shard_map/project/pallas_call | solution.py:70
  17.4 0.0 collective-permute-done
  17.4 0.8 subtract_exponential_fusion.1
  18.3 1.4 %add_select_fusion = f32[4,264,256]{2,1,0:T(8,128)S(1)} fusion(f32[4,264,256]{2,1,0:T(8,128)S(1)} %collective-permute-done, f32[4,264,256]{2,1,0:T(8,128)} %get-tuple-element.27, f32[4,256]{1,0:T(4,128)S(1)} %bitcast.38, f32[4,256]{1,0:T(4,128)S(1)} %get-tuple-element.70, f32[4,256]{1,0:T(4,128)S(1)} %get-tuple-element.71, pred[264]{0:T(512)(128)(4,1)S(1)} %iota_compare_fusion), kind=kLoop, calls=%fused_computation | loop fusion | flops 1081344 | bytes 3256584 | tf_op jit(solution)/shard_map/jit(_where)/select_n | solution.py:101
  19.7 0.1 fusion.11
  19.8 0.0 copy-start.1
  19.8 0.0 copy-start
  19.8 0.0 copy-start.2
  19.8 1.4 %collective-permute-start.1 = (f32[1,264,128]{2,1,0:T(8,128)S(1)}, f32[1,264,128]{2,1,0:T(8,128)S(1)}, u32[]{:S(2)}, u32[]{:S(2)}) collective-permute-start(f32[1,264,128]{2,1,0:T(8,128)S(1)} %get-tuple-element.55), channel_id=1, source_target_pairs={{0,8},{1,9},{2,10},{3,11},{4,12},{5,13},{6,14},{7,15},{8,0},{9,1},... | collective-permute-start | bytes 405512 | tf_op jit(solution)/shard_map/ppermute | solution.py:106
  21.2 1.2 %collective-permute-start.4 = (f32[1,264,128]{2,1,0:T(8,128)S(1)}, f32[1,264,128]{2,1,0:T(8,128)S(1)}, u32[]{:S(2)}, u32[]{:S(2)}) collective-permute-start(f32[1,264,128]{2,1,0:T(8,128)S(1)} %get-tuple-element.53), channel_id=1, source_target_pairs={{0,4},{1,5},{2,6},{3,7},{4,0},{5,1},{6,2},{7,3},{8,12},{9,13},{10,... | collective-permute-start | bytes 405512 | tf_op jit(solution)/shard_map/ppermute | solution.py:106
  22.4 0.1 collective-permute-start.5
  22.5 0.0 collective-permute-done.2.b_ref
  22.5 1.4 %collective-permute-done.3.a_ref = bf16[256,1024]{1,0:T(8,128)(2,1)S(1)} collective-permute-done((bf16[256,1024]{1,0:T(8,128)(2,1)}, bf16[256,1024]{1,0:T(8,128)(2,1)S(1)}, u32[]{:S(2)}, u32[]{:S(2)}) %collective-permute-start.3) | collective-permute-done | bytes 524320 | tf_op jit(solution)/shard_map/ppermute | solution.py:205
  23.9 0.5 collective-permute-done.1
  24.4 1.1 %collective-permute-start.6 = (f32[1,264,128]{2,1,0:T(8,128)S(1)}, f32[1,264,128]{2,1,0:T(8,128)S(1)}, u32[]{:S(2)}, u32[]{:S(2)}) collective-permute-start(f32[1,264,128]{2,1,0:T(8,128)S(1)} %get-tuple-element.32), channel_id=1, source_target_pairs={{0,2},{1,3},{2,0},{3,1},{4,6},{5,7},{6,4},{7,5},{8,10},{9,11},{10,... | collective-permute-start | bytes 405512 | tf_op jit(solution)/shard_map/ppermute | solution.py:106
  25.5 1.0 collective-permute-start.7
  26.5 2.5 %collective-permute-start.8 = (f32[1,264,128]{2,1,0:T(8,128)S(1)}, f32[1,264,128]{2,1,0:T(8,128)S(1)}, u32[]{:S(2)}, u32[]{:S(2)}) collective-permute-start(f32[1,264,128]{2,1,0:T(8,128)S(1)} %get-tuple-element.34), channel_id=1, source_target_pairs={{0,6},{1,7},{2,4},{3,5},{4,2},{5,3},{6,0},{7,1},{8,14},{9,15},{10,... | collective-permute-start | bytes 405512 | tf_op jit(solution)/shard_map/ppermute | solution.py:106
  29.0 0.0 collective-permute-done.4
  29.1 1.9 %collective-permute-start.9 = (f32[1,264,128]{2,1,0:T(8,128)S(1)}, f32[1,264,128]{2,1,0:T(8,128)S(1)}, u32[]{:S(2)}, u32[]{:S(2)}) collective-permute-start(f32[1,264,128]{2,1,0:T(8,128)S(1)} %get-tuple-element.35), channel_id=1, source_target_pairs={{0,14},{1,15},{2,12},{3,13},{4,10},{5,11},{6,8},{7,9},{8,6},{9,7},... | collective-permute-start | bytes 405512 | tf_op jit(solution)/shard_map/ppermute | solution.py:106
  30.9 0.0 collective-permute-done.5
  30.9 0.0 collective-permute-done.6
  30.9 0.0 collective-permute-done.7
  31.0 6.1 %collective-permute-done.8 = f32[1,264,128]{2,1,0:T(8,128)S(1)} collective-permute-done((f32[1,264,128]{2,1,0:T(8,128)S(1)}, f32[1,264,128]{2,1,0:T(8,128)S(1)}, u32[]{:S(2)}, u32[]{:S(2)}) %collective-permute-start.8) | collective-permute-done | bytes 135200 | tf_op jit(solution)/shard_map/ppermute | solution.py:106
  37.1 0.0 collective-permute-done.9
  37.1 0.1 fusion.7
  37.3 2.5 %collective-permute-start.10 = (f32[1,264,128]{2,1,0:T(8,128)S(1)}, f32[1,264,128]{2,1,0:T(8,128)S(1)}, u32[]{:S(2)}, u32[]{:S(2)}) collective-permute-start(f32[1,264,128]{2,1,0:T(8,128)S(1)} %fusion.7), channel_id=1, source_target_pairs={{0,16},{1,17},{2,18},{3,19},{4,20},{5,21},{6,22},{7,23},{8,24},{9,... | collective-permute-start | bytes 405512 | tf_op jit(solution)/shard_map/ppermute | solution.py:106
  39.7 2.9 %collective-permute-done.10 = f32[1,264,128]{2,1,0:T(8,128)S(1)} collective-permute-done((f32[1,264,128]{2,1,0:T(8,128)S(1)}, f32[1,264,128]{2,1,0:T(8,128)S(1)}, u32[]{:S(2)}, u32[]{:S(2)}) %collective-permute-start.10) | collective-permute-done | bytes 135200 | tf_op jit(solution)/shard_map/ppermute | solution.py:106
  42.7 0.1 add_select_fusion.1
  42.8 5.8 %collective-permute-start.11 = (bf16[1,1,256,128]{3,2,1,0:T(8,128)(2,1)S(1)}, bf16[1,1,256,128]{3,2,1,0:T(8,128)(2,1)S(1)}, u32[]{:S(2)}, u32[]{:S(2)}) collective-permute-start(bf16[1,1,256,128]{3,2,1,0:T(8,128)(2,1)S(1)} %fusion.9), channel_id=1, source_target_pairs={{0,2},{1,3},{2,0},{3,1},{4,6},{5,7},{6,4},{7,5},{8,10},{9,11},{10,... | collective-permute-start | bytes 196616 | tf_op jit(solution)/shard_map/ppermute | solution.py:106
  48.6 1.7 %collective-permute-done.11 = bf16[1,1,256,128]{3,2,1,0:T(8,128)(2,1)S(1)} collective-permute-done((bf16[1,1,256,128]{3,2,1,0:T(8,128)(2,1)S(1)}, bf16[1,1,256,128]{3,2,1,0:T(8,128)(2,1)S(1)}, u32[]{:S(2)}, u32[]{:S(2)}) %collective-permute-start.11) | collective-permute-done | bytes 65568 | tf_op jit(solution)/shard_map/ppermute | solution.py:106
  50.2 0.0 copy-done.1
  50.3 5.7 %collective-permute-start.14 = (bf16[256,1024]{1,0:T(8,128)(2,1)S(1)}, bf16[256,1024]{1,0:T(8,128)(2,1)S(1)}, u32[]{:S(2)}, u32[]{:S(2)}) collective-permute-start(bf16[256,1024]{1,0:T(8,128)(2,1)S(1)} %copy-done.1), channel_id=1, source_target_pairs={{0,1},{1,2},{2,3},{3,4},{4,5},{5,6},{6,7},{7,8},{8,9},{9,10},{10,1... | collective-permute-start | bytes 1572872 | tf_op jit(solution)/shard_map/ppermute | solution.py:228
  56.0 0.0 copy-done
  56.0 2.1 %collective-permute-start.15 = (bf16[256,1024]{1,0:T(8,128)(2,1)S(1)}, bf16[256,1024]{1,0:T(8,128)(2,1)S(1)}, u32[]{:S(2)}, u32[]{:S(2)}) collective-permute-start(bf16[256,1024]{1,0:T(8,128)(2,1)S(1)} %copy-done), channel_id=1, source_target_pairs={{1,0},{2,1},{3,2},{4,3},{5,4},{6,5},{7,6},{8,7},{9,8},{10,9},{11,1... | collective-permute-start | bytes 1572872 | tf_op jit(solution)/shard_map/ppermute | solution.py:229
  58.1 0.1 collective-permute-start.12
  58.2 0.0 copy-done.2
  58.2 6.1 %attend.4.refs_0_ = bf16[512,4096]{1,0:T(8,128)(2,1)} custom-call(s32[4]{0:T(128)S(1)} %copy-done.2, bf16[512,4096]{1,0:T(8,128)(2,1)} %q_ref.7, bf16[256,1024]{1,0:T(8,128)(2,1)S(1)} %collective-permute-done.2.b_ref, bf16[256,1024]{1,0:T(8,128)(2,1)S(1)} %copy-done, bf16[256,1024]{1,0:T(8,128)(2,1)S(1)} %copy-done.1, ...), custom_call_target="tpu_custom_call" | custom-call | flops 1342177280 | bytes 2097152 | tf_op jit(solution)/shard_map/attend/pallas_call | solution.py:159
  64.3 0.0 collective-permute-done.12.g_ref
  64.3 0.1 collective-permute-start.13
  64.4 6.1 %attend.5.refs_0_ = bf16[512,4096]{1,0:T(8,128)(2,1)} custom-call(s32[4]{0:T(128)S(1)} %copy-done.2, bf16[512,4096]{1,0:T(8,128)(2,1)} %q_ref.7, bf16[256,1024]{1,0:T(8,128)(2,1)S(1)} %collective-permute-done.2.b_ref, bf16[256,1024]{1,0:T(8,128)(2,1)S(1)} %copy-done, bf16[256,1024]{1,0:T(8,128)(2,1)S(1)} %copy-done.1, ...), custom_call_target="tpu_custom_call", output_to_operand_aliasing={{}: (7, {})} | custom-call | flops 1342177280 | bytes 2097152 | tf_op jit(solution)/shard_map/attend/pallas_call | solution.py:159
  70.4 0.0 collective-permute-done.13.g_ref
  70.4 0.0 collective-permute-done.14.b_ref
  70.4 0.0 collective-permute-done.15.a_ref
  70.5 0.1 pad_maximum_fusion
  70.5 0.0 copy-start.3
  70.5 0.0 copy-start.4
  70.5 5.8 %collective-permute-start.16 = (bf16[4,2,256,128]{3,2,1,0:T(8,128)(2,1)S(1)}, bf16[4,2,256,128]{3,2,1,0:T(8,128)(2,1)S(1)}, u32[]{:S(2)}, u32[]{:S(2)}) collective-permute-start(bf16[4,2,256,128]{3,2,1,0:T(8,128)(2,1)S(1)} %pad_maximum_fusion), channel_id=1, source_target_pairs={{0,1},{1,0},{2,3},{3,2},{4,5},{5,4},{6,7},{7,6},{8,9},{9,8},{10,11... | collective-permute-start | bytes 1572872 | tf_op jit(solution)/shard_map/ppermute | solution.py:106
  76.4 10.0 %attend.6.refs_0_ = bf16[512,4096]{1,0:T(8,128)(2,1)} custom-call(s32[4]{0:T(128)S(1)} %copy-done.2, bf16[512,4096]{1,0:T(8,128)(2,1)} %q_ref.7, bf16[256,1024]{1,0:T(8,128)(2,1)S(1)} %collective-permute-done.2.b_ref, bf16[256,1024]{1,0:T(8,128)(2,1)S(1)} %copy-done, bf16[256,1024]{1,0:T(8,128)(2,1)S(1)} %copy-done.1, ...), custom_call_target="tpu_custom_call", output_to_operand_aliasing={{}: (7, {})} | custom-call | flops 2684354560 | bytes 4194304 | tf_op jit(solution)/shard_map/attend/pallas_call | solution.py:159
  86.4 0.0 collective-permute-done.16.g_ref
  86.4 0.0 copy-done.3
  86.4 0.0 copy-done.4
  86.4 17.5 %attend.7 = bf16[512,4096]{1,0:T(8,128)(2,1)} custom-call(s32[4]{0:T(128)S(1)} %copy-done.2, bf16[512,4096]{1,0:T(8,128)(2,1)} %q_ref.7, bf16[256,1024]{1,0:T(8,128)(2,1)S(1)} %collective-permute-done.14.b_ref, bf16[256,1024]{1,0:T(8,128)(2,1)S(1)} %copy-done.3, bf16[256,1024]{1,0:T(8,128)(2,1)S(1)} %copy-done.4, ...), custom_call_target="tpu_custom_call", output_to_operand_aliasing={{}: (7, {})} | custom-call | flops 5368709120 | bytes 8388608 | tf_op jit(solution)/shard_map/attend/pallas_call | solution.py:159
  (11 shorter events, 0.1 us)
Async XLA Ops:
  5.8 11.6 %collective-permute-start = (f32[4,264,256]{2,1,0:T(8,128)}, f32[4,264,256]{2,1,0:T(8,128)S(1)}, u32[]{:S(2)}, u32[]{:S(2)}) collective-permute-start(f32[4,264,256]{2,1,0:T(8,128)} %get-tuple-element.28), channel_id=1, source_target_pairs={{0,1},{1,0},{2,3},{3,2},{4,5},{5,4},{6,7},{7,6},{8,9},{9,8},{10,11... | collective-permute-start | bytes 3244040 | tf_op jit(solution)/shard_map/ppermute | solution.py:106
  5.9 16.6 %collective-permute-start.2 = (bf16[256,1024]{1,0:T(8,128)(2,1)}, bf16[256,1024]{1,0:T(8,128)(2,1)S(1)}, u32[]{:S(2)}, u32[]{:S(2)}) collective-permute-start(bf16[256,1024]{1,0:T(8,128)(2,1)} %get-tuple-element.29.bot_ref), channel_id=1, source_target_pairs={{0,1},{1,2},{2,3},{3,4},{4,5},{5,6},{6,7},{7,8},{8,9},{9,10},{10,1... | collective-permute-start | bytes 1572872 | tf_op jit(solution)/shard_map/ppermute | solution.py:204
  10.3 13.6 %collective-permute-start.3 = (bf16[256,1024]{1,0:T(8,128)(2,1)}, bf16[256,1024]{1,0:T(8,128)(2,1)S(1)}, u32[]{:S(2)}, u32[]{:S(2)}) collective-permute-start(bf16[256,1024]{1,0:T(8,128)(2,1)} %get-tuple-element.30.top_ref), channel_id=1, source_target_pairs={{1,0},{2,1},{3,2},{4,3},{5,4},{6,5},{7,6},{8,7},{9,8},{10,9},{11,1... | collective-permute-start | bytes 1572872 | tf_op jit(solution)/shard_map/ppermute | solution.py:205
  19.8 30.5 %copy-start.1 = (bf16[256,1024]{1,0:T(8,128)(2,1)S(1)}, bf16[256,1024]{1,0:T(8,128)(2,1)}, u32[]{:S(2)}) copy-start(bf16[256,1024]{1,0:T(8,128)(2,1)} %get-tuple-element.43.bot_ref) | copy-start | bytes 1572868
  19.8 36.2 %copy-start = (bf16[256,1024]{1,0:T(8,128)(2,1)S(1)}, bf16[256,1024]{1,0:T(8,128)(2,1)}, u32[]{:S(2)}) copy-start(bf16[256,1024]{1,0:T(8,128)(2,1)} %get-tuple-element.44.top_ref) | copy-start | bytes 1572868
  19.8 38.4 %copy-start.2 = (s32[4]{0:T(128)S(1)}, s32[4]{0:T(128)}, u32[]{:S(2)}) copy-start(s32[4]{0:T(128)} %pad_add_fusion.own) | copy-start | bytes 52
  19.8 4.6 %collective-permute-start.1 = (f32[1,264,128]{2,1,0:T(8,128)S(1)}, f32[1,264,128]{2,1,0:T(8,128)S(1)}, u32[]{:S(2)}, u32[]{:S(2)}) collective-permute-start(f32[1,264,128]{2,1,0:T(8,128)S(1)} %get-tuple-element.55), channel_id=1, source_target_pairs={{0,8},{1,9},{2,10},{3,11},{4,12},{5,13},{6,14},{7,15},{8,0},{9,1},... | collective-permute-start | bytes 405512 | tf_op jit(solution)/shard_map/ppermute | solution.py:106
  21.2 7.9 %collective-permute-start.4 = (f32[1,264,128]{2,1,0:T(8,128)S(1)}, f32[1,264,128]{2,1,0:T(8,128)S(1)}, u32[]{:S(2)}, u32[]{:S(2)}) collective-permute-start(f32[1,264,128]{2,1,0:T(8,128)S(1)} %get-tuple-element.53), channel_id=1, source_target_pairs={{0,4},{1,5},{2,6},{3,7},{4,0},{5,1},{6,2},{7,3},{8,12},{9,13},{10,... | collective-permute-start | bytes 405512 | tf_op jit(solution)/shard_map/ppermute | solution.py:106
  22.4 8.6 %collective-permute-start.5 = (f32[1,264,128]{2,1,0:T(8,128)S(1)}, f32[1,264,128]{2,1,0:T(8,128)S(1)}, u32[]{:S(2)}, u32[]{:S(2)}) collective-permute-start(f32[1,264,128]{2,1,0:T(8,128)S(1)} %get-tuple-element.54), channel_id=1, source_target_pairs={{0,12},{1,13},{2,14},{3,15},{4,8},{5,9},{6,10},{7,11},{8,4},{9,5},... | collective-permute-start | bytes 405512 | tf_op jit(solution)/shard_map/ppermute | solution.py:106
  24.4 6.6 %collective-permute-start.6 = (f32[1,264,128]{2,1,0:T(8,128)S(1)}, f32[1,264,128]{2,1,0:T(8,128)S(1)}, u32[]{:S(2)}, u32[]{:S(2)}) collective-permute-start(f32[1,264,128]{2,1,0:T(8,128)S(1)} %get-tuple-element.32), channel_id=1, source_target_pairs={{0,2},{1,3},{2,0},{3,1},{4,6},{5,7},{6,4},{7,5},{8,10},{9,11},{10,... | collective-permute-start | bytes 405512 | tf_op jit(solution)/shard_map/ppermute | solution.py:106
  25.5 5.4 %collective-permute-start.7 = (f32[1,264,128]{2,1,0:T(8,128)S(1)}, f32[1,264,128]{2,1,0:T(8,128)S(1)}, u32[]{:S(2)}, u32[]{:S(2)}) collective-permute-start(f32[1,264,128]{2,1,0:T(8,128)S(1)} %get-tuple-element.33), channel_id=1, source_target_pairs={{0,10},{1,11},{2,8},{3,9},{4,14},{5,15},{6,12},{7,13},{8,2},{9,3},... | collective-permute-start | bytes 405512 | tf_op jit(solution)/shard_map/ppermute | solution.py:106
  26.5 10.6 %collective-permute-start.8 = (f32[1,264,128]{2,1,0:T(8,128)S(1)}, f32[1,264,128]{2,1,0:T(8,128)S(1)}, u32[]{:S(2)}, u32[]{:S(2)}) collective-permute-start(f32[1,264,128]{2,1,0:T(8,128)S(1)} %get-tuple-element.34), channel_id=1, source_target_pairs={{0,6},{1,7},{2,4},{3,5},{4,2},{5,3},{6,0},{7,1},{8,14},{9,15},{10,... | collective-permute-start | bytes 405512 | tf_op jit(solution)/shard_map/ppermute | solution.py:106
  29.1 8.0 %collective-permute-start.9 = (f32[1,264,128]{2,1,0:T(8,128)S(1)}, f32[1,264,128]{2,1,0:T(8,128)S(1)}, u32[]{:S(2)}, u32[]{:S(2)}) collective-permute-start(f32[1,264,128]{2,1,0:T(8,128)S(1)} %get-tuple-element.35), channel_id=1, source_target_pairs={{0,14},{1,15},{2,12},{3,13},{4,10},{5,11},{6,8},{7,9},{8,6},{9,7},... | collective-permute-start | bytes 405512 | tf_op jit(solution)/shard_map/ppermute | solution.py:106
  37.3 5.4 %collective-permute-start.10 = (f32[1,264,128]{2,1,0:T(8,128)S(1)}, f32[1,264,128]{2,1,0:T(8,128)S(1)}, u32[]{:S(2)}, u32[]{:S(2)}) collective-permute-start(f32[1,264,128]{2,1,0:T(8,128)S(1)} %fusion.7), channel_id=1, source_target_pairs={{0,16},{1,17},{2,18},{3,19},{4,20},{5,21},{6,22},{7,23},{8,24},{9,... | collective-permute-start | bytes 405512 | tf_op jit(solution)/shard_map/ppermute | solution.py:106
  42.8 7.4 %collective-permute-start.11 = (bf16[1,1,256,128]{3,2,1,0:T(8,128)(2,1)S(1)}, bf16[1,1,256,128]{3,2,1,0:T(8,128)(2,1)S(1)}, u32[]{:S(2)}, u32[]{:S(2)}) collective-permute-start(bf16[1,1,256,128]{3,2,1,0:T(8,128)(2,1)S(1)} %fusion.9), channel_id=1, source_target_pairs={{0,2},{1,3},{2,0},{3,1},{4,6},{5,7},{6,4},{7,5},{8,10},{9,11},{10,... | collective-permute-start | bytes 196616 | tf_op jit(solution)/shard_map/ppermute | solution.py:106
  50.3 20.2 %collective-permute-start.14 = (bf16[256,1024]{1,0:T(8,128)(2,1)S(1)}, bf16[256,1024]{1,0:T(8,128)(2,1)S(1)}, u32[]{:S(2)}, u32[]{:S(2)}) collective-permute-start(bf16[256,1024]{1,0:T(8,128)(2,1)S(1)} %copy-done.1), channel_id=1, source_target_pairs={{0,1},{1,2},{2,3},{3,4},{4,5},{5,6},{6,7},{7,8},{8,9},{9,10},{10,1... | collective-permute-start | bytes 1572872 | tf_op jit(solution)/shard_map/ppermute | solution.py:228
  56.0 14.5 %collective-permute-start.15 = (bf16[256,1024]{1,0:T(8,128)(2,1)S(1)}, bf16[256,1024]{1,0:T(8,128)(2,1)S(1)}, u32[]{:S(2)}, u32[]{:S(2)}) collective-permute-start(bf16[256,1024]{1,0:T(8,128)(2,1)S(1)} %copy-done), channel_id=1, source_target_pairs={{1,0},{2,1},{3,2},{4,3},{5,4},{6,5},{7,6},{8,7},{9,8},{10,9},{11,1... | collective-permute-start | bytes 1572872 | tf_op jit(solution)/shard_map/ppermute | solution.py:229
  58.1 6.2 %collective-permute-start.12 = (bf16[1,2,256,128]{3,2,1,0:T(8,128)(2,1)S(1)}, bf16[1,2,256,128]{3,2,1,0:T(8,128)(2,1)S(1)}, u32[]{:S(2)}, u32[]{:S(2)}) collective-permute-start(bf16[1,2,256,128]{3,2,1,0:T(8,128)(2,1)S(1)} %pad_maximum_fusion.2.g_ref), channel_id=1, source_target_pairs={{0,8},{1,9},{2,10},{3,11},{4,12},{5,13},{6,14},{7,15},{8,0},{9,1},... | collective-permute-start | bytes 393224 | tf_op jit(solution)/shard_map/ppermute | solution.py:106
  64.3 6.2 %collective-permute-start.13 = (bf16[2,2,256,128]{3,2,1,0:T(8,128)(2,1)S(1)}, bf16[2,2,256,128]{3,2,1,0:T(8,128)(2,1)S(1)}, u32[]{:S(2)}, u32[]{:S(2)}) collective-permute-start(bf16[2,2,256,128]{3,2,1,0:T(8,128)(2,1)S(1)} %pad_maximum_fusion.1), channel_id=1, source_target_pairs={{0,4},{1,5},{2,6},{3,7},{4,0},{5,1},{6,2},{7,3},{8,12},{9,13},{10,... | collective-permute-start | bytes 786440 | tf_op jit(solution)/shard_map/ppermute | solution.py:106
  70.5 15.9 %copy-start.3 = (bf16[256,1024]{1,0:T(8,128)(2,1)S(1)}, bf16[256,1024]{1,0:T(8,128)(2,1)}, u32[]{:S(2)}) copy-start(bf16[256,1024]{1,0:T(8,128)(2,1)} %get-tuple-element.30.top_ref) | copy-start | bytes 1572868
  70.5 15.8 %copy-start.4 = (bf16[256,1024]{1,0:T(8,128)(2,1)S(1)}, bf16[256,1024]{1,0:T(8,128)(2,1)}, u32[]{:S(2)}) copy-start(bf16[256,1024]{1,0:T(8,128)(2,1)} %get-tuple-element.29.bot_ref) | copy-start | bytes 1572868
  70.5 15.8 %collective-permute-start.16 = (bf16[4,2,256,128]{3,2,1,0:T(8,128)(2,1)S(1)}, bf16[4,2,256,128]{3,2,1,0:T(8,128)(2,1)S(1)}, u32[]{:S(2)}, u32[]{:S(2)}) collective-permute-start(bf16[4,2,256,128]{3,2,1,0:T(8,128)(2,1)S(1)} %pad_maximum_fusion), channel_id=1, source_target_pairs={{0,1},{1,0},{2,3},{3,2},{4,5},{5,4},{6,7},{7,6},{8,9},{9,8},{10,11... | collective-permute-start | bytes 1572872 | tf_op jit(solution)/shard_map/ppermute | solution.py:106

commit v3 on v2

--- a/solution.py
+++ b/solution.py
@@ -24,8 +24,9 @@
 PROJECT_VMEM = 60 << 20
 ATTEND_VMEM = 48 << 20
 
-HEAD_BITS = (8, 4, 1)
-HALF_BIT = 2
+HEAD_BITS = (4, 2, 1)
+HALF_BIT = 8
+CORE_BIT = 1
 
 
 def normalize(x):
@@ -34,7 +35,7 @@
     return centered * lax.rsqrt(spread + 1e-05)
 
 
-def project_kernel(own, k_ref, v_ref, w0_ref, w1_ref, top_ref, bot_ref, part_ref):
+def project_kernel(own, k_ref, v_ref, w0_ref, w1_ref, in_ref, out_ref, part_ref):
     for i in range(2):
         side = (i ^ own[0]) & 1
         lane = pl.multiple_of(side * HD, HD)
@@ -44,8 +45,9 @@
         near_v = normalize(values.astype(jnp.float32)).astype(jnp.bfloat16)
         near = jnp.concatenate([near_k, near_v], axis=1)
         wide = pl.multiple_of(side * 2 * HD, 2 * HD)
-        top_ref[:, pl.ds(wide, 2 * HD)] = near[:HALF]
-        bot_ref[:, pl.ds(wide, 2 * HD)] = near[HALF:]
+        odd = own[2] > 0
+        in_ref[:, pl.ds(wide, 2 * HD)] = jnp.where(odd, near[:HALF], near[HALF:])
+        out_ref[:, pl.ds(wide, 2 * HD)] = jnp.where(odd, near[HALF:], near[:HALF])
         weight = jnp.concatenate([w0_ref[side], w1_ref[side]], axis=1)
         logits = jnp.dot(near_k, weight, preferred_element_type=jnp.float32)
         top = jnp.max(logits, axis=0, keepdims=True)
@@ -106,16 +108,10 @@
     return lax.ppermute(x, "ctx", [(i, i ^ bits) for i in range(peers)])
 
 
-def attend_kernel(own, q_ref, b_ref, top_ref, bot_ref, a_ref, g_ref, *refs):
+def attend_kernel(own, q_ref, a_ref, b_ref, in_ref, out_ref, g_ref, *refs):
     o_ref, k_ref, v_ref = refs[-3:]
-    hide = (
-        jnp.where(own[2] > 0, 0.0, FAR_AWAY),
-        0.0,
-        0.0,
-        jnp.where(own[3] > 0, 0.0, FAR_AWAY),
-        0.0,
-    )
-    for i, x in enumerate((b_ref, top_ref, bot_ref, a_ref)):
+    hide = (0.0, 0.0, 0.0, jnp.where(own[3] > 0, 0.0, FAR_AWAY), 0.0)
+    for i, x in enumerate((a_ref, b_ref, in_ref, out_ref)):
         k_ref[i * HALF : (i + 1) * HALF] = x[:, :HD]
         v_ref[:, i * HALF : (i + 1) * HALF] = x[:, HD:].T
     for i in range(2):
@@ -150,11 +146,12 @@
         scores = ahead
 
 
-def attend(base, own, queries, before, top, bot, after, far, out=None):
+def attend(base, own, queries, nears, far, out=None):
     tok = queries.shape[0]
     count = far.shape[0]
     head = lambda i, own: base + i ^ own[0]
-    near = pl.BlockSpec((HALF, 2 * HD), lambda i, own: (0, head(i, own) % (KV // 2)))
+    place = lambda i, own: head(i, own) % (KV // 2)
+    edge = pl.BlockSpec((HALF, 2 * HD), lambda i, own: (0, place(i, own)))
     extra = [] if out is None else [out]
     return pl.pallas_call(
         attend_kernel,
@@ -164,10 +161,10 @@
             grid=(count,),
             in_specs=[
                 pl.BlockSpec((tok, GROUP * HD), lambda i, own: (0, head(i, own))),
-                near,
-                near,
-                near,
-                near,
+                edge,
+                edge,
+                edge,
+                edge,
                 pl.BlockSpec((1, 2, 2 * HD, R // 2), lambda i, own: (i, 0, 0, 0)),
             ]
             + [pl.BlockSpec(memory_space=pl.ANY)] * len(extra),
@@ -185,7 +182,7 @@
             transcendentals=count * GROUP * tok * 1280,
         ),
         name="attend",
-    )(own, queries, before, top, bot, after, far, *extra)
+    )(own, queries, *nears, far, *extra)
 
 
 def on_device(queries, keys, values, proj_weight):
@@ -193,28 +190,26 @@
     me = lax.axis_index("ctx")
     bit = lambda b: (me & b) // b
     own_head = sum(bit(b) << s for s, b in enumerate(HEAD_BITS))
-    own = jnp.stack(
-        [own_head, bit(HALF_BIT), (me > 0).astype(jnp.int32), (me < peers - 1).astype(jnp.int32)]
-    ).astype(jnp.int32)
+    edge = (me == 0) | (me == peers - 1)
+    own = jnp.stack([own_head, bit(HALF_BIT), bit(CORE_BIT), 1 - edge]).astype(jnp.int32)
     b0, b1, b2 = HEAD_BITS
-    up = [(i, i + 1) for i in range(peers - 1)]
-    down = [(i + 1, i) for i in range(peers - 1)]
-    top1, bot1, sent = project(KV // 2, own, keys, values, proj_weight)
-    top0, bot0, kept = project(0, own, keys, values, proj_weight)
-    before0 = lax.ppermute(bot1, "ctx", up)
-    after0 = lax.ppermute(top1, "ctx", down)
+    across = [(i, i + 1) for i in range(1, peers - 1, 2)]
+    across = across + [(j, i) for i, j in across]
+    in1, out1, sent = project(KV // 2, own, keys, values, proj_weight)
+    in0, out0, kept = project(0, own, keys, values, proj_weight)
+    outer0 = lax.ppermute(out1, "ctx", across)
+    inner0 = swap(in1, CORE_BIT)
+    outer1 = lax.ppermute(out0, "ctx", across)
+    inner1 = swap(in0, CORE_BIT)
     part = merge([kept, swap(sent, b2)])
     blocks = [(place, half) for place in range(KV // 2) for half in range(2)]
+    target = lambda place, half: b0 * (place & 1) ^ b1 * (place >> 1) ^ HALF_BIT * half
     cut = lambda place, half: part[place : place + 1, :, half * HD : (half + 1) * HD]
-    pieces = {block: cut(*block) for block in blocks}
-    late = [block for block in blocks if block[1]]
-    target = lambda place, half: b0 * (place & 1) ^ b1 * (place >> 1) ^ HALF_BIT * half
-    first = [swap(pieces[block], target(*block)) for block in blocks[2::2]]
-    held = lax.optimization_barrier(([pieces[x] for x in late], first[0], before0, after0))
-    _, first[0], before0, after0 = held
-    second = [swap(x, target(*block)) for x, block in zip(held[0], late)]
-    arrived = [pieces[0, 0]] + first + second
-    part = merge(arrived)
+    first = [swap(cut(*block), target(*block)) for block in blocks[1:4]]
+    late = [cut(*block) for block in blocks[4:]]
+    late, first[0], outer0 = lax.optimization_barrier((late, first[0], outer0))
+    second = [swap(x, target(*block)) for x, block in zip(late, blocks[4:])]
+    part = merge([cut(0, 0)] + first + second)
     rest = 1
     while rest < peers:
         if rest not in HEAD_BITS + (HALF_BIT,):
@@ -222,21 +217,18 @@
         rest *= 2
     far = (part[:, : 2 * HD] / part[:, T_ROW : T_ROW + 1]).astype(jnp.bfloat16)[:, None]
     at0 = jnp.concatenate([far, swap(far, HALF_BIT)], axis=1)
-    near0 = (before0, top0, bot0, after0)
-    at0, bot_sent, top_sent = lax.optimization_barrier((at0, bot0, top0))
     at1 = swap(at0, b0)
-    before1 = lax.ppermute(bot_sent, "ctx", up)
-    after1 = lax.ppermute(top_sent, "ctx", down)
-    out = attend(0, own, queries, *near0, at0)
-    at1, out = lax.optimization_barrier((at1, out))
+    nears0 = (in0, out0, inner0, outer0)
+    out = attend(0, own, queries, nears0, at0)
+    at1, out, outer1 = lax.optimization_barrier((at1, out, outer1))
     at01 = jnp.concatenate([at0, at1], axis=0)
     at23 = swap(at01, b1)
-    out = attend(1, own, queries, *near0, at1, out)
-    at23, out, before1, after1 = lax.optimization_barrier((at23, out, before1, after1))
-    near1 = (before1, top1, bot1, after1)
+    out = attend(1, own, queries, nears0, at1, out)
+    at23, out = lax.optimization_barrier((at23, out))
     at4567 = swap(jnp.concatenate([at01, at23], axis=0), b2)
-    out = attend(2, own, queries, *near0, at23, out)
-    return attend(4, own, queries, *near1, at4567, out)
+    nears1 = (in1, out1, inner1, outer1)
+    out = attend(2, own, queries, nears0, at23, out)
+    return attend(4, own, queries, nears1, at4567, out)
 
 
 def solution(mesh):

time: 104 us -> 97.1 us (0.934)
  starting transfers between devices: 37.7 us -> 27.7 us
  waiting for transfers between devices: 12.6 us -> 15.4 us
    ppermute x4 -> x2, starting transfers between devices: 14.2 us -> 7.28 us  [the longest x1 4.44 us: on_device(): outer0 = lax.ppermute(out1, 'ctx', across)]
    ppermute x13 -> x15, starting transfers between devices: 23.5 us -> 20.5 us  [swap(): return lax.ppermute(x, 'ctx', [(i, i ^ bits) for i in range(peers)])]
    ppermute x13 -> x15, waiting for transfers between devices: 11.2 us -> 12.8 us  [swap(): return lax.ppermute(x, 'ctx', [(i, i ^ bits) for i in range(peers)])]
    ppermute x4 -> x2, waiting for transfers between devices: 1.37 us -> 2.55 us  [the longest x1 1.76 us: on_device(): outer0 = lax.ppermute(out1, 'ctx', across)]
  transfers between devices with their start and end apart: 17 -> 17, of which waited for: 5 -> 6; matrix products, arithmetic and copies ran while one was open for 2% -> 3% of each run, Pallas kernels for 26% -> 28%
where the time goes in v3:
time: 97.1 us; the launch traced here: 96.4 us
  Pallas kernels  49.8 us (51%)
  starting transfers between devices  27.7 us (29%)
  waiting for transfers between devices  15.4 us (16%)
  other arithmetic  3.22 us (3%)
    pallas_call x4, Pallas kernels, attend(): pl.pallas_call(attend_kernel, out_shape=jax.ShapeDtypeStruct(queries.shap...  39.5 us
    ppermute x15, starting transfers between devices, swap(): return lax.ppermute(x, 'ctx', [(i, i ^ bits) for i in range(peers)])  20.5 us
    ppermute x15, waiting for transfers between devices, swap(): return lax.ppermute(x, 'ctx', [(i, i ^ bits) for i in range(peers)])  12.8 us
    pallas_call x2, Pallas kernels, project(): pl.pallas_call(project_kernel, out_shape=(jax.ShapeDtypeStruct((HALF, cou...  10.4 us
    ppermute x1, starting transfers between devices, on_device(): outer0 = lax.ppermute(out1, 'ctx', across)  4.44 us
    ppermute x1, starting transfers between devices, on_device(): outer1 = lax.ppermute(out0, 'ctx', across)  2.84 us
  transfers between devices with their start and end apart: 17, of which 6 were waited for; matrix products, arithmetic and copies ran while one was open for 3% of the time, Pallas kernels for 28%

profile of v3, /device:TPU:1, one launch (start us, length us, event | category | flops | bytes accessed | tf_op | source)
XLA Modules:
  0.0 96.4 jit_solution(7317261752800708716)
XLA Ops:
  0.0 0.6 pad_add_fusion.own
  0.6 5.2 %project.2 = (bf16[256,1024]{1,0:T(8,128)(2,1)}, bf16[256,1024]{1,0:T(8,128)(2,1)}, f32[4,264,256]{2,1,0:T(8,128)}) custom-call(s32[4]{0:T(128)} %pad_add_fusion.own, bf16[512,1024]{1,0:T(8,128)(2,1)} %k_ref.3, bf16[512,1024]{1,0:T(8,128)(2,1)} %v_ref.3, bf16[8,128,256]{2,1,0:T(8,128)(2,1)} %w1_ref.3, bf16[8,128,256]{2,1,0:T(8,128)(2,1)} %w1_ref.3), custom_call_target="tpu_custom_call" | custom-call | flops 671088640 | bytes 4194304 | tf_op jit(solution)/shard_map/project/pallas_call | solution.py:72
  5.8 0.1 collective-permute-start.1
  5.8 4.4 %collective-permute-start.3 = (bf16[256,1024]{1,0:T(8,128)(2,1)}, bf16[256,1024]{1,0:T(8,128)(2,1)S(1)}, u32[]{:S(2)}, u32[]{:S(2)}) collective-permute-start(bf16[256,1024]{1,0:T(8,128)(2,1)} %get-tuple-element.23.b_ref), channel_id=1, source_target_pairs={{1,2},{3,4},{5,6},{7,8},{9,10},{11,12},{13,14},{15,16},{17,18},{19... | collective-permute-start | bytes 1572872 | tf_op jit(solution)/shard_map/ppermute | solution.py:200
  10.3 5.2 %project.3 = (bf16[256,1024]{1,0:T(8,128)(2,1)}, bf16[256,1024]{1,0:T(8,128)(2,1)}, f32[4,264,256]{2,1,0:T(8,128)}) custom-call(s32[4]{0:T(128)} %pad_add_fusion.own, bf16[512,1024]{1,0:T(8,128)(2,1)} %k_ref.3, bf16[512,1024]{1,0:T(8,128)(2,1)} %v_ref.3, bf16[8,128,256]{2,1,0:T(8,128)(2,1)} %w1_ref.3, bf16[8,128,256]{2,1,0:T(8,128)(2,1)} %w1_ref.3), custom_call_target="tpu_custom_call" | custom-call | flops 671088640 | bytes 4194304 | tf_op jit(solution)/shard_map/project/pallas_call | solution.py:72
  15.5 0.0 collective-permute-done.1
  15.5 0.8 subtract_exponential_fusion.1
  16.3 1.4 %add_select_fusion = f32[4,264,256]{2,1,0:T(8,128)S(1)} fusion(f32[4,264,256]{2,1,0:T(8,128)S(1)} %collective-permute-done.1, f32[4,264,256]{2,1,0:T(8,128)} %get-tuple-element.25, f32[4,256]{1,0:T(4,128)S(1)} %bitcast.38, f32[4,256]{1,0:T(4,128)S(1)} %get-tuple-element.60, f32[4,256]{1,0:T(4,128)S(1)} %get-tuple-element.61, pred[264]{0:T(512)(128)(4,1)S(1)} %iota_compare_fusion), kind=kLoop, calls=%fused_computation | loop fusion | flops 1081344 | bytes 3256584 | tf_op jit(solution)/shard_map/jit(_where)/select_n | solution.py:103
  17.7 0.0 copy-start.3
  17.8 0.1 fusion.11
  17.8 0.0 copy-start.1
  17.8 0.0 copy-start
  17.9 0.0 copy-start.2
  17.9 1.4 %collective-permute-start.2 = (f32[1,264,128]{2,1,0:T(8,128)S(1)}, f32[1,264,128]{2,1,0:T(8,128)S(1)}, u32[]{:S(2)}, u32[]{:S(2)}) collective-permute-start(f32[1,264,128]{2,1,0:T(8,128)S(1)} %get-tuple-element.45), channel_id=1, source_target_pairs={{0,8},{1,9},{2,10},{3,11},{4,12},{5,13},{6,14},{7,15},{8,0},{9,1},... | collective-permute-start | bytes 405512 | tf_op jit(solution)/shard_map/ppermute | solution.py:108
  19.2 1.2 %collective-permute-start.4 = (f32[1,264,128]{2,1,0:T(8,128)S(1)}, f32[1,264,128]{2,1,0:T(8,128)S(1)}, u32[]{:S(2)}, u32[]{:S(2)}) collective-permute-start(f32[1,264,128]{2,1,0:T(8,128)S(1)} %get-tuple-element.43), channel_id=1, source_target_pairs={{0,4},{1,5},{2,6},{3,7},{4,0},{5,1},{6,2},{7,3},{8,12},{9,13},{10,... | collective-permute-start | bytes 405512 | tf_op jit(solution)/shard_map/ppermute | solution.py:108
  20.5 0.1 collective-permute-start.5
  20.6 1.8 %collective-permute-done.3.out_ref = bf16[256,1024]{1,0:T(8,128)(2,1)S(1)} collective-permute-done((bf16[256,1024]{1,0:T(8,128)(2,1)}, bf16[256,1024]{1,0:T(8,128)(2,1)S(1)}, u32[]{:S(2)}, u32[]{:S(2)}) %collective-permute-start.3) | collective-permute-done | bytes 524320 | tf_op jit(solution)/shard_map/ppermute | solution.py:200
  22.3 0.0 collective-permute-done.2
  22.3 2.8 %collective-permute-start.6 = (f32[1,264,128]{2,1,0:T(8,128)S(1)}, f32[1,264,128]{2,1,0:T(8,128)S(1)}, u32[]{:S(2)}, u32[]{:S(2)}) collective-permute-start(f32[1,264,128]{2,1,0:T(8,128)S(1)} %get-tuple-element.28), channel_id=1, source_target_pairs={{0,2},{1,3},{2,0},{3,1},{4,6},{5,7},{6,4},{7,5},{8,10},{9,11},{10,... | collective-permute-start | bytes 405512 | tf_op jit(solution)/shard_map/ppermute | solution.py:108
  25.2 1.0 %collective-permute-start.7 = (f32[1,264,128]{2,1,0:T(8,128)S(1)}, f32[1,264,128]{2,1,0:T(8,128)S(1)}, u32[]{:S(2)}, u32[]{:S(2)}) collective-permute-start(f32[1,264,128]{2,1,0:T(8,128)S(1)} %get-tuple-element.29), channel_id=1, source_target_pairs={{0,10},{1,11},{2,8},{3,9},{4,14},{5,15},{6,12},{7,13},{8,2},{9,3},... | collective-permute-start | bytes 405512 | tf_op jit(solution)/shard_map/ppermute | solution.py:108
  26.2 2.0 %collective-permute-start.8 = (f32[1,264,128]{2,1,0:T(8,128)S(1)}, f32[1,264,128]{2,1,0:T(8,128)S(1)}, u32[]{:S(2)}, u32[]{:S(2)}) collective-permute-start(f32[1,264,128]{2,1,0:T(8,128)S(1)} %get-tuple-element.30), channel_id=1, source_target_pairs={{0,6},{1,7},{2,4},{3,5},{4,2},{5,3},{6,0},{7,1},{8,14},{9,15},{10,... | collective-permute-start | bytes 405512 | tf_op jit(solution)/shard_map/ppermute | solution.py:108
  28.2 0.0 collective-permute-done.4
  28.2 1.6 %collective-permute-start.9 = (f32[1,264,128]{2,1,0:T(8,128)S(1)}, f32[1,264,128]{2,1,0:T(8,128)S(1)}, u32[]{:S(2)}, u32[]{:S(2)}) collective-permute-start(f32[1,264,128]{2,1,0:T(8,128)S(1)} %get-tuple-element.31), channel_id=1, source_target_pairs={{0,14},{1,15},{2,12},{3,13},{4,10},{5,11},{6,8},{7,9},{8,6},{9,7},... | collective-permute-start | bytes 405512 | tf_op jit(solution)/shard_map/ppermute | solution.py:108
  29.8 0.0 collective-permute-done.5
  29.8 1.5 %collective-permute-done.6 = f32[1,264,128]{2,1,0:T(8,128)S(1)} collective-permute-done((f32[1,264,128]{2,1,0:T(8,128)S(1)}, f32[1,264,128]{2,1,0:T(8,128)S(1)}, u32[]{:S(2)}, u32[]{:S(2)}) %collective-permute-start.6) | collective-permute-done | bytes 135200 | tf_op jit(solution)/shard_map/ppermute | solution.py:108
  31.3 0.0 collective-permute-done.7
  31.3 6.9 %collective-permute-done.8 = f32[1,264,128]{2,1,0:T(8,128)S(1)} collective-permute-done((f32[1,264,128]{2,1,0:T(8,128)S(1)}, f32[1,264,128]{2,1,0:T(8,128)S(1)}, u32[]{:S(2)}, u32[]{:S(2)}) %collective-permute-start.8) | collective-permute-done | bytes 135200 | tf_op jit(solution)/shard_map/ppermute | solution.py:108
  38.2 0.0 collective-permute-done.9
  38.2 0.1 fusion.7
  38.3 2.4 %collective-permute-start.10 = (f32[1,264,128]{2,1,0:T(8,128)S(1)}, f32[1,264,128]{2,1,0:T(8,128)S(1)}, u32[]{:S(2)}, u32[]{:S(2)}) collective-permute-start(f32[1,264,128]{2,1,0:T(8,128)S(1)} %fusion.7), channel_id=1, source_target_pairs={{0,16},{1,17},{2,18},{3,19},{4,20},{5,21},{6,22},{7,23},{8,24},{9,... | collective-permute-start | bytes 405512 | tf_op jit(solution)/shard_map/ppermute | solution.py:108
  40.7 0.0 copy-done.3
  40.7 1.7 %collective-permute-start.13 = (bf16[256,1024]{1,0:T(8,128)(2,1)S(1)}, bf16[256,1024]{1,0:T(8,128)(2,1)S(1)}, u32[]{:S(2)}, u32[]{:S(2)}) collective-permute-start(bf16[256,1024]{1,0:T(8,128)(2,1)S(1)} %copy-done.3), channel_id=1, source_target_pairs={{0,1},{1,0},{2,3},{3,2},{4,5},{5,4},{6,7},{7,6},{8,9},{9,8},{10,11... | collective-permute-start | bytes 1572872 | tf_op jit(solution)/shard_map/ppermute | solution.py:108
  42.4 0.0 copy-done.1
  42.4 2.8 %collective-permute-start.14 = (bf16[256,1024]{1,0:T(8,128)(2,1)S(1)}, bf16[256,1024]{1,0:T(8,128)(2,1)S(1)}, u32[]{:S(2)}, u32[]{:S(2)}) collective-permute-start(bf16[256,1024]{1,0:T(8,128)(2,1)S(1)} %copy-done.1), channel_id=1, source_target_pairs={{1,2},{3,4},{5,6},{7,8},{9,10},{11,12},{13,14},{15,16},{17,18},{19... | collective-permute-start | bytes 1572872 | tf_op jit(solution)/shard_map/ppermute | solution.py:202
  45.2 1.5 %collective-permute-done.10 = f32[1,264,128]{2,1,0:T(8,128)S(1)} collective-permute-done((f32[1,264,128]{2,1,0:T(8,128)S(1)}, f32[1,264,128]{2,1,0:T(8,128)S(1)}, u32[]{:S(2)}, u32[]{:S(2)}) %collective-permute-start.10) | collective-permute-done | bytes 135200 | tf_op jit(solution)/shard_map/ppermute | solution.py:108
  46.8 0.1 add_select_fusion.1
  46.9 1.1 %collective-permute-start.11 = (bf16[1,1,256,128]{3,2,1,0:T(8,128)(2,1)S(1)}, bf16[1,1,256,128]{3,2,1,0:T(8,128)(2,1)S(1)}, u32[]{:S(2)}, u32[]{:S(2)}) collective-permute-start(bf16[1,1,256,128]{3,2,1,0:T(8,128)(2,1)S(1)} %fusion.9), channel_id=1, source_target_pairs={{0,8},{1,9},{2,10},{3,11},{4,12},{5,13},{6,14},{7,15},{8,0},{9,1},... | collective-permute-start | bytes 196616 | tf_op jit(solution)/shard_map/ppermute | solution.py:108
  48.0 2.9 %collective-permute-done.11 = bf16[1,1,256,128]{3,2,1,0:T(8,128)(2,1)S(1)} collective-permute-done((bf16[1,1,256,128]{3,2,1,0:T(8,128)(2,1)S(1)}, bf16[1,1,256,128]{3,2,1,0:T(8,128)(2,1)S(1)}, u32[]{:S(2)}, u32[]{:S(2)}) %collective-permute-start.11) | collective-permute-done | bytes 65568 | tf_op jit(solution)/shard_map/ppermute | solution.py:108
  50.8 0.3 collective-permute-start.12
  51.1 0.0 collective-permute-done.13.in_ref
  51.1 0.0 copy-done
  51.1 0.0 copy-done.2
  51.1 6.0 %attend.4.refs_0_ = bf16[512,4096]{1,0:T(8,128)(2,1)} custom-call(s32[4]{0:T(128)S(1)} %copy-done.2, bf16[512,4096]{1,0:T(8,128)(2,1)} %q_ref.7, bf16[256,1024]{1,0:T(8,128)(2,1)S(1)} %copy-done, bf16[256,1024]{1,0:T(8,128)(2,1)S(1)} %copy-done.1, bf16[256,1024]{1,0:T(8,128)(2,1)S(1)} %collective-permute-done.13.in_ref, ...), custom_call_target="tpu_custom_call" | custom-call | flops 1342177280 | bytes 2097152 | tf_op jit(solution)/shard_map/attend/pallas_call | solution.py:156
  57.2 0.8 collective-permute-done.14.out_ref
  58.0 0.0 collective-permute-done.12.g_ref
  58.0 3.6 %collective-permute-start.15 = (bf16[2,2,256,128]{3,2,1,0:T(8,128)(2,1)S(1)}, bf16[2,2,256,128]{3,2,1,0:T(8,128)(2,1)S(1)}, u32[]{:S(2)}, u32[]{:S(2)}) collective-permute-start(bf16[2,2,256,128]{3,2,1,0:T(8,128)(2,1)S(1)} %pad_maximum_fusion.1), channel_id=1, source_target_pairs={{0,2},{1,3},{2,0},{3,1},{4,6},{5,7},{6,4},{7,5},{8,10},{9,11},{10,... | collective-permute-start | bytes 786440 | tf_op jit(solution)/shard_map/ppermute | solution.py:108
  61.6 0.7 collective-permute-start
  62.3 6.0 %attend.5.refs_0_ = bf16[512,4096]{1,0:T(8,128)(2,1)} custom-call(s32[4]{0:T(128)S(1)} %copy-done.2, bf16[512,4096]{1,0:T(8,128)(2,1)} %q_ref.7, bf16[256,1024]{1,0:T(8,128)(2,1)S(1)} %copy-done, bf16[256,1024]{1,0:T(8,128)(2,1)S(1)} %copy-done.1, bf16[256,1024]{1,0:T(8,128)(2,1)S(1)} %collective-permute-done.13.in_ref, ...), custom_call_target="tpu_custom_call", output_to_operand_aliasing={{}: (7, {})} | custom-call | flops 1342177280 | bytes 2097152 | tf_op jit(solution)/shard_map/attend/pallas_call | solution.py:156
  68.3 0.0 collective-permute-done.15.g_ref
  68.3 0.1 pad_maximum_fusion
  68.4 0.0 copy-start.4
  68.4 0.6 collective-permute-start.16
  69.0 10.0 %attend.6.refs_0_ = bf16[512,4096]{1,0:T(8,128)(2,1)} custom-call(s32[4]{0:T(128)S(1)} %copy-done.2, bf16[512,4096]{1,0:T(8,128)(2,1)} %q_ref.7, bf16[256,1024]{1,0:T(8,128)(2,1)S(1)} %copy-done, bf16[256,1024]{1,0:T(8,128)(2,1)S(1)} %copy-done.1, bf16[256,1024]{1,0:T(8,128)(2,1)S(1)} %collective-permute-done.13.in_ref, ...), custom_call_target="tpu_custom_call", output_to_operand_aliasing={{}: (7, {})} | custom-call | flops 2684354560 | bytes 4194304 | tf_op jit(solution)/shard_map/attend/pallas_call | solution.py:156
  79.0 0.0 collective-permute-done.in_ref
  79.0 0.0 collective-permute-done.16.g_ref
  79.0 0.0 copy-done.4
  79.0 17.4 %attend.7 = bf16[512,4096]{1,0:T(8,128)(2,1)} custom-call(s32[4]{0:T(128)S(1)} %copy-done.2, bf16[512,4096]{1,0:T(8,128)(2,1)} %q_ref.7, bf16[256,1024]{1,0:T(8,128)(2,1)S(1)} %copy-done.3, bf16[256,1024]{1,0:T(8,128)(2,1)S(1)} %copy-done.4, bf16[256,1024]{1,0:T(8,128)(2,1)S(1)} %collective-permute-done.in_ref, ...), custom_call_target="tpu_custom_call", output_to_operand_aliasing={{}: (7, {})} | custom-call | flops 5368709120 | bytes 8388608 | tf_op jit(solution)/shard_map/attend/pallas_call | solution.py:156
  (11 shorter events, 0.1 us)
Async XLA Ops:
  5.8 9.7 %collective-permute-start.1 = (f32[4,264,256]{2,1,0:T(8,128)}, f32[4,264,256]{2,1,0:T(8,128)S(1)}, u32[]{:S(2)}, u32[]{:S(2)}) collective-permute-start(f32[4,264,256]{2,1,0:T(8,128)} %get-tuple-element.26), channel_id=1, source_target_pairs={{0,1},{1,0},{2,3},{3,2},{4,5},{5,4},{6,7},{7,6},{8,9},{9,8},{10,11... | collective-permute-start | bytes 3244040 | tf_op jit(solution)/shard_map/ppermute | solution.py:108
  5.8 16.5 %collective-permute-start.3 = (bf16[256,1024]{1,0:T(8,128)(2,1)}, bf16[256,1024]{1,0:T(8,128)(2,1)S(1)}, u32[]{:S(2)}, u32[]{:S(2)}) collective-permute-start(bf16[256,1024]{1,0:T(8,128)(2,1)} %get-tuple-element.23.b_ref), channel_id=1, source_target_pairs={{1,2},{3,4},{5,6},{7,8},{9,10},{11,12},{13,14},{15,16},{17,18},{19... | collective-permute-start | bytes 1572872 | tf_op jit(solution)/shard_map/ppermute | solution.py:200
  17.7 23.0 %copy-start.3 = (bf16[256,1024]{1,0:T(8,128)(2,1)S(1)}, bf16[256,1024]{1,0:T(8,128)(2,1)}, u32[]{:S(2)}) copy-start(bf16[256,1024]{1,0:T(8,128)(2,1)} %get-tuple-element.22.a_ref) | copy-start | bytes 1572868
  17.8 24.5 %copy-start.1 = (bf16[256,1024]{1,0:T(8,128)(2,1)S(1)}, bf16[256,1024]{1,0:T(8,128)(2,1)}, u32[]{:S(2)}) copy-start(bf16[256,1024]{1,0:T(8,128)(2,1)} %get-tuple-element.32.b_ref) | copy-start | bytes 1572868
  17.8 33.3 %copy-start = (bf16[256,1024]{1,0:T(8,128)(2,1)S(1)}, bf16[256,1024]{1,0:T(8,128)(2,1)}, u32[]{:S(2)}) copy-start(bf16[256,1024]{1,0:T(8,128)(2,1)} %get-tuple-element.24.a_ref) | copy-start | bytes 1572868
  17.9 33.3 %copy-start.2 = (s32[4]{0:T(128)S(1)}, s32[4]{0:T(128)}, u32[]{:S(2)}) copy-start(s32[4]{0:T(128)} %pad_add_fusion.own) | copy-start | bytes 52
  17.9 4.5 %collective-permute-start.2 = (f32[1,264,128]{2,1,0:T(8,128)S(1)}, f32[1,264,128]{2,1,0:T(8,128)S(1)}, u32[]{:S(2)}, u32[]{:S(2)}) collective-permute-start(f32[1,264,128]{2,1,0:T(8,128)S(1)} %get-tuple-element.45), channel_id=1, source_target_pairs={{0,8},{1,9},{2,10},{3,11},{4,12},{5,13},{6,14},{7,15},{8,0},{9,1},... | collective-permute-start | bytes 405512 | tf_op jit(solution)/shard_map/ppermute | solution.py:108
  19.2 9.0 %collective-permute-start.4 = (f32[1,264,128]{2,1,0:T(8,128)S(1)}, f32[1,264,128]{2,1,0:T(8,128)S(1)}, u32[]{:S(2)}, u32[]{:S(2)}) collective-permute-start(f32[1,264,128]{2,1,0:T(8,128)S(1)} %get-tuple-element.43), channel_id=1, source_target_pairs={{0,4},{1,5},{2,6},{3,7},{4,0},{5,1},{6,2},{7,3},{8,12},{9,13},{10,... | collective-permute-start | bytes 405512 | tf_op jit(solution)/shard_map/ppermute | solution.py:108
  20.5 9.3 %collective-permute-start.5 = (f32[1,264,128]{2,1,0:T(8,128)S(1)}, f32[1,264,128]{2,1,0:T(8,128)S(1)}, u32[]{:S(2)}, u32[]{:S(2)}) collective-permute-start(f32[1,264,128]{2,1,0:T(8,128)S(1)} %get-tuple-element.44), channel_id=1, source_target_pairs={{0,12},{1,13},{2,14},{3,15},{4,8},{5,9},{6,10},{7,11},{8,4},{9,5},... | collective-permute-start | bytes 405512 | tf_op jit(solution)/shard_map/ppermute | solution.py:108
  22.3 8.9 %collective-permute-start.6 = (f32[1,264,128]{2,1,0:T(8,128)S(1)}, f32[1,264,128]{2,1,0:T(8,128)S(1)}, u32[]{:S(2)}, u32[]{:S(2)}) collective-permute-start(f32[1,264,128]{2,1,0:T(8,128)S(1)} %get-tuple-element.28), channel_id=1, source_target_pairs={{0,2},{1,3},{2,0},{3,1},{4,6},{5,7},{6,4},{7,5},{8,10},{9,11},{10,... | collective-permute-start | bytes 405512 | tf_op jit(solution)/shard_map/ppermute | solution.py:108
  25.2 6.1 %collective-permute-start.7 = (f32[1,264,128]{2,1,0:T(8,128)S(1)}, f32[1,264,128]{2,1,0:T(8,128)S(1)}, u32[]{:S(2)}, u32[]{:S(2)}) collective-permute-start(f32[1,264,128]{2,1,0:T(8,128)S(1)} %get-tuple-element.29), channel_id=1, source_target_pairs={{0,10},{1,11},{2,8},{3,9},{4,14},{5,15},{6,12},{7,13},{8,2},{9,3},... | collective-permute-start | bytes 405512 | tf_op jit(solution)/shard_map/ppermute | solution.py:108
  26.2 12.0 %collective-permute-start.8 = (f32[1,264,128]{2,1,0:T(8,128)S(1)}, f32[1,264,128]{2,1,0:T(8,128)S(1)}, u32[]{:S(2)}, u32[]{:S(2)}) collective-permute-start(f32[1,264,128]{2,1,0:T(8,128)S(1)} %get-tuple-element.30), channel_id=1, source_target_pairs={{0,6},{1,7},{2,4},{3,5},{4,2},{5,3},{6,0},{7,1},{8,14},{9,15},{10,... | collective-permute-start | bytes 405512 | tf_op jit(solution)/shard_map/ppermute | solution.py:108
  28.2 10.0 %collective-permute-start.9 = (f32[1,264,128]{2,1,0:T(8,128)S(1)}, f32[1,264,128]{2,1,0:T(8,128)S(1)}, u32[]{:S(2)}, u32[]{:S(2)}) collective-permute-start(f32[1,264,128]{2,1,0:T(8,128)S(1)} %get-tuple-element.31), channel_id=1, source_target_pairs={{0,14},{1,15},{2,12},{3,13},{4,10},{5,11},{6,8},{7,9},{8,6},{9,7},... | collective-permute-start | bytes 405512 | tf_op jit(solution)/shard_map/ppermute | solution.py:108
  38.3 8.4 %collective-permute-start.10 = (f32[1,264,128]{2,1,0:T(8,128)S(1)}, f32[1,264,128]{2,1,0:T(8,128)S(1)}, u32[]{:S(2)}, u32[]{:S(2)}) collective-permute-start(f32[1,264,128]{2,1,0:T(8,128)S(1)} %fusion.7), channel_id=1, source_target_pairs={{0,16},{1,17},{2,18},{3,19},{4,20},{5,21},{6,22},{7,23},{8,24},{9,... | collective-permute-start | bytes 405512 | tf_op jit(solution)/shard_map/ppermute | solution.py:108
  40.7 10.4 %collective-permute-start.13 = (bf16[256,1024]{1,0:T(8,128)(2,1)S(1)}, bf16[256,1024]{1,0:T(8,128)(2,1)S(1)}, u32[]{:S(2)}, u32[]{:S(2)}) collective-permute-start(bf16[256,1024]{1,0:T(8,128)(2,1)S(1)} %copy-done.3), channel_id=1, source_target_pairs={{0,1},{1,0},{2,3},{3,2},{4,5},{5,4},{6,7},{7,6},{8,9},{9,8},{10,11... | collective-permute-start | bytes 1572872 | tf_op jit(solution)/shard_map/ppermute | solution.py:108
  42.4 15.6 %collective-permute-start.14 = (bf16[256,1024]{1,0:T(8,128)(2,1)S(1)}, bf16[256,1024]{1,0:T(8,128)(2,1)S(1)}, u32[]{:S(2)}, u32[]{:S(2)}) collective-permute-start(bf16[256,1024]{1,0:T(8,128)(2,1)S(1)} %copy-done.1), channel_id=1, source_target_pairs={{1,2},{3,4},{5,6},{7,8},{9,10},{11,12},{13,14},{15,16},{17,18},{19... | collective-permute-start | bytes 1572872 | tf_op jit(solution)/shard_map/ppermute | solution.py:202
  46.9 3.9 %collective-permute-start.11 = (bf16[1,1,256,128]{3,2,1,0:T(8,128)(2,1)S(1)}, bf16[1,1,256,128]{3,2,1,0:T(8,128)(2,1)S(1)}, u32[]{:S(2)}, u32[]{:S(2)}) collective-permute-start(bf16[1,1,256,128]{3,2,1,0:T(8,128)(2,1)S(1)} %fusion.9), channel_id=1, source_target_pairs={{0,8},{1,9},{2,10},{3,11},{4,12},{5,13},{6,14},{7,15},{8,0},{9,1},... | collective-permute-start | bytes 196616 | tf_op jit(solution)/shard_map/ppermute | solution.py:108
  50.8 7.1 %collective-permute-start.12 = (bf16[1,2,256,128]{3,2,1,0:T(8,128)(2,1)S(1)}, bf16[1,2,256,128]{3,2,1,0:T(8,128)(2,1)S(1)}, u32[]{:S(2)}, u32[]{:S(2)}) collective-permute-start(bf16[1,2,256,128]{3,2,1,0:T(8,128)(2,1)S(1)} %pad_maximum_fusion.2.g_ref), channel_id=1, source_target_pairs={{0,4},{1,5},{2,6},{3,7},{4,0},{5,1},{6,2},{7,3},{8,12},{9,13},{10,... | collective-permute-start | bytes 393224 | tf_op jit(solution)/shard_map/ppermute | solution.py:108
  58.0 10.3 %collective-permute-start.15 = (bf16[2,2,256,128]{3,2,1,0:T(8,128)(2,1)S(1)}, bf16[2,2,256,128]{3,2,1,0:T(8,128)(2,1)S(1)}, u32[]{:S(2)}, u32[]{:S(2)}) collective-permute-start(bf16[2,2,256,128]{3,2,1,0:T(8,128)(2,1)S(1)} %pad_maximum_fusion.1), channel_id=1, source_target_pairs={{0,2},{1,3},{2,0},{3,1},{4,6},{5,7},{6,4},{7,5},{8,10},{9,11},{10,... | collective-permute-start | bytes 786440 | tf_op jit(solution)/shard_map/ppermute | solution.py:108
  61.6 17.4 %collective-permute-start = (bf16[256,1024]{1,0:T(8,128)(2,1)S(1)}, bf16[256,1024]{1,0:T(8,128)(2,1)S(1)}, u32[]{:S(2)}, u32[]{:S(2)}) collective-permute-start(bf16[256,1024]{1,0:T(8,128)(2,1)S(1)} %copy-done), channel_id=1, source_target_pairs={{0,1},{1,0},{2,3},{3,2},{4,5},{5,4},{6,7},{7,6},{8,9},{9,8},{10,11... | collective-permute-start | bytes 1572872 | tf_op jit(solution)/shard_map/ppermute | solution.py:108
  68.4 10.6 %copy-start.4 = (bf16[256,1024]{1,0:T(8,128)(2,1)S(1)}, bf16[256,1024]{1,0:T(8,128)(2,1)}, u32[]{:S(2)}) copy-start(bf16[256,1024]{1,0:T(8,128)(2,1)} %get-tuple-element.23.b_ref) | copy-start | bytes 1572868
  68.4 10.6 %collective-permute-start.16 = (bf16[4,2,256,128]{3,2,1,0:T(8,128)(2,1)S(1)}, bf16[4,2,256,128]{3,2,1,0:T(8,128)(2,1)S(1)}, u32[]{:S(2)}, u32[]{:S(2)}) collective-permute-start(bf16[4,2,256,128]{3,2,1,0:T(8,128)(2,1)S(1)} %pad_maximum_fusion), channel_id=1, source_target_pairs={{0,1},{1,0},{2,3},{3,2},{4,5},{5,4},{6,7},{7,6},{8,9},{9,8},{10,11... | collective-permute-start | bytes 1572872 | tf_op jit(solution)/shard_map/ppermute | solution.py:108

commit v4 on v3

--- a/solution.py
+++ b/solution.py
@@ -21,8 +21,8 @@
 EXP2_SCALE = math.log2(math.e) / math.sqrt(HD)
 FAR_AWAY = 1e30
 BLOCKS = 5
-PROJECT_VMEM = 60 << 20
-ATTEND_VMEM = 48 << 20
+PROJECT_VMEM = 16 << 20
+ATTEND_VMEM = 24 << 20
 
 HEAD_BITS = (4, 2, 1)
 HALF_BIT = 8
@@ -57,8 +57,9 @@
         lower = (expo - upper.astype(jnp.float32)).astype(jnp.bfloat16)
         pair = jnp.concatenate([keys, values], axis=1)
         dims = (((0,), (0,)), ((), ()))
-        both = lax.dot_general(pair, upper, dims, preferred_element_type=jnp.float32)
-        both = both + lax.dot_general(pair, lower, dims, preferred_element_type=jnp.float32)
+        split = jnp.concatenate([upper, lower], axis=1)
+        both = lax.dot_general(pair, split, dims, preferred_element_type=jnp.float32)
+        both = both[:, :R] + both[:, R:]
         part_ref[i, : 2 * HD] = both
         row = lax.broadcasted_iota(jnp.int32, (AUX, R), 0)
         part_ref[i, 2 * HD :] = jnp.where(row == 0, total, jnp.where(row == 1, top, 0.0))
@@ -108,70 +109,84 @@
     return lax.ppermute(x, "ctx", [(i, i ^ bits) for i in range(peers)])
 
 
-def attend_kernel(own, q_ref, a_ref, b_ref, in_ref, out_ref, g_ref, *refs):
+def attend_kernel(per, own, q_ref, a_ref, b_ref, in_ref, out_ref, g_ref, *refs):
     o_ref, k_ref, v_ref = refs[-3:]
     hide = (0.0, 0.0, 0.0, jnp.where(own[3] > 0, 0.0, FAR_AWAY), 0.0)
-    for i, x in enumerate((a_ref, b_ref, in_ref, out_ref)):
-        k_ref[i * HALF : (i + 1) * HALF] = x[:, :HD]
-        v_ref[:, i * HALF : (i + 1) * HALF] = x[:, HD:].T
-    for i in range(2):
-        at = 4 * HALF + i * HD
-        k_ref[at : at + HD] = g_ref[0, i, :HD].T
-        v_ref[:, at : at + HD] = g_ref[0, i, HD:]
     flip = (((1,), (1,)), ((), ()))
-
-    def score(g, i):
+    sides = [(h ^ own[0]) & (per - 1) for h in range(per)]
+
+    def columns(h, start, width, size):
+        if per == 1:
+            return slice(start, start + width)
+        return pl.ds(pl.multiple_of(sides[h] * size + start, HD), width)
+
+    def load(h):
+        for i, x in enumerate((a_ref, b_ref, in_ref, out_ref)):
+            k_ref[h, i * HALF : (i + 1) * HALF] = x[:, columns(h, 0, HD, 2 * HD)]
+            v_ref[h, :, i * HALF : (i + 1) * HALF] = x[:, columns(h, HD, HD, 2 * HD)].T
+        for i in range(2):
+            at = 4 * HALF + i * HD
+            k_ref[h, at : at + HD] = g_ref[h, i, :HD].T
+            v_ref[h, :, at : at + HD] = g_ref[h, i, HD:]
+
+    def score(h, g, i):
         return lax.dot_general(
-            k_ref[i * HALF : (i + 1) * HALF],
-            q_ref[:, g * HD : (g + 1) * HD],
+            k_ref[h, i * HALF : (i + 1) * HALF],
+            q_ref[:, columns(h, g * HD, HD, GROUP * HD)],
             flip,
             preferred_element_type=jnp.float32,
         )
 
-    scores = [score(0, i) for i in range(BLOCKS)]
-    for g in range(GROUP):
+    load(0)
+    tiles = [(h, g) for h in range(per) for g in range(GROUP)]
+    scores = [score(0, 0, i) for i in range(BLOCKS)]
+    for n, (h, g) in enumerate(tiles):
+        if g == 1 and h + 1 < per:
+            load(h + 1)
         tops = [jnp.max(s, axis=0, keepdims=True) - w for s, w in zip(scores, hide)]
         top = functools.reduce(jnp.maximum, tops)
         ahead, expo, total = [], [], 0.0
         for i in range(BLOCKS):
-            if g + 1 < GROUP:
-                ahead.append(score(g + 1, i))
+            if n + 1 < len(tiles):
+                ahead.append(score(*tiles[n + 1], i))
             e = jnp.exp2((scores[i] - (top + hide[i])) * EXP2_SCALE)
             total = total + jnp.sum(e, axis=0, keepdims=True)
             expo.append(e)
         inverse = 1.0 / total
         probs = jnp.concatenate([(e * inverse).astype(jnp.bfloat16) for e in expo], axis=0)
-        mixed = jnp.dot(v_ref[...], probs, preferred_element_type=jnp.float32)
-        o_ref[:, g * HD : (g + 1) * HD] = mixed.T.astype(jnp.bfloat16)
+        mixed = jnp.dot(v_ref[h], probs, preferred_element_type=jnp.float32)
+        o_ref[:, columns(h, g * HD, HD, GROUP * HD)] = mixed.T.astype(jnp.bfloat16)
         scores = ahead
 
 
-def attend(base, own, queries, nears, far, out=None):
+def attend(base, own, queries, nears, far, out=None, per=1):
     tok = queries.shape[0]
     count = far.shape[0]
-    head = lambda i, own: base + i ^ own[0]
-    place = lambda i, own: head(i, own) % (KV // 2)
-    edge = pl.BlockSpec((HALF, 2 * HD), lambda i, own: (0, place(i, own)))
+    block = lambda i, own: (base + per * i ^ own[0]) // per
+    edge = pl.BlockSpec(
+        (HALF, per * 2 * HD), lambda i, own: (0, block(i, own) % (KV // 2 // per))
+    )
+    whole = pl.BlockSpec((tok, per * GROUP * HD), lambda i, own: (0, block(i, own)))
     extra = [] if out is None else [out]
     return pl.pallas_call(
-        attend_kernel,
+        functools.partial(attend_kernel, per),
         out_shape=jax.ShapeDtypeStruct(queries.shape, jnp.bfloat16),
         grid_spec=pltpu.PrefetchScalarGridSpec(
             num_scalar_prefetch=1,
-            grid=(count,),
+            grid=(count // per,),
             in_specs=[
-                pl.BlockSpec((tok, GROUP * HD), lambda i, own: (0, head(i, own))),
-                edge,
-                edge,
-                edge,
-                edge,
-                pl.BlockSpec((1, 2, 2 * HD, R // 2), lambda i, own: (i, 0, 0, 0)),
+                whole,
+                edge,
+                edge,
+                edge,
+                edge,
+                pl.BlockSpec((per, 2, 2 * HD, R // 2), lambda i, own: (i, 0, 0, 0)),
             ]
             + [pl.BlockSpec(memory_space=pl.ANY)] * len(extra),
-            out_specs=pl.BlockSpec((tok, GROUP * HD), lambda i, own: (0, head(i, own))),
+            out_specs=whole,
             scratch_shapes=[
-                pltpu.VMEM((BLOCKS * HALF, HD), jnp.bfloat16),
-                pltpu.VMEM((HD, BLOCKS * HALF), jnp.bfloat16),
+                pltpu.VMEM((per, BLOCKS * HALF, HD), jnp.bfloat16),
+                pltpu.VMEM((per, HD, BLOCKS * HALF), jnp.bfloat16),
             ],
         ),
         input_output_aliases={7: 0} if extra else {},
@@ -195,6 +210,9 @@
     b0, b1, b2 = HEAD_BITS
     across = [(i, i + 1) for i in range(1, peers - 1, 2)]
     across = across + [(j, i) for i, j in across]
+    keys, values, proj_weight = [
+        pltpu.with_memory_space_constraint(x, pltpu.HBM) for x in (keys, values, proj_weight)
+    ]
     in1, out1, sent = project(KV // 2, own, keys, values, proj_weight)
     in0, out0, kept = project(0, own, keys, values, proj_weight)
     outer0 = lax.ppermute(out1, "ctx", across)
@@ -227,8 +245,8 @@
     at23, out = lax.optimization_barrier((at23, out))
     at4567 = swap(jnp.concatenate([at01, at23], axis=0), b2)
     nears1 = (in1, out1, inner1, outer1)
-    out = attend(2, own, queries, nears0, at23, out)
-    return attend(4, own, queries, nears1, at4567, out)
+    out = attend(2, own, queries, nears0, at23, out, 2)
+    return attend(4, own, queries, nears1, at4567, out, 2)
 
 
 def solution(mesh):

time: 97.1 us -> 92.3 us (0.951)
  Pallas kernels: 49.8 us -> 44.2 us
  waiting for transfers between devices: 15.4 us -> 18 us
  other arithmetic: 3.22 us -> 0.75 us
  starting transfers between devices: 27.7 us -> 28.9 us
    pallas_call x4, Pallas kernels: 39.5 us -> 35.7 us  [attend(): pl.pallas_call(functools.partial(attend_kernel, per), out_shape=jax.Shape...]
    ppermute x1, waiting for transfers between devices: 1.76 us -> 4.45 us  [on_device(): outer0 = lax.ppermute(out1, 'ctx', across)]
    ppermute x15, starting transfers between devices: 20.5 us -> 22.4 us  [swap(): return lax.ppermute(x, 'ctx', [(i, i ^ bits) for i in range(peers)])]
    pallas_call x2, Pallas kernels: 10.4 us -> 8.56 us  [project(): pl.pallas_call(project_kernel, out_shape=(jax.ShapeDtypeStruct((HALF, cou...]
    select_n x3, other arithmetic: 1.67 us -> 0.48 us  [merge(): return jnp.where(row == M_ROW, top, added)]
  transfers between devices with their start and end apart: 17 -> 17, of which waited for: 6 -> 6; matrix products, arithmetic and copies ran while one was open for 3% -> 1% of each run, Pallas kernels for 28% -> 26%
where the time goes in v4:
time: 92.3 us; the launch traced here: 92.1 us
  Pallas kernels  44.2 us (48%)
  starting transfers between devices  28.9 us (31%)
  waiting for transfers between devices  18 us (20%)
    pallas_call x4, Pallas kernels, attend(): pl.pallas_call(functools.partial(attend_kernel, per), out_shape=jax.Shape...  35.7 us
    ppermute x15, starting transfers between devices, swap(): return lax.ppermute(x, 'ctx', [(i, i ^ bits) for i in range(peers)])  22.4 us
    ppermute x15, waiting for transfers between devices, swap(): return lax.ppermute(x, 'ctx', [(i, i ^ bits) for i in range(peers)])  12.8 us
    pallas_call x2, Pallas kernels, project(): pl.pallas_call(project_kernel, out_shape=(jax.ShapeDtypeStruct((HALF, cou...  8.56 us
    ppermute x1, starting transfers between devices, on_device(): outer0 = lax.ppermute(out1, 'ctx', across)  4.47 us
    ppermute x1, waiting for transfers between devices, on_device(): outer0 = lax.ppermute(out1, 'ctx', across)  4.45 us
    ppermute x1, starting transfers between devices, on_device(): outer1 = lax.ppermute(out0, 'ctx', across)  2.09 us
  transfers between devices with their start and end apart: 17, of which 6 were waited for; matrix products, arithmetic and copies ran while one was open for 1% of the time, Pallas kernels for 26%

profile of v4, /device:TPU:1, one launch (start us, length us, event | category | flops | bytes accessed | tf_op | source)
XLA Modules:
  0.0 92.1 jit_solution(8705805224399916410)
XLA Ops:
  0.0 0.1 pad_add_fusion.own
  0.1 4.3 %project.2 = (bf16[256,1024]{1,0:T(8,128)(2,1)S(1)}, bf16[256,1024]{1,0:T(8,128)(2,1)S(1)}, f32[4,264,256]{2,1,0:T(8,128)S(1)}) custom-call(s32[4]{0:T(128)S(1)} %pad_add_fusion.own, bf16[512,1024]{1,0:T(8,128)(2,1)} %k_ref.3, bf16[512,1024]{1,0:T(8,128)(2,1)} %v_ref.3, bf16[8,128,256]{2,1,0:T(8,128)(2,1)} %w1_ref.3, bf16[8,128,256]{2,1,0:T(8,128)(2,1)} %w1_ref.3), custom_call_target="tpu_custom_call" | custom-call | flops 671088640 | bytes 4194304 | tf_op jit(solution)/shard_map/project/pallas_call | solution.py:73
  4.4 0.1 collective-permute-start.1
  4.5 4.5 %collective-permute-start.3 = (bf16[256,1024]{1,0:T(8,128)(2,1)S(1)}, bf16[256,1024]{1,0:T(8,128)(2,1)S(1)}, u32[]{:S(2)}, u32[]{:S(2)}) collective-permute-start(bf16[256,1024]{1,0:T(8,128)(2,1)S(1)} %get-tuple-element.23.b_ref), channel_id=1, source_target_pairs={{1,2},{3,4},{5,6},{7,8},{9,10},{11,12},{13,14},{15,16},{17,18},{19... | collective-permute-start | bytes 1572872 | tf_op jit(solution)/shard_map/ppermute | solution.py:218
  9.0 4.3 %project.3 = (bf16[256,1024]{1,0:T(8,128)(2,1)S(1)}, bf16[256,1024]{1,0:T(8,128)(2,1)S(1)}, f32[4,264,256]{2,1,0:T(8,128)S(1)}) custom-call(s32[4]{0:T(128)S(1)} %pad_add_fusion.own, bf16[512,1024]{1,0:T(8,128)(2,1)} %k_ref.3, bf16[512,1024]{1,0:T(8,128)(2,1)} %v_ref.3, bf16[8,128,256]{2,1,0:T(8,128)(2,1)} %w1_ref.3, bf16[8,128,256]{2,1,0:T(8,128)(2,1)} %w1_ref.3), custom_call_target="tpu_custom_call" | custom-call | flops 671088640 | bytes 4194304 | tf_op jit(solution)/shard_map/project/pallas_call | solution.py:73
  13.3 0.0 collective-permute-done.1
  13.3 0.0 copy-start
  13.4 0.2 add_select_fusion
  13.6 0.1 fusion.11
  13.7 1.4 %collective-permute-start.2 = (f32[1,264,128]{2,1,0:T(8,128)S(1)}, f32[1,264,128]{2,1,0:T(8,128)S(1)}, u32[]{:S(2)}, u32[]{:S(2)}) collective-permute-start(f32[1,264,128]{2,1,0:T(8,128)S(1)} %get-tuple-element.45), channel_id=1, source_target_pairs={{0,8},{1,9},{2,10},{3,11},{4,12},{5,13},{6,14},{7,15},{8,0},{9,1},... | collective-permute-start | bytes 405512 | tf_op jit(solution)/shard_map/ppermute | solution.py:109
  15.0 1.2 %collective-permute-start.4 = (f32[1,264,128]{2,1,0:T(8,128)S(1)}, f32[1,264,128]{2,1,0:T(8,128)S(1)}, u32[]{:S(2)}, u32[]{:S(2)}) collective-permute-start(f32[1,264,128]{2,1,0:T(8,128)S(1)} %get-tuple-element.43), channel_id=1, source_target_pairs={{0,4},{1,5},{2,6},{3,7},{4,0},{5,1},{6,2},{7,3},{8,12},{9,13},{10,... | collective-permute-start | bytes 405512 | tf_op jit(solution)/shard_map/ppermute | solution.py:109
  16.3 0.1 collective-permute-start.5
  16.4 4.5 %collective-permute-done.3.out_ref = bf16[256,1024]{1,0:T(8,128)(2,1)S(1)} collective-permute-done((bf16[256,1024]{1,0:T(8,128)(2,1)S(1)}, bf16[256,1024]{1,0:T(8,128)(2,1)S(1)}, u32[]{:S(2)}, u32[]{:S(2)}) %collective-permute-start.3) | collective-permute-done | bytes 524320 | tf_op jit(solution)/shard_map/ppermute | solution.py:218
  20.8 0.0 collective-permute-done.2
  20.8 3.8 %collective-permute-start.6 = (f32[1,264,128]{2,1,0:T(8,128)S(1)}, f32[1,264,128]{2,1,0:T(8,128)S(1)}, u32[]{:S(2)}, u32[]{:S(2)}) collective-permute-start(f32[1,264,128]{2,1,0:T(8,128)S(1)} %get-tuple-element.28), channel_id=1, source_target_pairs={{0,2},{1,3},{2,0},{3,1},{4,6},{5,7},{6,4},{7,5},{8,10},{9,11},{10,... | collective-permute-start | bytes 405512 | tf_op jit(solution)/shard_map/ppermute | solution.py:109
  24.7 1.0 %collective-permute-start.7 = (f32[1,264,128]{2,1,0:T(8,128)S(1)}, f32[1,264,128]{2,1,0:T(8,128)S(1)}, u32[]{:S(2)}, u32[]{:S(2)}) collective-permute-start(f32[1,264,128]{2,1,0:T(8,128)S(1)} %get-tuple-element.29), channel_id=1, source_target_pairs={{0,10},{1,11},{2,8},{3,9},{4,14},{5,15},{6,12},{7,13},{8,2},{9,3},... | collective-permute-start | bytes 405512 | tf_op jit(solution)/shard_map/ppermute | solution.py:109
  25.7 0.1 collective-permute-start.8
  25.8 0.0 collective-permute-done.4
  25.8 2.3 %collective-permute-start.9 = (f32[1,264,128]{2,1,0:T(8,128)S(1)}, f32[1,264,128]{2,1,0:T(8,128)S(1)}, u32[]{:S(2)}, u32[]{:S(2)}) collective-permute-start(f32[1,264,128]{2,1,0:T(8,128)S(1)} %get-tuple-element.31), channel_id=1, source_target_pairs={{0,14},{1,15},{2,12},{3,13},{4,10},{5,11},{6,8},{7,9},{8,6},{9,7},... | collective-permute-start | bytes 405512 | tf_op jit(solution)/shard_map/ppermute | solution.py:109
  28.0 0.0 collective-permute-done.5
  28.0 5.7 %collective-permute-done.6 = f32[1,264,128]{2,1,0:T(8,128)S(1)} collective-permute-done((f32[1,264,128]{2,1,0:T(8,128)S(1)}, f32[1,264,128]{2,1,0:T(8,128)S(1)}, u32[]{:S(2)}, u32[]{:S(2)}) %collective-permute-start.6) | collective-permute-done | bytes 135200 | tf_op jit(solution)/shard_map/ppermute | solution.py:109
  33.7 0.0 collective-permute-done.7
  33.7 2.2 %collective-permute-done.8 = f32[1,264,128]{2,1,0:T(8,128)S(1)} collective-permute-done((f32[1,264,128]{2,1,0:T(8,128)S(1)}, f32[1,264,128]{2,1,0:T(8,128)S(1)}, u32[]{:S(2)}, u32[]{:S(2)}) %collective-permute-start.8) | collective-permute-done | bytes 135200 | tf_op jit(solution)/shard_map/ppermute | solution.py:109
  36.0 0.0 collective-permute-done.9
  36.0 0.1 fusion.7
  36.1 3.0 %collective-permute-start.10 = (f32[1,264,128]{2,1,0:T(8,128)S(1)}, f32[1,264,128]{2,1,0:T(8,128)S(1)}, u32[]{:S(2)}, u32[]{:S(2)}) collective-permute-start(f32[1,264,128]{2,1,0:T(8,128)S(1)} %fusion.7), channel_id=1, source_target_pairs={{0,16},{1,17},{2,18},{3,19},{4,20},{5,21},{6,22},{7,23},{8,24},{9,... | collective-permute-start | bytes 405512 | tf_op jit(solution)/shard_map/ppermute | solution.py:109
  39.1 1.7 %collective-permute-start.13 = (bf16[256,1024]{1,0:T(8,128)(2,1)S(1)}, bf16[256,1024]{1,0:T(8,128)(2,1)S(1)}, u32[]{:S(2)}, u32[]{:S(2)}) collective-permute-start(bf16[256,1024]{1,0:T(8,128)(2,1)S(1)} %get-tuple-element.22.a_ref), channel_id=1, source_target_pairs={{0,1},{1,0},{2,3},{3,2},{4,5},{5,4},{6,7},{7,6},{8,9},{9,8},{10,11... | collective-permute-start | bytes 1572872 | tf_op jit(solution)/shard_map/ppermute | solution.py:109
  40.8 2.1 %collective-permute-start.14 = (bf16[256,1024]{1,0:T(8,128)(2,1)S(1)}, bf16[256,1024]{1,0:T(8,128)(2,1)S(1)}, u32[]{:S(2)}, u32[]{:S(2)}) collective-permute-start(bf16[256,1024]{1,0:T(8,128)(2,1)S(1)} %get-tuple-element.32.b_ref), channel_id=1, source_target_pairs={{1,2},{3,4},{5,6},{7,8},{9,10},{11,12},{13,14},{15,16},{17,18},{19... | collective-permute-start | bytes 1572872 | tf_op jit(solution)/shard_map/ppermute | solution.py:220
  42.9 2.1 %collective-permute-done.10 = f32[1,264,128]{2,1,0:T(8,128)S(1)} collective-permute-done((f32[1,264,128]{2,1,0:T(8,128)S(1)}, f32[1,264,128]{2,1,0:T(8,128)S(1)}, u32[]{:S(2)}, u32[]{:S(2)}) %collective-permute-start.10) | collective-permute-done | bytes 135200 | tf_op jit(solution)/shard_map/ppermute | solution.py:109
  45.0 0.1 add_select_fusion.1
  45.1 1.2 %collective-permute-start.11 = (bf16[1,1,256,128]{3,2,1,0:T(8,128)(2,1)S(1)}, bf16[1,1,256,128]{3,2,1,0:T(8,128)(2,1)S(1)}, u32[]{:S(2)}, u32[]{:S(2)}) collective-permute-start(bf16[1,1,256,128]{3,2,1,0:T(8,128)(2,1)S(1)} %fusion.9), channel_id=1, source_target_pairs={{0,8},{1,9},{2,10},{3,11},{4,12},{5,13},{6,14},{7,15},{8,0},{9,1},... | collective-permute-start | bytes 196616 | tf_op jit(solution)/shard_map/ppermute | solution.py:109
  46.3 2.8 %collective-permute-done.11 = bf16[1,1,256,128]{3,2,1,0:T(8,128)(2,1)S(1)} collective-permute-done((bf16[1,1,256,128]{3,2,1,0:T(8,128)(2,1)S(1)}, bf16[1,1,256,128]{3,2,1,0:T(8,128)(2,1)S(1)}, u32[]{:S(2)}, u32[]{:S(2)}) %collective-permute-start.11) | collective-permute-done | bytes 65568 | tf_op jit(solution)/shard_map/ppermute | solution.py:109
  49.1 2.1 %collective-permute-start.12 = (bf16[1,2,256,128]{3,2,1,0:T(8,128)(2,1)S(1)}, bf16[1,2,256,128]{3,2,1,0:T(8,128)(2,1)S(1)}, u32[]{:S(2)}, u32[]{:S(2)}) collective-permute-start(bf16[1,2,256,128]{3,2,1,0:T(8,128)(2,1)S(1)} %pad_maximum_fusion.2.g_ref), channel_id=1, source_target_pairs={{0,4},{1,5},{2,6},{3,7},{4,0},{5,1},{6,2},{7,3},{8,12},{9,13},{10,... | collective-permute-start | bytes 393224 | tf_op jit(solution)/shard_map/ppermute | solution.py:109
  51.2 0.0 collective-permute-done.13.in_ref
  51.2 0.0 copy-done
  51.2 5.1 %attend.4.refs_0_ = bf16[512,4096]{1,0:T(8,128)(2,1)} custom-call(s32[4]{0:T(128)S(1)} %pad_add_fusion.own, bf16[512,4096]{1,0:T(8,128)(2,1)S(1)} %copy-done, bf16[256,1024]{1,0:T(8,128)(2,1)S(1)} %get-tuple-element.24.a_ref, bf16[256,1024]{1,0:T(8,128)(2,1)S(1)} %get-tuple-element.32.b_ref, bf16[256,1024]{1,0:T(8,128)(2,1)S(1)} %collective-permute-done.13.in_ref, ...), custom_call_target="tpu_custom_call" | custom-call | flops 1342177280 | bytes 2097152 | tf_op jit(solution)/shard_map/attend/pallas_call | solution.py:171
  56.3 0.8 collective-permute-done.14.out_ref
  57.1 0.0 collective-permute-done.12.g_ref
  57.1 2.2 %collective-permute-start.15 = (bf16[2,2,256,128]{3,2,1,0:T(8,128)(2,1)S(1)}, bf16[2,2,256,128]{3,2,1,0:T(8,128)(2,1)S(1)}, u32[]{:S(2)}, u32[]{:S(2)}) collective-permute-start(bf16[2,2,256,128]{3,2,1,0:T(8,128)(2,1)S(1)} %pad_maximum_fusion.1), channel_id=1, source_target_pairs={{0,2},{1,3},{2,0},{3,1},{4,6},{5,7},{6,4},{7,5},{8,10},{9,11},{10,... | collective-permute-start | bytes 786440 | tf_op jit(solution)/shard_map/ppermute | solution.py:109
  59.3 0.7 collective-permute-start
  60.0 5.1 %attend.5.refs_0_ = bf16[512,4096]{1,0:T(8,128)(2,1)} custom-call(s32[4]{0:T(128)S(1)} %pad_add_fusion.own, bf16[512,4096]{1,0:T(8,128)(2,1)S(1)} %copy-done, bf16[256,1024]{1,0:T(8,128)(2,1)S(1)} %get-tuple-element.24.a_ref, bf16[256,1024]{1,0:T(8,128)(2,1)S(1)} %get-tuple-element.32.b_ref, ...), custom_call_target="tpu_custom_call", output_to_operand_aliasing={{}: (7, {})} | custom-call | flops 1342177280 | bytes 2097152 | tf_op jit(solution)/shard_map/attend/pallas_call | solution.py:171
  65.1 0.0 collective-permute-done.15.g_ref
  65.1 0.1 pad_maximum_fusion
  65.2 1.5 %collective-permute-start.16 = (bf16[4,2,256,128]{3,2,1,0:T(8,128)(2,1)S(1)}, bf16[4,2,256,128]{3,2,1,0:T(8,128)(2,1)S(1)}, u32[]{:S(2)}, u32[]{:S(2)}) collective-permute-start(bf16[4,2,256,128]{3,2,1,0:T(8,128)(2,1)S(1)} %pad_maximum_fusion), channel_id=1, source_target_pairs={{0,1},{1,0},{2,3},{3,2},{4,5},{5,4},{6,7},{7,6},{8,9},{9,8},{10,11... | collective-permute-start | bytes 1572872 | tf_op jit(solution)/shard_map/ppermute | solution.py:109
  66.7 9.2 %attend.6.refs_0_ = bf16[512,4096]{1,0:T(8,128)(2,1)} custom-call(s32[4]{0:T(128)S(1)} %pad_add_fusion.own, bf16[512,4096]{1,0:T(8,128)(2,1)S(1)} %copy-done, bf16[256,1024]{1,0:T(8,128)(2,1)S(1)} %get-tuple-element.24.a_ref, bf16[256,1024]{1,0:T(8,128)(2,1)S(1)} %get-tuple-element.32.b_ref, ...), custom_call_target="tpu_custom_call", output_to_operand_aliasing={{}: (7, {})} | custom-call | flops 2684354560 | bytes 4194304 | tf_op jit(solution)/shard_map/attend/pallas_call | solution.py:171
  75.9 0.0 collective-permute-done.in_ref
  75.9 0.0 collective-permute-done.16.g_ref
  75.9 16.2 %attend.7 = bf16[512,4096]{1,0:T(8,128)(2,1)} custom-call(s32[4]{0:T(128)S(1)} %pad_add_fusion.own, bf16[512,4096]{1,0:T(8,128)(2,1)S(1)} %copy-done, bf16[256,1024]{1,0:T(8,128)(2,1)S(1)} %get-tuple-element.22.a_ref, bf16[256,1024]{1,0:T(8,128)(2,1)S(1)} %get-tuple-element.23.b_ref, ...), custom_call_target="tpu_custom_call", output_to_operand_aliasing={{}: (7, {})} | custom-call | flops 5368709120 | bytes 8388608 | tf_op jit(solution)/shard_map/attend/pallas_call | solution.py:171
  (12 shorter events, 0.2 us)
Async XLA Ops:
  4.4 8.9 %collective-permute-start.1 = (f32[4,264,256]{2,1,0:T(8,128)S(1)}, f32[4,264,256]{2,1,0:T(8,128)S(1)}, u32[]{:S(2)}, u32[]{:S(2)}) collective-permute-start(f32[4,264,256]{2,1,0:T(8,128)S(1)} %get-tuple-element.26), channel_id=1, source_target_pairs={{0,1},{1,0},{2,3},{3,2},{4,5},{5,4},{6,7},{7,6},{8,9},{9,8},{10,11... | collective-permute-start | bytes 3244040 | tf_op jit(solution)/shard_map/ppermute | solution.py:109
  4.5 16.3 %collective-permute-start.3 = (bf16[256,1024]{1,0:T(8,128)(2,1)S(1)}, bf16[256,1024]{1,0:T(8,128)(2,1)S(1)}, u32[]{:S(2)}, u32[]{:S(2)}) collective-permute-start(bf16[256,1024]{1,0:T(8,128)(2,1)S(1)} %get-tuple-element.23.b_ref), channel_id=1, source_target_pairs={{1,2},{3,4},{5,6},{7,8},{9,10},{11,12},{13,14},{15,16},{17,18},{19... | collective-permute-start | bytes 1572872 | tf_op jit(solution)/shard_map/ppermute | solution.py:218
  13.3 37.8 %copy-start = (bf16[512,4096]{1,0:T(8,128)(2,1)S(1)}, bf16[512,4096]{1,0:T(8,128)(2,1)}, u32[]{:S(2)}) copy-start(bf16[512,4096]{1,0:T(8,128)(2,1)} %q_ref.7) | copy-start | bytes 12582916
  13.7 7.2 %collective-permute-start.2 = (f32[1,264,128]{2,1,0:T(8,128)S(1)}, f32[1,264,128]{2,1,0:T(8,128)S(1)}, u32[]{:S(2)}, u32[]{:S(2)}) collective-permute-start(f32[1,264,128]{2,1,0:T(8,128)S(1)} %get-tuple-element.45), channel_id=1, source_target_pairs={{0,8},{1,9},{2,10},{3,11},{4,12},{5,13},{6,14},{7,15},{8,0},{9,1},... | collective-permute-start | bytes 405512 | tf_op jit(solution)/shard_map/ppermute | solution.py:109
  15.0 10.8 %collective-permute-start.4 = (f32[1,264,128]{2,1,0:T(8,128)S(1)}, f32[1,264,128]{2,1,0:T(8,128)S(1)}, u32[]{:S(2)}, u32[]{:S(2)}) collective-permute-start(f32[1,264,128]{2,1,0:T(8,128)S(1)} %get-tuple-element.43), channel_id=1, source_target_pairs={{0,4},{1,5},{2,6},{3,7},{4,0},{5,1},{6,2},{7,3},{8,12},{9,13},{10,... | collective-permute-start | bytes 405512 | tf_op jit(solution)/shard_map/ppermute | solution.py:109
  16.3 11.8 %collective-permute-start.5 = (f32[1,264,128]{2,1,0:T(8,128)S(1)}, f32[1,264,128]{2,1,0:T(8,128)S(1)}, u32[]{:S(2)}, u32[]{:S(2)}) collective-permute-start(f32[1,264,128]{2,1,0:T(8,128)S(1)} %get-tuple-element.44), channel_id=1, source_target_pairs={{0,12},{1,13},{2,14},{3,15},{4,8},{5,9},{6,10},{7,11},{8,4},{9,5},... | collective-permute-start | bytes 405512 | tf_op jit(solution)/shard_map/ppermute | solution.py:109
  20.8 12.9 %collective-permute-start.6 = (f32[1,264,128]{2,1,0:T(8,128)S(1)}, f32[1,264,128]{2,1,0:T(8,128)S(1)}, u32[]{:S(2)}, u32[]{:S(2)}) collective-permute-start(f32[1,264,128]{2,1,0:T(8,128)S(1)} %get-tuple-element.28), channel_id=1, source_target_pairs={{0,2},{1,3},{2,0},{3,1},{4,6},{5,7},{6,4},{7,5},{8,10},{9,11},{10,... | collective-permute-start | bytes 405512 | tf_op jit(solution)/shard_map/ppermute | solution.py:109
  24.7 9.1 %collective-permute-start.7 = (f32[1,264,128]{2,1,0:T(8,128)S(1)}, f32[1,264,128]{2,1,0:T(8,128)S(1)}, u32[]{:S(2)}, u32[]{:S(2)}) collective-permute-start(f32[1,264,128]{2,1,0:T(8,128)S(1)} %get-tuple-element.29), channel_id=1, source_target_pairs={{0,10},{1,11},{2,8},{3,9},{4,14},{5,15},{6,12},{7,13},{8,2},{9,3},... | collective-permute-start | bytes 405512 | tf_op jit(solution)/shard_map/ppermute | solution.py:109
  25.7 10.3 %collective-permute-start.8 = (f32[1,264,128]{2,1,0:T(8,128)S(1)}, f32[1,264,128]{2,1,0:T(8,128)S(1)}, u32[]{:S(2)}, u32[]{:S(2)}) collective-permute-start(f32[1,264,128]{2,1,0:T(8,128)S(1)} %get-tuple-element.30), channel_id=1, source_target_pairs={{0,6},{1,7},{2,4},{3,5},{4,2},{5,3},{6,0},{7,1},{8,14},{9,15},{10,... | collective-permute-start | bytes 405512 | tf_op jit(solution)/shard_map/ppermute | solution.py:109
  25.8 10.2 %collective-permute-start.9 = (f32[1,264,128]{2,1,0:T(8,128)S(1)}, f32[1,264,128]{2,1,0:T(8,128)S(1)}, u32[]{:S(2)}, u32[]{:S(2)}) collective-permute-start(f32[1,264,128]{2,1,0:T(8,128)S(1)} %get-tuple-element.31), channel_id=1, source_target_pairs={{0,14},{1,15},{2,12},{3,13},{4,10},{5,11},{6,8},{7,9},{8,6},{9,7},... | collective-permute-start | bytes 405512 | tf_op jit(solution)/shard_map/ppermute | solution.py:109
  36.1 8.8 %collective-permute-start.10 = (f32[1,264,128]{2,1,0:T(8,128)S(1)}, f32[1,264,128]{2,1,0:T(8,128)S(1)}, u32[]{:S(2)}, u32[]{:S(2)}) collective-permute-start(f32[1,264,128]{2,1,0:T(8,128)S(1)} %fusion.7), channel_id=1, source_target_pairs={{0,16},{1,17},{2,18},{3,19},{4,20},{5,21},{6,22},{7,23},{8,24},{9,... | collective-permute-start | bytes 405512 | tf_op jit(solution)/shard_map/ppermute | solution.py:109
  39.1 12.1 %collective-permute-start.13 = (bf16[256,1024]{1,0:T(8,128)(2,1)S(1)}, bf16[256,1024]{1,0:T(8,128)(2,1)S(1)}, u32[]{:S(2)}, u32[]{:S(2)}) collective-permute-start(bf16[256,1024]{1,0:T(8,128)(2,1)S(1)} %get-tuple-element.22.a_ref), channel_id=1, source_target_pairs={{0,1},{1,0},{2,3},{3,2},{4,5},{5,4},{6,7},{7,6},{8,9},{9,8},{10,11... | collective-permute-start | bytes 1572872 | tf_op jit(solution)/shard_map/ppermute | solution.py:109
  40.8 16.3 %collective-permute-start.14 = (bf16[256,1024]{1,0:T(8,128)(2,1)S(1)}, bf16[256,1024]{1,0:T(8,128)(2,1)S(1)}, u32[]{:S(2)}, u32[]{:S(2)}) collective-permute-start(bf16[256,1024]{1,0:T(8,128)(2,1)S(1)} %get-tuple-element.32.b_ref), channel_id=1, source_target_pairs={{1,2},{3,4},{5,6},{7,8},{9,10},{11,12},{13,14},{15,16},{17,18},{19... | collective-permute-start | bytes 1572872 | tf_op jit(solution)/shard_map/ppermute | solution.py:220
  45.1 3.9 %collective-permute-start.11 = (bf16[1,1,256,128]{3,2,1,0:T(8,128)(2,1)S(1)}, bf16[1,1,256,128]{3,2,1,0:T(8,128)(2,1)S(1)}, u32[]{:S(2)}, u32[]{:S(2)}) collective-permute-start(bf16[1,1,256,128]{3,2,1,0:T(8,128)(2,1)S(1)} %fusion.9), channel_id=1, source_target_pairs={{0,8},{1,9},{2,10},{3,11},{4,12},{5,13},{6,14},{7,15},{8,0},{9,1},... | collective-permute-start | bytes 196616 | tf_op jit(solution)/shard_map/ppermute | solution.py:109
  49.1 8.0 %collective-permute-start.12 = (bf16[1,2,256,128]{3,2,1,0:T(8,128)(2,1)S(1)}, bf16[1,2,256,128]{3,2,1,0:T(8,128)(2,1)S(1)}, u32[]{:S(2)}, u32[]{:S(2)}) collective-permute-start(bf16[1,2,256,128]{3,2,1,0:T(8,128)(2,1)S(1)} %pad_maximum_fusion.2.g_ref), channel_id=1, source_target_pairs={{0,4},{1,5},{2,6},{3,7},{4,0},{5,1},{6,2},{7,3},{8,12},{9,13},{10,... | collective-permute-start | bytes 393224 | tf_op jit(solution)/shard_map/ppermute | solution.py:109
  57.1 8.0 %collective-permute-start.15 = (bf16[2,2,256,128]{3,2,1,0:T(8,128)(2,1)S(1)}, bf16[2,2,256,128]{3,2,1,0:T(8,128)(2,1)S(1)}, u32[]{:S(2)}, u32[]{:S(2)}) collective-permute-start(bf16[2,2,256,128]{3,2,1,0:T(8,128)(2,1)S(1)} %pad_maximum_fusion.1), channel_id=1, source_target_pairs={{0,2},{1,3},{2,0},{3,1},{4,6},{5,7},{6,4},{7,5},{8,10},{9,11},{10,... | collective-permute-start | bytes 786440 | tf_op jit(solution)/shard_map/ppermute | solution.py:109
  59.3 16.5 %collective-permute-start = (bf16[256,1024]{1,0:T(8,128)(2,1)S(1)}, bf16[256,1024]{1,0:T(8,128)(2,1)S(1)}, u32[]{:S(2)}, u32[]{:S(2)}) collective-permute-start(bf16[256,1024]{1,0:T(8,128)(2,1)S(1)} %get-tuple-element.24.a_ref), channel_id=1, source_target_pairs={{0,1},{1,0},{2,3},{3,2},{4,5},{5,4},{6,7},{7,6},{8,9},{9,8},{10,11... | collective-permute-start | bytes 1572872 | tf_op jit(solution)/shard_map/ppermute | solution.py:109
  65.2 10.7 %collective-permute-start.16 = (bf16[4,2,256,128]{3,2,1,0:T(8,128)(2,1)S(1)}, bf16[4,2,256,128]{3,2,1,0:T(8,128)(2,1)S(1)}, u32[]{:S(2)}, u32[]{:S(2)}) collective-permute-start(bf16[4,2,256,128]{3,2,1,0:T(8,128)(2,1)S(1)} %pad_maximum_fusion), channel_id=1, source_target_pairs={{0,1},{1,0},{2,3},{3,2},{4,5},{5,4},{6,7},{7,6},{8,9},{9,8},{10,11... | collective-permute-start | bytes 1572872 | tf_op jit(solution)/shard_map/ppermute | solution.py:109

commit v5 on v4

--- a/solution.py
+++ b/solution.py
@@ -228,6 +228,7 @@
     late, first[0], outer0 = lax.optimization_barrier((late, first[0], outer0))
     second = [swap(x, target(*block)) for x, block in zip(late, blocks[4:])]
     part = merge([cut(0, 0)] + first + second)
+    part, inner0, inner1 = lax.optimization_barrier((part, inner0, inner1))
     rest = 1
     while rest < peers:
         if rest not in HEAD_BITS + (HALF_BIT,):
@@ -241,12 +242,14 @@
     at1, out, outer1 = lax.optimization_barrier((at1, out, outer1))
     at01 = jnp.concatenate([at0, at1], axis=0)
     at23 = swap(at01, b1)
+    at45 = swap(at01, b2)
     out = attend(1, own, queries, nears0, at1, out)
+    nears1 = (in1, out1, inner1, outer1)
+    out = attend(4, own, queries, nears1, at45, out, 2)
     at23, out = lax.optimization_barrier((at23, out))
-    at4567 = swap(jnp.concatenate([at01, at23], axis=0), b2)
-    nears1 = (in1, out1, inner1, outer1)
+    at67 = swap(at23, b2)
     out = attend(2, own, queries, nears0, at23, out, 2)
-    return attend(4, own, queries, nears1, at4567, out, 2)
+    return attend(6, own, queries, nears1, at67, out, 2)
 
 
 def solution(mesh):

time: 92.3 us -> 92.7 us (level)
  Pallas kernels: 44.2 us -> 46.1 us
  waiting for transfers between devices: 18 us -> 16.6 us
    pallas_call x4 -> x5, Pallas kernels: 35.7 us -> 37.5 us  [attend(): pl.pallas_call(functools.partial(attend_kernel, per), out_shape=jax.Shape...]
    ppermute x15 -> x16, starting transfers between devices: 22.4 us -> 21 us  [swap(): return lax.ppermute(x, 'ctx', [(i, i ^ bits) for i in range(peers)])]
    ppermute x1, starting transfers between devices: 2.09 us -> 3.37 us  [on_device(): outer1 = lax.ppermute(out0, 'ctx', across)]
    ppermute x15 -> x16, waiting for transfers between devices: 12.8 us -> 12.1 us  [swap(): return lax.ppermute(x, 'ctx', [(i, i ^ bits) for i in range(peers)])]
  transfers between devices with their start and end apart: 17 -> 18, of which waited for: 6 -> 6; matrix products, arithmetic and copies ran while one was open for 1% -> 1% of each run, Pallas kernels for 26% -> 35%
where the time goes in v5:
time: 92.7 us; the launch traced here: 92.4 us
  Pallas kernels  46.1 us (50%)
  starting transfers between devices  28.9 us (31%)
  waiting for transfers between devices  16.6 us (18%)
    pallas_call x5, Pallas kernels, attend(): pl.pallas_call(functools.partial(attend_kernel, per), out_shape=jax.Shape...  37.5 us
    ppermute x16, starting transfers between devices, swap(): return lax.ppermute(x, 'ctx', [(i, i ^ bits) for i in range(peers)])  21 us
    ppermute x16, waiting for transfers between devices, swap(): return lax.ppermute(x, 'ctx', [(i, i ^ bits) for i in range(peers)])  12.1 us
    pallas_call x2, Pallas kernels, project(): pl.pallas_call(project_kernel, out_shape=(jax.ShapeDtypeStruct((HALF, cou...  8.56 us
    ppermute x1, waiting for transfers between devices, on_device(): outer0 = lax.ppermute(out1, 'ctx', across)  4.47 us
    ppermute x1, starting transfers between devices, on_device(): outer0 = lax.ppermute(out1, 'ctx', across)  4.47 us
    ppermute x1, starting transfers between devices, on_device(): outer1 = lax.ppermute(out0, 'ctx', across)  3.37 us
  transfers between devices with their start and end apart: 18, of which 6 were waited for; matrix products, arithmetic and copies ran while one was open for 1% of the time, Pallas kernels for 35%

profile of v5, /device:TPU:1, one launch (start us, length us, event | category | flops | bytes accessed | tf_op | source)
XLA Modules:
  0.0 92.4 jit_solution(2081749757426512962)
XLA Ops:
  0.0 0.1 pad_add_fusion.own
  0.1 4.3 %project.2 = (bf16[256,1024]{1,0:T(8,128)(2,1)S(1)}, bf16[256,1024]{1,0:T(8,128)(2,1)S(1)}, f32[4,264,256]{2,1,0:T(8,128)S(1)}) custom-call(s32[4]{0:T(128)S(1)} %pad_add_fusion.own, bf16[512,1024]{1,0:T(8,128)(2,1)} %k_ref.3, bf16[512,1024]{1,0:T(8,128)(2,1)} %v_ref.3, bf16[8,128,256]{2,1,0:T(8,128)(2,1)} %w1_ref.3, bf16[8,128,256]{2,1,0:T(8,128)(2,1)} %w1_ref.3), custom_call_target="tpu_custom_call" | custom-call | flops 671088640 | bytes 4194304 | tf_op jit(solution)/shard_map/project/pallas_call | solution.py:73
  4.4 0.1 collective-permute-start
  4.5 4.5 %collective-permute-start.2 = (bf16[256,1024]{1,0:T(8,128)(2,1)S(1)}, bf16[256,1024]{1,0:T(8,128)(2,1)S(1)}, u32[]{:S(2)}, u32[]{:S(2)}) collective-permute-start(bf16[256,1024]{1,0:T(8,128)(2,1)S(1)} %get-tuple-element.26.b_ref), channel_id=1, source_target_pairs={{1,2},{3,4},{5,6},{7,8},{9,10},{11,12},{13,14},{15,16},{17,18},{19... | collective-permute-start | bytes 1572872 | tf_op jit(solution)/shard_map/ppermute | solution.py:218
  9.0 4.3 %project.3 = (bf16[256,1024]{1,0:T(8,128)(2,1)S(1)}, bf16[256,1024]{1,0:T(8,128)(2,1)S(1)}, f32[4,264,256]{2,1,0:T(8,128)S(1)}) custom-call(s32[4]{0:T(128)S(1)} %pad_add_fusion.own, bf16[512,1024]{1,0:T(8,128)(2,1)} %k_ref.3, bf16[512,1024]{1,0:T(8,128)(2,1)} %v_ref.3, bf16[8,128,256]{2,1,0:T(8,128)(2,1)} %w1_ref.3, bf16[8,128,256]{2,1,0:T(8,128)(2,1)} %w1_ref.3), custom_call_target="tpu_custom_call" | custom-call | flops 671088640 | bytes 4194304 | tf_op jit(solution)/shard_map/project/pallas_call | solution.py:73
  13.3 0.0 collective-permute-done
  13.3 0.0 copy-start
  13.4 0.2 add_select_fusion
  13.6 0.1 fusion.11
  13.6 1.4 %collective-permute-start.1 = (f32[1,264,128]{2,1,0:T(8,128)S(1)}, f32[1,264,128]{2,1,0:T(8,128)S(1)}, u32[]{:S(2)}, u32[]{:S(2)}) collective-permute-start(f32[1,264,128]{2,1,0:T(8,128)S(1)} %get-tuple-element.51), channel_id=1, source_target_pairs={{0,8},{1,9},{2,10},{3,11},{4,12},{5,13},{6,14},{7,15},{8,0},{9,1},... | collective-permute-start | bytes 405512 | tf_op jit(solution)/shard_map/ppermute | solution.py:109
  15.0 1.2 %collective-permute-start.3 = (f32[1,264,128]{2,1,0:T(8,128)S(1)}, f32[1,264,128]{2,1,0:T(8,128)S(1)}, u32[]{:S(2)}, u32[]{:S(2)}) collective-permute-start(f32[1,264,128]{2,1,0:T(8,128)S(1)} %get-tuple-element.49), channel_id=1, source_target_pairs={{0,4},{1,5},{2,6},{3,7},{4,0},{5,1},{6,2},{7,3},{8,12},{9,13},{10,... | collective-permute-start | bytes 405512 | tf_op jit(solution)/shard_map/ppermute | solution.py:109
  16.2 0.1 collective-permute-start.4
  16.4 4.5 %collective-permute-done.2.out_ref = bf16[256,1024]{1,0:T(8,128)(2,1)S(1)} collective-permute-done((bf16[256,1024]{1,0:T(8,128)(2,1)S(1)}, bf16[256,1024]{1,0:T(8,128)(2,1)S(1)}, u32[]{:S(2)}, u32[]{:S(2)}) %collective-permute-start.2) | collective-permute-done | bytes 524320 | tf_op jit(solution)/shard_map/ppermute | solution.py:218
  20.8 0.0 collective-permute-done.1
  20.8 3.8 %collective-permute-start.5 = (f32[1,264,128]{2,1,0:T(8,128)S(1)}, f32[1,264,128]{2,1,0:T(8,128)S(1)}, u32[]{:S(2)}, u32[]{:S(2)}) collective-permute-start(f32[1,264,128]{2,1,0:T(8,128)S(1)} %get-tuple-element.30), channel_id=1, source_target_pairs={{0,2},{1,3},{2,0},{3,1},{4,6},{5,7},{6,4},{7,5},{8,10},{9,11},{10,... | collective-permute-start | bytes 405512 | tf_op jit(solution)/shard_map/ppermute | solution.py:109
  24.7 1.0 %collective-permute-start.6 = (f32[1,264,128]{2,1,0:T(8,128)S(1)}, f32[1,264,128]{2,1,0:T(8,128)S(1)}, u32[]{:S(2)}, u32[]{:S(2)}) collective-permute-start(f32[1,264,128]{2,1,0:T(8,128)S(1)} %get-tuple-element.31), channel_id=1, source_target_pairs={{0,10},{1,11},{2,8},{3,9},{4,14},{5,15},{6,12},{7,13},{8,2},{9,3},... | collective-permute-start | bytes 405512 | tf_op jit(solution)/shard_map/ppermute | solution.py:109
  25.7 0.1 collective-permute-start.7
  25.8 0.0 collective-permute-done.3
  25.8 2.3 %collective-permute-start.8 = (f32[1,264,128]{2,1,0:T(8,128)S(1)}, f32[1,264,128]{2,1,0:T(8,128)S(1)}, u32[]{:S(2)}, u32[]{:S(2)}) collective-permute-start(f32[1,264,128]{2,1,0:T(8,128)S(1)} %get-tuple-element.33), channel_id=1, source_target_pairs={{0,14},{1,15},{2,12},{3,13},{4,10},{5,11},{6,8},{7,9},{8,6},{9,7},... | collective-permute-start | bytes 405512 | tf_op jit(solution)/shard_map/ppermute | solution.py:109
  28.0 0.0 collective-permute-done.4
  28.0 1.2 %collective-permute-start.10 = (bf16[256,1024]{1,0:T(8,128)(2,1)S(1)}, bf16[256,1024]{1,0:T(8,128)(2,1)S(1)}, u32[]{:S(2)}, u32[]{:S(2)}) collective-permute-start(bf16[256,1024]{1,0:T(8,128)(2,1)S(1)} %get-tuple-element.34.a_ref), channel_id=1, source_target_pairs={{0,1},{1,0},{2,3},{3,2},{4,5},{5,4},{6,7},{7,6},{8,9},{9,8},{10,11... | collective-permute-start | bytes 1572872 | tf_op jit(solution)/shard_map/ppermute | solution.py:109
  29.2 4.5 %collective-permute-done.5 = f32[1,264,128]{2,1,0:T(8,128)S(1)} collective-permute-done((f32[1,264,128]{2,1,0:T(8,128)S(1)}, f32[1,264,128]{2,1,0:T(8,128)S(1)}, u32[]{:S(2)}, u32[]{:S(2)}) %collective-permute-start.5) | collective-permute-done | bytes 135200 | tf_op jit(solution)/shard_map/ppermute | solution.py:109
  33.7 1.8 %collective-permute-start.9 = (bf16[256,1024]{1,0:T(8,128)(2,1)S(1)}, bf16[256,1024]{1,0:T(8,128)(2,1)S(1)}, u32[]{:S(2)}, u32[]{:S(2)}) collective-permute-start(bf16[256,1024]{1,0:T(8,128)(2,1)S(1)} %get-tuple-element.25.a_ref), channel_id=1, source_target_pairs={{0,1},{1,0},{2,3},{3,2},{4,5},{5,4},{6,7},{7,6},{8,9},{9,8},{10,11... | collective-permute-start | bytes 1572872 | tf_op jit(solution)/shard_map/ppermute | solution.py:109
  35.6 0.0 collective-permute-done.6
  35.6 0.4 collective-permute-done.7
  36.0 0.0 collective-permute-done.8
  36.0 0.1 fusion.7
  36.1 0.0 collective-permute-done.10.in_ref
  36.2 1.0 %collective-permute-done.9.in_ref = bf16[256,1024]{1,0:T(8,128)(2,1)S(1)} collective-permute-done((bf16[256,1024]{1,0:T(8,128)(2,1)S(1)}, bf16[256,1024]{1,0:T(8,128)(2,1)S(1)}, u32[]{:S(2)}, u32[]{:S(2)}) %collective-permute-start.9) | collective-permute-done | bytes 524320 | tf_op jit(solution)/shard_map/ppermute | solution.py:109
  37.1 2.3 %collective-permute-start.11 = (f32[1,264,128]{2,1,0:T(8,128)S(1)}, f32[1,264,128]{2,1,0:T(8,128)S(1)}, u32[]{:S(2)}, u32[]{:S(2)}) collective-permute-start(f32[1,264,128]{2,1,0:T(8,128)S(1)} %fusion.7), channel_id=1, source_target_pairs={{0,16},{1,17},{2,18},{3,19},{4,20},{5,21},{6,22},{7,23},{8,24},{9,... | collective-permute-start | bytes 405512 | tf_op jit(solution)/shard_map/ppermute | solution.py:109
  39.4 3.4 %collective-permute-start.14 = (bf16[256,1024]{1,0:T(8,128)(2,1)S(1)}, bf16[256,1024]{1,0:T(8,128)(2,1)S(1)}, u32[]{:S(2)}, u32[]{:S(2)}) collective-permute-start(bf16[256,1024]{1,0:T(8,128)(2,1)S(1)} %get-tuple-element.37.b_ref), channel_id=1, source_target_pairs={{1,2},{3,4},{5,6},{7,8},{9,10},{11,12},{13,14},{15,16},{17,18},{19... | collective-permute-start | bytes 1572872 | tf_op jit(solution)/shard_map/ppermute | solution.py:220
  42.8 2.9 %collective-permute-done.11 = f32[1,264,128]{2,1,0:T(8,128)S(1)} collective-permute-done((f32[1,264,128]{2,1,0:T(8,128)S(1)}, f32[1,264,128]{2,1,0:T(8,128)S(1)}, u32[]{:S(2)}, u32[]{:S(2)}) %collective-permute-start.11) | collective-permute-done | bytes 135200 | tf_op jit(solution)/shard_map/ppermute | solution.py:109
  45.7 0.1 add_select_fusion.1
  45.9 0.6 collective-permute-start.12
  46.5 3.3 %collective-permute-done.12 = bf16[1,1,256,128]{3,2,1,0:T(8,128)(2,1)S(1)} collective-permute-done((bf16[1,1,256,128]{3,2,1,0:T(8,128)(2,1)S(1)}, bf16[1,1,256,128]{3,2,1,0:T(8,128)(2,1)S(1)}, u32[]{:S(2)}, u32[]{:S(2)}) %collective-permute-start.12) | collective-permute-done | bytes 65568 | tf_op jit(solution)/shard_map/ppermute | solution.py:109
  49.8 0.8 collective-permute-start.13
  50.6 0.0 copy-done
  50.6 5.1 %attend.5.refs_0_ = bf16[512,4096]{1,0:T(8,128)(2,1)} custom-call(s32[4]{0:T(128)S(1)} %pad_add_fusion.own, bf16[512,4096]{1,0:T(8,128)(2,1)S(1)} %copy-done, bf16[256,1024]{1,0:T(8,128)(2,1)S(1)} %get-tuple-element.34.a_ref, bf16[256,1024]{1,0:T(8,128)(2,1)S(1)} %get-tuple-element.37.b_ref, bf16[256,1024]{1,0:T(8,128)(2,1)S(1)} %collective-permute-done.9.in_ref, ...), custom_call_target="tpu_custom_call" | custom-call | flops 1342177280 | bytes 2097152 | tf_op jit(solution)/shard_map/attend/pallas_call | solution.py:171
  55.8 0.0 collective-permute-done.14.out_ref
  55.8 0.0 collective-permute-done.13.g_ref
  55.8 3.5 %collective-permute-start.16 = (bf16[2,2,256,128]{3,2,1,0:T(8,128)(2,1)S(1)}, bf16[2,2,256,128]{3,2,1,0:T(8,128)(2,1)S(1)}, u32[]{:S(2)}, u32[]{:S(2)}) collective-permute-start(bf16[2,2,256,128]{3,2,1,0:T(8,128)(2,1)S(1)} %pad_maximum_fusion), channel_id=1, source_target_pairs={{0,1},{1,0},{2,3},{3,2},{4,5},{5,4},{6,7},{7,6},{8,9},{9,8},{10,11... | collective-permute-start | bytes 786440 | tf_op jit(solution)/shard_map/ppermute | solution.py:109
  59.3 0.4 collective-permute-start.15
  59.7 5.1 %attend.6.refs_0_ = bf16[512,4096]{1,0:T(8,128)(2,1)} custom-call(s32[4]{0:T(128)S(1)} %pad_add_fusion.own, bf16[512,4096]{1,0:T(8,128)(2,1)S(1)} %copy-done, bf16[256,1024]{1,0:T(8,128)(2,1)S(1)} %get-tuple-element.34.a_ref, bf16[256,1024]{1,0:T(8,128)(2,1)S(1)} %get-tuple-element.37.b_ref, ...), custom_call_target="tpu_custom_call", output_to_operand_aliasing={{}: (7, {})} | custom-call | flops 1342177280 | bytes 2097152 | tf_op jit(solution)/shard_map/attend/pallas_call | solution.py:171
  64.8 0.0 collective-permute-done.16.g_ref
  64.8 9.2 %attend.7.refs_0_ = bf16[512,4096]{1,0:T(8,128)(2,1)} custom-call(s32[4]{0:T(128)S(1)} %pad_add_fusion.own, bf16[512,4096]{1,0:T(8,128)(2,1)S(1)} %copy-done, bf16[256,1024]{1,0:T(8,128)(2,1)S(1)} %get-tuple-element.25.a_ref, bf16[256,1024]{1,0:T(8,128)(2,1)S(1)} %get-tuple-element.26.b_ref, ...), custom_call_target="tpu_custom_call", output_to_operand_aliasing={{}: (7, {})} | custom-call | flops 2684354560 | bytes 4194304 | tf_op jit(solution)/shard_map/attend/pallas_call | solution.py:171
  74.0 0.0 collective-permute-done.15.g_ref
  74.0 0.3 collective-permute-start.17
  74.4 8.9 %attend.8.refs_0_ = bf16[512,4096]{1,0:T(8,128)(2,1)} custom-call(s32[4]{0:T(128)S(1)} %pad_add_fusion.own, bf16[512,4096]{1,0:T(8,128)(2,1)S(1)} %copy-done, bf16[256,1024]{1,0:T(8,128)(2,1)S(1)} %get-tuple-element.34.a_ref, bf16[256,1024]{1,0:T(8,128)(2,1)S(1)} %get-tuple-element.37.b_ref, ...), custom_call_target="tpu_custom_call", output_to_operand_aliasing={{}: (7, {})} | custom-call | flops 2684354560 | bytes 4194304 | tf_op jit(solution)/shard_map/attend/pallas_call | solution.py:171
  83.3 0.0 collective-permute-done.17.g_ref
  83.3 9.2 %attend.9 = bf16[512,4096]{1,0:T(8,128)(2,1)} custom-call(s32[4]{0:T(128)S(1)} %pad_add_fusion.own, bf16[512,4096]{1,0:T(8,128)(2,1)S(1)} %copy-done, bf16[256,1024]{1,0:T(8,128)(2,1)S(1)} %get-tuple-element.25.a_ref, bf16[256,1024]{1,0:T(8,128)(2,1)S(1)} %get-tuple-element.26.b_ref, ...), custom_call_target="tpu_custom_call", output_to_operand_aliasing={{}: (7, {})} | custom-call | flops 2684354560 | bytes 4194304 | tf_op jit(solution)/shard_map/attend/pallas_call | solution.py:171
  (12 shorter events, 0.2 us)
Async XLA Ops:
  4.4 8.9 %collective-permute-start = (f32[4,264,256]{2,1,0:T(8,128)S(1)}, f32[4,264,256]{2,1,0:T(8,128)S(1)}, u32[]{:S(2)}, u32[]{:S(2)}) collective-permute-start(f32[4,264,256]{2,1,0:T(8,128)S(1)} %get-tuple-element.28), channel_id=1, source_target_pairs={{0,1},{1,0},{2,3},{3,2},{4,5},{5,4},{6,7},{7,6},{8,9},{9,8},{10,11... | collective-permute-start | bytes 3244040 | tf_op jit(solution)/shard_map/ppermute | solution.py:109
  4.5 16.3 %collective-permute-start.2 = (bf16[256,1024]{1,0:T(8,128)(2,1)S(1)}, bf16[256,1024]{1,0:T(8,128)(2,1)S(1)}, u32[]{:S(2)}, u32[]{:S(2)}) collective-permute-start(bf16[256,1024]{1,0:T(8,128)(2,1)S(1)} %get-tuple-element.26.b_ref), channel_id=1, source_target_pairs={{1,2},{3,4},{5,6},{7,8},{9,10},{11,12},{13,14},{15,16},{17,18},{19... | collective-permute-start | bytes 1572872 | tf_op jit(solution)/shard_map/ppermute | solution.py:218
  13.3 37.3 %copy-start = (bf16[512,4096]{1,0:T(8,128)(2,1)S(1)}, bf16[512,4096]{1,0:T(8,128)(2,1)}, u32[]{:S(2)}) copy-start(bf16[512,4096]{1,0:T(8,128)(2,1)} %q_ref.9) | copy-start | bytes 12582916
  13.6 7.2 %collective-permute-start.1 = (f32[1,264,128]{2,1,0:T(8,128)S(1)}, f32[1,264,128]{2,1,0:T(8,128)S(1)}, u32[]{:S(2)}, u32[]{:S(2)}) collective-permute-start(f32[1,264,128]{2,1,0:T(8,128)S(1)} %get-tuple-element.51), channel_id=1, source_target_pairs={{0,8},{1,9},{2,10},{3,11},{4,12},{5,13},{6,14},{7,15},{8,0},{9,1},... | collective-permute-start | bytes 405512 | tf_op jit(solution)/shard_map/ppermute | solution.py:109
  15.0 10.8 %collective-permute-start.3 = (f32[1,264,128]{2,1,0:T(8,128)S(1)}, f32[1,264,128]{2,1,0:T(8,128)S(1)}, u32[]{:S(2)}, u32[]{:S(2)}) collective-permute-start(f32[1,264,128]{2,1,0:T(8,128)S(1)} %get-tuple-element.49), channel_id=1, source_target_pairs={{0,4},{1,5},{2,6},{3,7},{4,0},{5,1},{6,2},{7,3},{8,12},{9,13},{10,... | collective-permute-start | bytes 405512 | tf_op jit(solution)/shard_map/ppermute | solution.py:109
  16.2 11.8 %collective-permute-start.4 = (f32[1,264,128]{2,1,0:T(8,128)S(1)}, f32[1,264,128]{2,1,0:T(8,128)S(1)}, u32[]{:S(2)}, u32[]{:S(2)}) collective-permute-start(f32[1,264,128]{2,1,0:T(8,128)S(1)} %get-tuple-element.50), channel_id=1, source_target_pairs={{0,12},{1,13},{2,14},{3,15},{4,8},{5,9},{6,10},{7,11},{8,4},{9,5},... | collective-permute-start | bytes 405512 | tf_op jit(solution)/shard_map/ppermute | solution.py:109
  20.8 12.9 %collective-permute-start.5 = (f32[1,264,128]{2,1,0:T(8,128)S(1)}, f32[1,264,128]{2,1,0:T(8,128)S(1)}, u32[]{:S(2)}, u32[]{:S(2)}) collective-permute-start(f32[1,264,128]{2,1,0:T(8,128)S(1)} %get-tuple-element.30), channel_id=1, source_target_pairs={{0,2},{1,3},{2,0},{3,1},{4,6},{5,7},{6,4},{7,5},{8,10},{9,11},{10,... | collective-permute-start | bytes 405512 | tf_op jit(solution)/shard_map/ppermute | solution.py:109
  24.7 10.9 %collective-permute-start.6 = (f32[1,264,128]{2,1,0:T(8,128)S(1)}, f32[1,264,128]{2,1,0:T(8,128)S(1)}, u32[]{:S(2)}, u32[]{:S(2)}) collective-permute-start(f32[1,264,128]{2,1,0:T(8,128)S(1)} %get-tuple-element.31), channel_id=1, source_target_pairs={{0,10},{1,11},{2,8},{3,9},{4,14},{5,15},{6,12},{7,13},{8,2},{9,3},... | collective-permute-start | bytes 405512 | tf_op jit(solution)/shard_map/ppermute | solution.py:109
  25.7 10.3 %collective-permute-start.7 = (f32[1,264,128]{2,1,0:T(8,128)S(1)}, f32[1,264,128]{2,1,0:T(8,128)S(1)}, u32[]{:S(2)}, u32[]{:S(2)}) collective-permute-start(f32[1,264,128]{2,1,0:T(8,128)S(1)} %get-tuple-element.32), channel_id=1, source_target_pairs={{0,6},{1,7},{2,4},{3,5},{4,2},{5,3},{6,0},{7,1},{8,14},{9,15},{10,... | collective-permute-start | bytes 405512 | tf_op jit(solution)/shard_map/ppermute | solution.py:109
  25.8 10.2 %collective-permute-start.8 = (f32[1,264,128]{2,1,0:T(8,128)S(1)}, f32[1,264,128]{2,1,0:T(8,128)S(1)}, u32[]{:S(2)}, u32[]{:S(2)}) collective-permute-start(f32[1,264,128]{2,1,0:T(8,128)S(1)} %get-tuple-element.33), channel_id=1, source_target_pairs={{0,14},{1,15},{2,12},{3,13},{4,10},{5,11},{6,8},{7,9},{8,6},{9,7},... | collective-permute-start | bytes 405512 | tf_op jit(solution)/shard_map/ppermute | solution.py:109
  28.0 8.1 %collective-permute-start.10 = (bf16[256,1024]{1,0:T(8,128)(2,1)S(1)}, bf16[256,1024]{1,0:T(8,128)(2,1)S(1)}, u32[]{:S(2)}, u32[]{:S(2)}) collective-permute-start(bf16[256,1024]{1,0:T(8,128)(2,1)S(1)} %get-tuple-element.34.a_ref), channel_id=1, source_target_pairs={{0,1},{1,0},{2,3},{3,2},{4,5},{5,4},{6,7},{7,6},{8,9},{9,8},{10,11... | collective-permute-start | bytes 1572872 | tf_op jit(solution)/shard_map/ppermute | solution.py:109
  33.7 3.4 %collective-permute-start.9 = (bf16[256,1024]{1,0:T(8,128)(2,1)S(1)}, bf16[256,1024]{1,0:T(8,128)(2,1)S(1)}, u32[]{:S(2)}, u32[]{:S(2)}) collective-permute-start(bf16[256,1024]{1,0:T(8,128)(2,1)S(1)} %get-tuple-element.25.a_ref), channel_id=1, source_target_pairs={{0,1},{1,0},{2,3},{3,2},{4,5},{5,4},{6,7},{7,6},{8,9},{9,8},{10,11... | collective-permute-start | bytes 1572872 | tf_op jit(solution)/shard_map/ppermute | solution.py:109
  37.1 8.6 %collective-permute-start.11 = (f32[1,264,128]{2,1,0:T(8,128)S(1)}, f32[1,264,128]{2,1,0:T(8,128)S(1)}, u32[]{:S(2)}, u32[]{:S(2)}) collective-permute-start(f32[1,264,128]{2,1,0:T(8,128)S(1)} %fusion.7), channel_id=1, source_target_pairs={{0,16},{1,17},{2,18},{3,19},{4,20},{5,21},{6,22},{7,23},{8,24},{9,... | collective-permute-start | bytes 405512 | tf_op jit(solution)/shard_map/ppermute | solution.py:109
  39.4 16.3 %collective-permute-start.14 = (bf16[256,1024]{1,0:T(8,128)(2,1)S(1)}, bf16[256,1024]{1,0:T(8,128)(2,1)S(1)}, u32[]{:S(2)}, u32[]{:S(2)}) collective-permute-start(bf16[256,1024]{1,0:T(8,128)(2,1)S(1)} %get-tuple-element.37.b_ref), channel_id=1, source_target_pairs={{1,2},{3,4},{5,6},{7,8},{9,10},{11,12},{13,14},{15,16},{17,18},{19... | collective-permute-start | bytes 1572872 | tf_op jit(solution)/shard_map/ppermute | solution.py:220
  45.9 3.9 %collective-permute-start.12 = (bf16[1,1,256,128]{3,2,1,0:T(8,128)(2,1)S(1)}, bf16[1,1,256,128]{3,2,1,0:T(8,128)(2,1)S(1)}, u32[]{:S(2)}, u32[]{:S(2)}) collective-permute-start(bf16[1,1,256,128]{3,2,1,0:T(8,128)(2,1)S(1)} %fusion.9), channel_id=1, source_target_pairs={{0,8},{1,9},{2,10},{3,11},{4,12},{5,13},{6,14},{7,15},{8,0},{9,1},... | collective-permute-start | bytes 196616 | tf_op jit(solution)/shard_map/ppermute | solution.py:109
  49.8 5.9 %collective-permute-start.13 = (bf16[1,2,256,128]{3,2,1,0:T(8,128)(2,1)S(1)}, bf16[1,2,256,128]{3,2,1,0:T(8,128)(2,1)S(1)}, u32[]{:S(2)}, u32[]{:S(2)}) collective-permute-start(bf16[1,2,256,128]{3,2,1,0:T(8,128)(2,1)S(1)} %pad_maximum_fusion.1.g_ref), channel_id=1, source_target_pairs={{0,4},{1,5},{2,6},{3,7},{4,0},{5,1},{6,2},{7,3},{8,12},{9,13},{10,... | collective-permute-start | bytes 393224 | tf_op jit(solution)/shard_map/ppermute | solution.py:109
  55.8 9.0 %collective-permute-start.16 = (bf16[2,2,256,128]{3,2,1,0:T(8,128)(2,1)S(1)}, bf16[2,2,256,128]{3,2,1,0:T(8,128)(2,1)S(1)}, u32[]{:S(2)}, u32[]{:S(2)}) collective-permute-start(bf16[2,2,256,128]{3,2,1,0:T(8,128)(2,1)S(1)} %pad_maximum_fusion), channel_id=1, source_target_pairs={{0,1},{1,0},{2,3},{3,2},{4,5},{5,4},{6,7},{7,6},{8,9},{9,8},{10,11... | collective-permute-start | bytes 786440 | tf_op jit(solution)/shard_map/ppermute | solution.py:109
  59.3 14.7 %collective-permute-start.15 = (bf16[2,2,256,128]{3,2,1,0:T(8,128)(2,1)S(1)}, bf16[2,2,256,128]{3,2,1,0:T(8,128)(2,1)S(1)}, u32[]{:S(2)}, u32[]{:S(2)}) collective-permute-start(bf16[2,2,256,128]{3,2,1,0:T(8,128)(2,1)S(1)} %pad_maximum_fusion), channel_id=1, source_target_pairs={{0,2},{1,3},{2,0},{3,1},{4,6},{5,7},{6,4},{7,5},{8,10},{9,11},{10,... | collective-permute-start | bytes 786440 | tf_op jit(solution)/shard_map/ppermute | solution.py:109
  74.0 9.3 %collective-permute-start.17 = (bf16[2,2,256,128]{3,2,1,0:T(8,128)(2,1)S(1)}, bf16[2,2,256,128]{3,2,1,0:T(8,128)(2,1)S(1)}, u32[]{:S(2)}, u32[]{:S(2)}) collective-permute-start(bf16[2,2,256,128]{3,2,1,0:T(8,128)(2,1)S(1)} %collective-permute-done.15.g_ref), channel_id=1, source_target_pairs={{0,1},{1,0},{2,3},{3,2},{4,5},{5,4},{6,7},{7,6},{8,9},{9,8},{10,11... | collective-permute-start | bytes 786440 | tf_op jit(solution)/shard_map/ppermute | solution.py:109
